TPU v7x, 256 devices: a whole 4x4x8 slice. The times are simulated.
256 devices in a mesh: space: 8 (over z), mem: 32 (over x, y, core).
Axes of the slice: x: 4, y: 4, z: 8, core: 2. Of those that a mesh axis runs over, the one named last changes fastest.
Arguments:
- deviations: bfloat16 [1024, 524288], P('mem', 'space'), may hold values from -6 to 6
- obs_cell: int32 [524288], P(('space', 'mem')), may hold values from 0 to 2047, as said below
- obs_weight: float32 [524288], P(('space', 'mem')), may hold values from 0.5 to 6
- block_obs: int32 [4096, 128], P(('space', 'mem')), may hold values from 0 to 524287, as said below
- block_count: int32 [4096], P(('space', 'mem')), may hold values from 32 to 128, as said below
Outputs:
- analysis: bfloat16 [1024, 524288], P('mem', 'space')
Inputs may be any that keep to these rules, and one draw needn't show every extreme that they name: `obs_cell`: within each device's 2048 observations the cells do not decrease. `block_obs`: each block's list holds 128 different observation numbers, all held by the block's own device or within 1024 numbers of that device's range. Only the first block_count[b] entries of block b's list are used; some block uses all 128.
All inputs are finite; a program needn't handle non-finite values.
Results may differ from a plain program's by a relative error of at most 0.0026.
Values may be sent and summed in bfloat16 or wider, within the bound.
No kernel may reach another device: no remote copies, remote signals or barrier semaphores. Data moves between devices by JAX's collectives and lax.ppermute only.
A program may use at most 128 MiB of HBM per device.

v0:
```python
import math

import jax
import jax.numpy as jnp
from jax import lax
from jax.sharding import PartitionSpec as P


def with_halo(shard, sides, width):
    edges = {}
    for axis, dim in sides:
        size, length = (lax.axis_size(axis), shard.shape[dim])
        up = [(i, (i + 1) % size) for i in range(size - 1)]
        last = lax.slice_in_dim(shard, length - width, length, axis=dim)
        first = lax.slice_in_dim(shard, 0, width, axis=dim)
        edges[dim] = (
            lax.ppermute(last, axis, up),
            lax.ppermute(first, axis, [(b, a) for a, b in up]),
        )
    done = []
    for _, dim in sides:
        low, high = edges[dim]
        around = [(width, width) if d in done else (0, 0) for d in range(shard.ndim)]
        shard = jnp.concatenate([jnp.pad(low, around), shard, jnp.pad(high, around)], axis=dim)
        done.append(dim)
    return shard


def solve_each(factor, moved):
    return jax.scipy.linalg.cho_solve((factor, True), moved)


def on_device(deviations, obs_cell, obs_weight, block_obs, block_count):
    groups = lax.axis_size("mem")
    members = deviations.shape[0] * groups
    dev_cells = deviations.shape[1] // groups
    obs_dev = obs_cell.shape[0]
    weight = obs_weight * (1.0 / math.sqrt(members - 1))
    regrouped = lax.all_to_all(deviations, "mem", split_axis=1, concat_axis=0, tiled=True)
    projected = (
        jnp.take(regrouped, obs_cell, axis=1).astype(jnp.float32) * weight[None, :]
    ).astype(jnp.bfloat16)
    halo_width = obs_dev // 2
    window = with_halo(projected, ((("space", "mem"), 1),), halo_width)
    line_index = lax.axis_index("space") * groups + lax.axis_index("mem")
    window_start = line_index * obs_dev - halo_width
    local_index = block_obs - window_start
    blocks = block_obs.shape[0]
    block_width = dev_cells // blocks
    kslots = block_obs.shape[1]
    slot_ids = jnp.arange(kslots, dtype=jnp.int32)
    columns = jnp.take(window, local_index, axis=1)
    used = slot_ids[None, :] < block_count[:, None]
    columns = jnp.where(used[None, :, :], columns, jnp.zeros_like(columns))
    states = regrouped.reshape(members, blocks, block_width)
    inner = jnp.eye(kslots, dtype=jnp.float32)[None] + jnp.einsum(
        "mbk,mbl->bkl", columns, columns, preferred_element_type=jnp.float32
    )
    factor = jnp.linalg.cholesky(inner)
    moved = jnp.einsum("mbk,mbc->bkc", columns, states, preferred_element_type=jnp.float32)
    solved = jax.vmap(solve_each)(factor, moved)
    change = jnp.einsum(
        "mbk,bkc->mbc", columns.astype(jnp.float32), solved, precision=lax.Precision.HIGHEST
    )
    updated = states.astype(jnp.float32) - 0.5 * change
    analysis = updated.reshape(members, dev_cells).astype(jnp.bfloat16)
    return lax.all_to_all(analysis, "mem", split_axis=0, concat_axis=1, tiled=True)


def solution(mesh):
    in_specs = (
        P("mem", "space"),
        P(("space", "mem")),
        P(("space", "mem")),
        P(("space", "mem"), None),
        P(("space", "mem")),
    )
    out_specs = P("mem", "space")
    return jax.shard_map(
        on_device, mesh=mesh, in_specs=in_specs, out_specs=out_specs, check_vma=False
    )
```

profile of v0, /device:TPU:97, one launch (start us, length us, event | category | flops | bytes accessed | tf_op | source)
XLA Modules:
  0.0 596.4 jit_solution(2378069619990431616)
XLA Ops:
  0.0 4.8 copy.62
  4.8 0.0 copy-start.3
  4.8 0.0 copy-start.5
  4.8 7.9 %all-to-all-start = ((bf16[32,32,2048]{2,0,1:T(8,128)(2,1)}), bf16[32,32,2048]{2,0,1:T(8,128)(2,1)}, u32[]{:S(2)}, u32[]{:S(2)}) async-start(bf16[32,32,2048]{2,0,1:T(8,128)(2,1)} %bitcast.49), calls=%async_computation | async-start | bytes 8388608 | tf_op jit(solution)/shard_map/all_to_all | solution.py:39
  12.7 0.0 copy-done.3
  12.8 0.0 copy-done.5
  12.8 52.1 %all-to-all-done = bf16[32,32,2048]{2,0,1:T(8,128)(2,1)} async-done(((bf16[32,32,2048]{2,0,1:T(8,128)(2,1)}), bf16[32,32,2048]{2,0,1:T(8,128)(2,1)}, u32[]{:S(2)}, u32[]{:S(2)}) %all-to-all-start) | async-done | bytes 4194336 | tf_op jit(solution)/shard_map/all_to_all | solution.py:39
  64.9 6.4 %copy.44 = bf16[1024,2048]{0,1:T(8,128)(2,1)} copy(bf16[1024,2048]{1,0:T(8,128)(2,1)} %bitcast.1) | data formatting | bytes 8388608 | tf_op jit(solution)/shard_map/all_to_all | solution.py:39
  71.3 13.8 %gather_fusion = bf16[2048,1024]{1,0:T(8,128)(2,1)} fusion(bf16[1024,2048]{0,1:T(8,128)(2,1)} %copy.44, s32[2048]{0:T(1024)S(1)} %fusion.24), kind=kCustom, calls=%fused_computation | custom fusion | bytes 8396800 | tf_op jit(solution)/shard_map/jit(_take)/gather | solution.py:41
  85.0 2.8 fusion.1
  87.8 0.0 copy-start
  87.8 0.0 copy-start.4
  87.9 0.0 copy-start.6
  87.9 2.1 fusion.31
  89.9 0.5 copy-done
  90.4 4.6 collective-permute-start
  95.0 2.1 collective-permute-start.1
  97.2 0.0 copy-done.4
  97.2 0.0 copy-done.6
  97.2 0.1 iota_compare_fusion.3
  97.3 5.6 copy.60
  102.9 6.7 %copy.43 = bf16[1024,16,128]{0,2,1:T(8,128)(2,1)} copy(bf16[1024,16,128]{2,1,0:T(8,128)(2,1)} %bitcast.50) | data formatting | bytes 8388608 | tf_op jit(solution)/shard_map/reshape | solution.py:55
  109.7 8.6 %collective-permute-done = bf16[1024,1024]{0,1:T(8,128)(2,1)} collective-permute-done((bf16[1024,1024]{0,1:T(8,128)(2,1)}, bf16[1024,1024]{0,1:T(8,128)(2,1)}, u32[]{:S(2)}, u32[]{:S(2)}) %collective-permute-start) | collective-permute-done | bytes 2097184 | tf_op jit(solution)/shard_map/ppermute | solution.py:17
  118.3 4.3 collective-permute-done.1
  122.6 7.1 %pad_maximum_fusion = bf16[1024,4096]{0,1:T(8,128)(2,1)} fusion(bf16[1024,1024]{0,1:T(8,128)(2,1)} %collective-permute-done.1, bf16[1024,2048]{0,1:T(8,128)(2,1)} %copy-done, bf16[1024,1024]{0,1:T(8,128)(2,1)} %collective-permute-done), kind=kLoop, calls=%fused_computation.2 | loop fusion | flops 25165824 | bytes 16777216 | tf_op jit(solution)/shard_map/concatenate | solution.py:24
  129.7 15.4 %gather_fusion.1 = bf16[2048,1024]{1,0:T(8,128)(2,1)} fusion(bf16[1024,4096]{0,1:T(8,128)(2,1)} %pad_maximum_fusion, s32[2048]{0:T(1024)S(1)} %bitcast_clamp_fusion), kind=kCustom, calls=%fused_computation.1 | custom fusion | bytes 8396800 | tf_op jit(solution)/shard_map/jit(_take)/gather | solution.py:52
  145.1 6.4 %copy.45 = bf16[16,128,1024]{1,2,0:T(8,128)(2,1)} copy(bf16[16,128,1024]{2,1,0:T(8,128)(2,1)} %bitcast.48) | data formatting | bytes 8388608 | tf_op jit(solution)/shard_map/jit(_take)/gather | solution.py:52
  151.5 5.3 fusion.6
  156.7 0.3 copy.47
  157.1 0.2 fusion.21
  157.2 187.5 %custom-call.11 = f32[16,128,128]{2,1,0:T(8,128)S(1)} custom-call(f32[16,128,128]{2,1,0:T(8,128)S(1)} %fusion.21), custom_call_target="Cholesky" | custom-call | tf_op jit(solution)/shard_map/jit(cholesky)/cholesky | solution.py:59
  344.8 0.1 select_reduce_fusion
  344.9 0.1 compare_reduce_fusion
  345.0 0.2 select_bitcast_fusion
  345.2 157.4 %custom-call.12 = f32[16,1,128,128]{2,3,1,0:T(8,128)S(1)} custom-call(f32[16,1,128,128]{3,2,1,0:T(8,128)S(1)} %select_bitcast_fusion), custom_call_target="InvertDiagBlocksLowerTriangular" | custom-call | tf_op jit(solution)/shard_map/vmap(jit(_cho_solve))/triangular_solve | solution.py:30
  502.6 0.0 copy-start.2
  502.6 5.2 fusion.4
  507.8 0.0 copy-start.1
  507.8 1.8 fusion.18
  509.6 1.8 fusion.16
  511.5 0.0 copy-done.2
  511.5 0.0 copy-done.1
  511.5 5.5 fusion
  517.0 6.9 %copy.52 = bf16[1024,16,128]{2,1,0:T(8,128)(2,1)} copy(bf16[1024,16,128]{0,2,1:T(8,128)(2,1)} %fusion) | data formatting | bytes 8388608 | tf_op jit(solution)/shard_map/convert_element_type | solution.py:66
  523.8 7.3 %convert_element_type.33 = bf16[32,32,2048]{2,1,0:T(8,128)(2,1)} reshape(bf16[1024,16,128]{2,1,0:T(8,128)(2,1)} %copy.52) | data formatting | bytes 8388608 | tf_op jit(solution)/shard_map/convert_element_type | solution.py:66
  531.1 63.0 %all_to_all.35 = bf16[32,32,2048]{2,1,0:T(8,128)(2,1)S(1)} all-to-all(bf16[32,32,2048]{2,1,0:T(8,128)(2,1)} %convert_element_type.33), channel_id=1, replica_groups=mesh['space'=8,'mem'=32] {'mem'}, dimensions={0} | all-to-all | bytes 8388608 | tf_op jit(solution)/shard_map/all_to_all | solution.py:67
  594.1 2.3 copy.59
  (7 shorter events, 0.1 us)
Async XLA Ops:
  4.8 8.0 %copy-start.3 = (s32[2048]{0:T(1024)S(1)}, s32[2048]{0:T(1024)}, u32[]{:S(2)}) copy-start(s32[2048]{0:T(1024)} %param.6) | copy-start | bytes 24580
  4.8 8.0 %copy-start.5 = (f32[2048]{0:T(1024)S(1)}, f32[2048]{0:T(1024)}, u32[]{:S(2)}) copy-start(f32[2048]{0:T(1024)} %param.7) | copy-start | bytes 24580
  4.8 60.1 %all-to-all-start = ((bf16[32,32,2048]{2,0,1:T(8,128)(2,1)}), bf16[32,32,2048]{2,0,1:T(8,128)(2,1)}, u32[]{:S(2)}, u32[]{:S(2)}) async-start(bf16[32,32,2048]{2,0,1:T(8,128)(2,1)} %bitcast.49), calls=%async_computation | async-start | bytes 8388608 | tf_op jit(solution)/shard_map/all_to_all | solution.py:39
  87.8 2.6 copy-start
  87.8 9.4 %copy-start.4 = (s32[16,128]{1,0:T(8,128)S(1)}, s32[16,128]{1,0:T(8,128)}, u32[]{:S(2)}) copy-start(s32[16,128]{1,0:T(8,128)} %param.8) | copy-start | bytes 24580
  87.9 9.4 %copy-start.6 = (s32[16]{0:T(128)S(1)}, s32[16]{0:T(128)}, u32[]{:S(2)}) copy-start(s32[16]{0:T(128)} %param.9) | copy-start | bytes 196
  90.4 27.9 %collective-permute-start = (bf16[1024,1024]{0,1:T(8,128)(2,1)}, bf16[1024,1024]{0,1:T(8,128)(2,1)}, u32[]{:S(2)}, u32[]{:S(2)}) collective-permute-start(bf16[1024,1024]{0,1:T(8,128)(2,1)} %get-tuple-element.5), channel_id=1, source_target_pairs={{0,1},{1,2},{2,3},{3,4},{4,5},{5,6},{6,7},{7,8},{8,9},{9,10},{10,1... | collective-permute-start | bytes 6291464 | tf_op jit(solution)/shard_map/ppermute | solution.py:17
  95.0 27.6 %collective-permute-start.1 = (bf16[1024,1024]{0,1:T(8,128)(2,1)S(1)}, bf16[1024,1024]{0,1:T(8,128)(2,1)}, u32[]{:S(2)}, u32[]{:S(2)}) collective-permute-start(bf16[1024,1024]{0,1:T(8,128)(2,1)S(1)} %get-tuple-element.6), channel_id=1, source_target_pairs={{1,0},{2,1},{3,2},{4,3},{5,4},{6,5},{7,6},{8,7},{9,8},{10,9},{11,1... | collective-permute-start | bytes 6291464 | tf_op jit(solution)/shard_map/ppermute | solution.py:18
  502.6 8.9 %copy-start.2 = (bf16[16,128,1024]{1,2,0:T(8,128)(2,1)S(1)}, bf16[16,128,1024]{1,2,0:T(8,128)(2,1)}, u32[]{:S(2)}) copy-start(bf16[16,128,1024]{1,2,0:T(8,128)(2,1)} %copy.45) | copy-start | bytes 12582916
  507.8 3.7 copy-start.1
where the time goes:
time: 598 us; the launch traced here: 596 us
  other arithmetic  356 us (60%)
  local copies, waits for them, and re-layouts  78.5 us (13%)
  waiting for transfers between devices  65 us (11%)
  blocking collectives  63 us (11%)
  matrix products  19.6 us (3%)
  starting transfers between devices  14.6 us (2%)
    another operation x4, other arithmetic, on_device(): factor = jnp.linalg.cholesky(inner)  188 us
    another operation x3, other arithmetic, solve_each(): return jax.scipy.linalg.cho_solve((factor, True), moved)  158 us
    all_to_all x1, blocking collectives, on_device(): lax.all_to_all(analysis, 'mem', split_axis=0, concat_axis=1, tiled=True)  63 us
    all_to_all x1, waiting for transfers between devices, on_device(): lax.all_to_all(deviations, 'mem', split_axis=1, concat_axis=0, tiled=True)  52.1 us
    gather x2, local copies, waits for them, and re-layouts, on_device(): columns = jnp.take(window, local_index, axis=1)  21.8 us
    convert_element_type x2, local copies, waits for them, and re-layouts, on_device(): analysis = updated.reshape(members, dev_cells).astype(jnp.bfloat16)  14.2 us
    gather x1, local copies, waits for them, and re-layouts, on_device(): jnp.take(regrouped, obs_cell, axis=1).astype(jnp.float32) * weight[None, :]  13.8 us
  transfers between devices with their start and end apart: 3, of which 3 were waited for; matrix products, arithmetic and copies ran while one was open for 2% of the time, Pallas kernels for 0%

commit v1 on v0

--- a/solution.py
+++ b/solution.py
@@ -3,8 +3,9 @@
 import jax
 import jax.numpy as jnp
 from jax import lax
+from jax.experimental import pallas as pl
+from jax.experimental.pallas import tpu as pltpu
 from jax.sharding import PartitionSpec as P
-
 
 def with_halo(shard, sides, width):
     edges = {}
@@ -26,9 +27,55 @@
     return shard
 
 
-def solve_each(factor, moved):
-    return jax.scipy.linalg.cho_solve((factor, True), moved)
+NB = 16
 
+def three_way(v):
+    hi = v.astype(jnp.bfloat16)
+    rest = v - hi.astype(jnp.float32)
+    mid = rest.astype(jnp.bfloat16)
+    low = (rest - mid.astype(jnp.float32)).astype(jnp.bfloat16)
+    return hi, mid, low
+
+def invert_kernel(inner_ref, out_ref, work):
+    nblk, n, _ = inner_ref.shape
+    lane = lax.broadcasted_iota(jnp.int32, (1, 1, n), 2)
+    sub = lax.broadcasted_iota(jnp.int32, (1, NB, 1), 1)
+    work[...] = inner_ref[...]
+
+    def step(_, carry):
+        panel = work[:, 0:NB, :]
+        for k in range(NB):
+            row = panel[:, k:k+1, :]
+            col = panel[:, :, k:k+1]
+            inv = 1.0 / panel[:, k:k+1, k:k+1]
+            scaled = jnp.where(lane == k, inv, row * inv)
+            panel = jnp.where(sub == k, scaled, jnp.where(lane == k, 0.0, panel) - col * scaled)
+        lane2 = lax.broadcasted_iota(jnp.int32, (1, n), 1)
+        seg = lane2 // NB
+        pick = lax.broadcasted_iota(jnp.int32, (n - NB, n), 1) % NB
+        for b in range(nblk):
+            rolled = pltpu.roll(panel[b], n - NB, 1)
+            rh, rm, rl = three_way(rolled)
+            rhs = jnp.concatenate([rh, rm, rh, rl, rm, rh, rl, rm], axis=0)
+            rest = work[b, NB:n, :]
+            rep = jnp.take_along_axis(rest, pick, axis=1)
+            hi = rep.astype(jnp.bfloat16).astype(jnp.float32)
+            d1 = rep - hi
+            mid = d1.astype(jnp.bfloat16).astype(jnp.float32)
+            low = d1 - mid
+            lhs = jnp.where((seg == 0) | (seg == 1) | (seg == 3), hi,
+                   jnp.where((seg == 2) | (seg == 4) | (seg == 6), mid, low)).astype(jnp.bfloat16)
+            kept = pltpu.roll(jnp.where(lane2 < NB, 0.0, rest), n - NB, 1)
+            work[b, 0:n - NB, :] = kept - jnp.dot(lhs, rhs, preferred_element_type=jnp.float32)
+            work[b, n - NB:n, :] = rolled
+        return carry
+    lax.fori_loop(0, n // NB, step, 0)
+    out_ref[...] = work[...]
+
+def invert(inner):
+    return pl.pallas_call(invert_kernel, out_shape=jax.ShapeDtypeStruct(inner.shape, jnp.float32),
+        scratch_shapes=[pltpu.VMEM(inner.shape, jnp.float32)],
+        name="invert_blocks")(inner)
 
 def on_device(deviations, obs_cell, obs_weight, block_obs, block_count):
     groups = lax.axis_size("mem")
@@ -56,12 +103,14 @@
     inner = jnp.eye(kslots, dtype=jnp.float32)[None] + jnp.einsum(
         "mbk,mbl->bkl", columns, columns, preferred_element_type=jnp.float32
     )
-    factor = jnp.linalg.cholesky(inner)
+    inverse = invert(inner)
     moved = jnp.einsum("mbk,mbc->bkc", columns, states, preferred_element_type=jnp.float32)
-    solved = jax.vmap(solve_each)(factor, moved)
+    solved = jnp.einsum("bkl,blc->bkc", inverse, moved, precision=lax.Precision.HIGHEST)
+    high = solved.astype(jnp.bfloat16)
+    low = (solved - high.astype(jnp.float32)).astype(jnp.bfloat16)
     change = jnp.einsum(
-        "mbk,bkc->mbc", columns.astype(jnp.float32), solved, precision=lax.Precision.HIGHEST
-    )
+        "mbk,bkc->mbc", columns, high, preferred_element_type=jnp.float32
+    ) + jnp.einsum("mbk,bkc->mbc", columns, low, preferred_element_type=jnp.float32)
     updated = states.astype(jnp.float32) - 0.5 * change
     analysis = updated.reshape(members, dev_cells).astype(jnp.bfloat16)
     return lax.all_to_all(analysis, "mem", split_axis=0, concat_axis=1, tiled=True)

time: 598 us -> 271 us (0.45)
  other arithmetic: 356 us -> 9.95 us
  Pallas kernels: 0 us -> 20.1 us
    another operation x7 -> x0, other arithmetic: 345 us -> none  [the longest x4 188 us: on_device(): factor = jnp.linalg.cholesky(inner)]
    pallas_call x0 -> x1, Pallas kernels: none -> 20.1 us  [invert(): pl.pallas_call(invert_kernel, out_shape=jax.ShapeDtypeStruct(inner.shape,...]
  transfers between devices with their start and end apart: 3 -> 3, of which waited for: 3 -> 3; matrix products, arithmetic and copies ran while one was open for 2% -> 5% of each run, Pallas kernels for 0% -> 0%
where the time goes in v1:
time: 271 us; the launch traced here: 270 us
  local copies, waits for them, and re-layouts  78.2 us (29%)
  waiting for transfers between devices  65.2 us (24%)
  blocking collectives  63 us (23%)
  Pallas kernels  20.1 us (7%)
  matrix products  19.2 us (7%)
  starting transfers between devices  14.4 us (5%)
  other arithmetic  9.95 us (4%)
    all_to_all x1, blocking collectives, on_device(): lax.all_to_all(analysis, 'mem', split_axis=0, concat_axis=1, tiled=True)  63 us
    all_to_all x1, waiting for transfers between devices, on_device(): lax.all_to_all(deviations, 'mem', split_axis=1, concat_axis=0, tiled=True)  52.1 us
    gather x2, local copies, waits for them, and re-layouts, on_device(): columns = jnp.take(window, local_index, axis=1)  21.8 us
    pallas_call x1, Pallas kernels, invert(): pl.pallas_call(invert_kernel, out_shape=jax.ShapeDtypeStruct(inner.shape,...  20.1 us
    convert_element_type x2, local copies, waits for them, and re-layouts, on_device(): analysis = updated.reshape(members, dev_cells).astype(jnp.bfloat16)  14.2 us
    gather x1, local copies, waits for them, and re-layouts, on_device(): jnp.take(regrouped, obs_cell, axis=1).astype(jnp.float32) * weight[None, :]  13.7 us
    all_to_all x2, local copies, waits for them, and re-layouts, on_device(): lax.all_to_all(deviations, 'mem', split_axis=1, concat_axis=0, tiled=True)  11.2 us
    ppermute x1, waiting for transfers between devices, with_halo(): lax.ppermute(last, axis, up)  8.87 us
  transfers between devices with their start and end apart: 3, of which 3 were waited for; matrix products, arithmetic and copies ran while one was open for 5% of the time, Pallas kernels for 0%

profile of v1, /device:TPU:97, one launch (start us, length us, event | category | flops | bytes accessed | tf_op | source)
XLA Modules:
  0.0 270.2 jit_solution(16984167942738918224)
XLA Ops:
  0.0 4.8 %copy.48 = bf16[4,32,8,2048]{3,2,0,1:T(8,128)(2,1)} copy(bf16[4,32,8,2048]{3,2,1,0:T(8,128)(2,1)} %bitcast.42) | data formatting | bytes 8388608 | tf_op jit(solution)/shard_map/all_to_all | solution.py:86
  4.8 0.0 copy-start.3
  4.8 0.0 copy-start.5
  4.8 7.9 %all-to-all-start = ((bf16[32,32,2048]{2,0,1:T(8,128)(2,1)}), bf16[32,32,2048]{2,0,1:T(8,128)(2,1)}, u32[]{:S(2)}, u32[]{:S(2)}) async-start(bf16[32,32,2048]{2,0,1:T(8,128)(2,1)} %bitcast.39), calls=%async_computation | async-start | bytes 8388608 | tf_op jit(solution)/shard_map/all_to_all | solution.py:86
  12.7 0.0 copy-done.3
  12.8 0.0 copy-done.5
  12.8 52.1 %all-to-all-done = bf16[32,32,2048]{2,0,1:T(8,128)(2,1)} async-done(((bf16[32,32,2048]{2,0,1:T(8,128)(2,1)}), bf16[32,32,2048]{2,0,1:T(8,128)(2,1)}, u32[]{:S(2)}, u32[]{:S(2)}) %all-to-all-start) | async-done | bytes 4194336 | tf_op jit(solution)/shard_map/all_to_all | solution.py:86
  64.9 6.4 %copy.31 = bf16[1024,2048]{0,1:T(8,128)(2,1)} copy(bf16[1024,2048]{1,0:T(8,128)(2,1)} %bitcast.1) | data formatting | bytes 8388608 | tf_op jit(solution)/shard_map/all_to_all | solution.py:86
  71.3 13.7 %gather_fusion = bf16[2048,1024]{1,0:T(8,128)(2,1)} fusion(bf16[1024,2048]{0,1:T(8,128)(2,1)} %copy.31, s32[2048]{0:T(1024)S(1)} %fusion.18), kind=kCustom, calls=%fused_computation | custom fusion | bytes 8396800 | tf_op jit(solution)/shard_map/jit(_take)/gather | solution.py:88
  85.0 2.8 %fusion.1 = bf16[1024,2048]{0,1:T(8,128)(2,1)S(1)} fusion(f32[2048]{0:T(1024)S(1)} %broadcast_multiply_fusion, bf16[2048,1024]{1,0:T(8,128)(2,1)} %gather_fusion, pred[2048]{0:T(1024)(128)(4,1)S(1)} %compare_and_fusion), kind=kLoop, calls=%fused_computation.6 | loop fusion | flops 8388608 | bytes 8398848 | tf_op jit(solution)/shard_map/convert_element_type | solution.py:89
  87.8 0.0 copy-start
  87.8 0.0 copy-start.4
  87.8 0.0 copy-start.6
  87.8 2.2 fusion.27
  90.0 0.4 copy-done
  90.4 4.6 %collective-permute-start = (bf16[1024,1024]{0,1:T(8,128)(2,1)}, bf16[1024,1024]{0,1:T(8,128)(2,1)}, u32[]{:S(2)}, u32[]{:S(2)}) collective-permute-start(bf16[1024,1024]{0,1:T(8,128)(2,1)} %get-tuple-element.5), channel_id=1, source_target_pairs={{0,1},{1,2},{2,3},{3,4},{4,5},{5,6},{6,7},{7,8},{8,9},{9,10},{10,1... | collective-permute-start | bytes 6291464 | tf_op jit(solution)/shard_map/ppermute | solution.py:18
  95.0 1.9 collective-permute-start.1
  97.0 0.0 copy-done.4
  97.0 0.0 copy-done.6
  97.0 0.1 iota_compare_fusion.1
  97.1 5.7 %copy.46 = bf16[128,8,16,128]{3,2,1,0:T(8,128)(2,1)} copy(bf16[128,8,16,128]{3,1,2,0:T(8,128)(2,1)} %bitcast.14) | data formatting | bytes 8388608
  102.7 6.7 %copy.30 = bf16[1024,16,128]{0,2,1:T(8,128)(2,1)} copy(bf16[1024,16,128]{2,1,0:T(8,128)(2,1)} %bitcast.40) | data formatting | bytes 8388608 | tf_op jit(solution)/shard_map/reshape | solution.py:102
  109.4 8.9 %collective-permute-done = bf16[1024,1024]{0,1:T(8,128)(2,1)} collective-permute-done((bf16[1024,1024]{0,1:T(8,128)(2,1)}, bf16[1024,1024]{0,1:T(8,128)(2,1)}, u32[]{:S(2)}, u32[]{:S(2)}) %collective-permute-start) | collective-permute-done | bytes 2097184 | tf_op jit(solution)/shard_map/ppermute | solution.py:18
  118.3 4.3 %collective-permute-done.1 = bf16[1024,1024]{0,1:T(8,128)(2,1)} collective-permute-done((bf16[1024,1024]{0,1:T(8,128)(2,1)S(1)}, bf16[1024,1024]{0,1:T(8,128)(2,1)}, u32[]{:S(2)}, u32[]{:S(2)}) %collective-permute-start.1) | collective-permute-done | bytes 2097184 | tf_op jit(solution)/shard_map/ppermute | solution.py:19
  122.6 7.0 %pad_maximum_fusion = bf16[1024,4096]{0,1:T(8,128)(2,1)} fusion(bf16[1024,1024]{0,1:T(8,128)(2,1)} %collective-permute-done.1, bf16[1024,2048]{0,1:T(8,128)(2,1)} %copy-done, bf16[1024,1024]{0,1:T(8,128)(2,1)} %collective-permute-done), kind=kLoop, calls=%fused_computation.2 | loop fusion | flops 25165824 | bytes 16777216 | tf_op jit(solution)/shard_map/concatenate | solution.py:25
  129.6 15.4 %gather_fusion.1 = bf16[2048,1024]{1,0:T(8,128)(2,1)} fusion(bf16[1024,4096]{0,1:T(8,128)(2,1)} %pad_maximum_fusion, s32[2048]{0:T(1024)S(1)} %bitcast_clamp_fusion), kind=kCustom, calls=%fused_computation.1 | custom fusion | bytes 8396800 | tf_op jit(solution)/shard_map/jit(_take)/gather | solution.py:99
  145.0 6.4 %copy.32 = bf16[16,128,1024]{1,2,0:T(8,128)(2,1)} copy(bf16[16,128,1024]{2,1,0:T(8,128)(2,1)} %bitcast.38) | data formatting | bytes 8388608 | tf_op jit(solution)/shard_map/jit(_take)/gather | solution.py:99
  151.4 0.0 copy-start.1
  151.4 5.2 %fusion.6 = f32[16,128,128]{2,1,0:T(8,128)S(1)} fusion(bf16[1024,16,128]{0,2,1:T(8,128)(2,1)} %copy.30, bf16[16,128,1024]{1,2,0:T(8,128)(2,1)} %copy.32, pred[16,128]{1,0:T(8,128)(4,1)S(1)} %get-tuple-element.7, pred[16,128]{1,0:T(8,128)(4,1)S(1)} %get-tuple-element.8), kind=kOutput, calls=%fused_computation.12 | convolution fusion | flops 541065216 | bytes 9441280 | tf_op jit(solution)/shard_map/mbk,mbc->bkc/dot_general | solution.py:107
  156.6 0.0 copy-done.1
  156.6 2.8 %fusion.12.inner_ref = f32[16,128,128]{2,1,0:T(8,128)} fusion(bf16[16,128,1024]{1,2,0:T(8,128)(2,1)S(1)} %copy-done.1, pred[16,128]{1,0:T(8,128)(4,1)S(1)} %get-tuple-element.7, pred[16,128]{1,0:T(8,128)(4,1)S(1)} %get-tuple-element.8, f32[128,128]{1,0:T(8,128)S(1)} %fusion.17), kind=kOutput, calls=%fused_computation.17 | convolution fusion | flops 541327360 | bytes 5312512 | tf_op jit(solution)/shard_map/mbk,mbl->bkl/dot_general | solution.py:103
  159.4 20.1 %invert_blocks.1 = f32[16,128,128]{2,1,0:T(8,128)} custom-call(f32[16,128,128]{2,1,0:T(8,128)} %fusion.12.inner_ref), custom_call_target="tpu_custom_call" | custom-call | tf_op jit(solution)/shard_map/invert_blocks/pallas_call | solution.py:76
  179.4 2.4 fusion.28
  181.9 0.0 copy-start.2
  181.9 3.6 %fusion.2 = f32[16,128,1024]{2,1,0:T(8,128)S(1)} fusion(bf16[16,128,1024]{1,2,0:T(8,128)(2,1)} %copy.32, pred[16,128]{1,0:T(8,128)(4,1)S(1)} %get-tuple-element.7, pred[16,128]{1,0:T(8,128)(4,1)S(1)} %get-tuple-element.8, f32[16,128,128]{2,1,0:T(8,128)S(1)} %fusion.28), kind=kOutput, calls=%fused_computation.8 | convolution fusion | flops 542113792 | bytes 13635584 | tf_op jit(solution)/shard_map/mbk,bkc->mbc/dot_general | solution.py:113
  185.5 0.0 copy-done.2
  185.5 5.2 %fusion = bf16[1024,16,128]{0,2,1:T(8,128)(2,1)} fusion(f32[16,128,1024]{2,1,0:T(8,128)S(1)} %fusion.2, bf16[1024,16,128]{0,2,1:T(8,128)(2,1)} %copy.30, bf16[16,128,1024]{1,2,0:T(8,128)(2,1)S(1)} %copy-done.2, pred[16,128]{1,0:T(8,128)(4,1)S(1)} %get-tuple-element.7, pred[16,128]{1,0:T(8,128)(4,1)S(1)} %get-tuple-element.8, f32[16,128,128]{2,1,0:T(8,128)S(1)} %fusion.28), kind=kOutput, calls=%fused_computation.4 | convolution fusion | flops 551813120 | bytes 22024192 | tf_op jit(solution)/shard_map/mbk,bkc->mbc/dot_general | solution.py:111
  190.7 6.9 %copy.38 = bf16[1024,16,128]{2,1,0:T(8,128)(2,1)} copy(bf16[1024,16,128]{0,2,1:T(8,128)(2,1)} %fusion) | data formatting | bytes 8388608 | tf_op jit(solution)/shard_map/convert_element_type | solution.py:115
  197.6 7.3 %convert_element_type.40 = bf16[32,32,2048]{2,1,0:T(8,128)(2,1)} reshape(bf16[1024,16,128]{2,1,0:T(8,128)(2,1)} %copy.38) | data formatting | bytes 8388608 | tf_op jit(solution)/shard_map/convert_element_type | solution.py:115
  204.9 63.0 %all_to_all.35 = bf16[32,32,2048]{2,1,0:T(8,128)(2,1)S(1)} all-to-all(bf16[32,32,2048]{2,1,0:T(8,128)(2,1)} %convert_element_type.40), channel_id=1, replica_groups=mesh['space'=8,'mem'=32] {'mem'}, dimensions={0} | all-to-all | bytes 8388608 | tf_op jit(solution)/shard_map/all_to_all | solution.py:116
  267.9 2.3 copy.45
  (5 shorter events, 0.0 us)
Async XLA Ops:
  4.8 8.0 %copy-start.3 = (s32[2048]{0:T(1024)S(1)}, s32[2048]{0:T(1024)}, u32[]{:S(2)}) copy-start(s32[2048]{0:T(1024)} %param.6) | copy-start | bytes 24580
  4.8 8.0 %copy-start.5 = (f32[2048]{0:T(1024)S(1)}, f32[2048]{0:T(1024)}, u32[]{:S(2)}) copy-start(f32[2048]{0:T(1024)} %param.7) | copy-start | bytes 24580
  4.8 60.1 %all-to-all-start = ((bf16[32,32,2048]{2,0,1:T(8,128)(2,1)}), bf16[32,32,2048]{2,0,1:T(8,128)(2,1)}, u32[]{:S(2)}, u32[]{:S(2)}) async-start(bf16[32,32,2048]{2,0,1:T(8,128)(2,1)} %bitcast.39), calls=%async_computation | async-start | bytes 8388608 | tf_op jit(solution)/shard_map/all_to_all | solution.py:86
  87.8 2.6 copy-start
  87.8 9.2 %copy-start.4 = (s32[16,128]{1,0:T(8,128)S(1)}, s32[16,128]{1,0:T(8,128)}, u32[]{:S(2)}) copy-start(s32[16,128]{1,0:T(8,128)} %param.8) | copy-start | bytes 24580
  87.8 9.2 %copy-start.6 = (s32[16]{0:T(128)S(1)}, s32[16]{0:T(128)}, u32[]{:S(2)}) copy-start(s32[16]{0:T(128)} %param.9) | copy-start | bytes 196
  90.4 27.9 %collective-permute-start = (bf16[1024,1024]{0,1:T(8,128)(2,1)}, bf16[1024,1024]{0,1:T(8,128)(2,1)}, u32[]{:S(2)}, u32[]{:S(2)}) collective-permute-start(bf16[1024,1024]{0,1:T(8,128)(2,1)} %get-tuple-element.5), channel_id=1, source_target_pairs={{0,1},{1,2},{2,3},{3,4},{4,5},{5,6},{6,7},{7,8},{8,9},{9,10},{10,1... | collective-permute-start | bytes 6291464 | tf_op jit(solution)/shard_map/ppermute | solution.py:18
  95.0 27.6 %collective-permute-start.1 = (bf16[1024,1024]{0,1:T(8,128)(2,1)S(1)}, bf16[1024,1024]{0,1:T(8,128)(2,1)}, u32[]{:S(2)}, u32[]{:S(2)}) collective-permute-start(bf16[1024,1024]{0,1:T(8,128)(2,1)S(1)} %get-tuple-element.6), channel_id=1, source_target_pairs={{1,0},{2,1},{3,2},{4,3},{5,4},{6,5},{7,6},{8,7},{9,8},{10,9},{11,1... | collective-permute-start | bytes 6291464 | tf_op jit(solution)/shard_map/ppermute | solution.py:19
  151.4 5.2 %copy-start.1 = (bf16[16,128,1024]{1,2,0:T(8,128)(2,1)S(1)}, bf16[16,128,1024]{1,2,0:T(8,128)(2,1)}, u32[]{:S(2)}) copy-start(bf16[16,128,1024]{1,2,0:T(8,128)(2,1)} %copy.32) | copy-start | bytes 12582916
  181.9 3.7 %copy-start.2 = (bf16[16,128,1024]{1,2,0:T(8,128)(2,1)S(1)}, bf16[16,128,1024]{1,2,0:T(8,128)(2,1)}, u32[]{:S(2)}) copy-start(bf16[16,128,1024]{1,2,0:T(8,128)(2,1)} %copy.32) | copy-start | bytes 12582916

commit v2 on v1

v2 whole, which is shorter than its diff:
```python
import math

import jax
import jax.numpy as jnp
from jax import lax
from jax.experimental import pallas as pl
from jax.experimental.pallas import tpu as pltpu
from jax.sharding import PartitionSpec as P

NB = 16
TILE = 256
ROWS = (16, 16)

NT = (((1,), (1,)), ((), ()))
TN = (((0,), (0,)), ((), ()))


def dot(a, b, dims=(((1,), (0,)), ((), ())), precision=None):
    return lax.dot_general(a, b, dims, precision=precision, preferred_element_type=jnp.float32)


def project_kernel(cell_ref, cells_ref, weight_ref, states_ref, out_ref, acc_ref):
    tile = pl.program_id(0)
    lane = lax.broadcasted_iota(jnp.int32, (TILE, 128), 1)
    first = cell_ref[tile * TILE] // TILE
    last = cell_ref[tile * TILE + TILE - 1] // TILE
    acc_ref[...] = jnp.zeros_like(acc_ref)
    cells = cells_ref[...]

    def add(step, carry):
        start = pl.multiple_of(step * TILE, TILE)
        pick = jnp.concatenate(
            [(cells == lane + (start + at)).astype(jnp.float32) for at in range(0, TILE, 128)], axis=1
        ).astype(jnp.bfloat16)
        acc_ref[...] += dot(pick, states_ref[:, pl.ds(start, TILE)], NT)
        return carry

    lax.fori_loop(first, last + 1, add, 0)
    out_ref[...] = (acc_ref[...] * weight_ref[:, 0:1]).astype(jnp.bfloat16)


def project(obs_cell, cells, weight, states):
    members, width = states.shape
    obs = obs_cell.shape[0]
    return pl.pallas_call(
        project_kernel,
        grid_spec=pltpu.PrefetchScalarGridSpec(
            num_scalar_prefetch=1,
            grid=(obs // TILE,),
            in_specs=[
                pl.BlockSpec((TILE, 128), lambda i, c: (i, 0)),
                pl.BlockSpec((TILE, 128), lambda i, c: (i, 0)),
                pl.BlockSpec((members, width), lambda i, c: (0, 0)),
            ],
            out_specs=pl.BlockSpec((TILE, members), lambda i, c: (i, 0)),
            scratch_shapes=[pltpu.VMEM((TILE, members), jnp.float32)],
        ),
        out_shape=jax.ShapeDtypeStruct((obs, members), jnp.bfloat16),
        cost_estimate=pl.CostEstimate(
            flops=4 * obs * members * TILE, bytes_accessed=8 * obs * members, transcendentals=0
        ),
        name="project",
    )(obs_cell, cells, weight, states)


def gram_kernel(slots_ref, low_ref, own_ref, high_ref, states_ref, *refs):
    if len(refs) == 5:
        gram_in, moved_in, columns_ref, gram_ref, moved_ref = refs
    else:
        columns_ref, gram_ref, moved_ref = refs
    lane = lax.broadcasted_iota(jnp.int32, (128, 128), 1)
    slots = slots_ref[...]

    def pick(start, length):
        return jnp.concatenate(
            [(slots == lane + at).astype(jnp.float32) for at in range(start, start + length, 128)], axis=1
        ).astype(jnp.bfloat16)

    edge, length = low_ref.shape[0], own_ref.shape[0]
    chosen = (
        dot(pick(0, edge), low_ref[...])
        + dot(pick(edge, length), own_ref[...])
        + dot(pick(edge + length, edge), high_ref[...])
    ).astype(jnp.bfloat16)
    columns_ref[0] = chosen
    gram = dot(chosen, chosen, NT)
    moved = dot(chosen, states_ref[...])
    if len(refs) == 5:
        gram = gram + gram_in[0]
        moved = moved + moved_in[0]
    gram_ref[0] = gram
    moved_ref[0] = moved


def gather_gram(slots, low, own, high, states, before):
    members, width = states.shape
    blocks, kslots = slots.shape[0] // 128, 128
    whole = lambda a: pl.BlockSpec(a.shape, lambda i: (0, 0))
    square = pl.BlockSpec((1, kslots, kslots), lambda i: (i, 0, 0))
    squares = jax.ShapeDtypeStruct((blocks, kslots, kslots), jnp.float32)
    return pl.pallas_call(
        gram_kernel,
        grid=(blocks,),
        in_specs=[
            pl.BlockSpec((128, 128), lambda i: (i, 0)),
            whole(low),
            whole(own),
            whole(high),
            pl.BlockSpec((members, kslots), lambda i: (0, i)),
        ]
        + [square] * len(before),
        out_specs=(pl.BlockSpec((1, kslots, members), lambda i: (i, 0, 0)), square, square),
        out_shape=(jax.ShapeDtypeStruct((blocks, kslots, members), jnp.bfloat16), squares, squares),
        cost_estimate=pl.CostEstimate(
            flops=2 * blocks * kslots * members * 4096, bytes_accessed=16 * members * width, transcendentals=0
        ),
        name="gather_gram",
    )(slots, low, own, high, states, *before)


def three_way(v):
    hi = v.astype(jnp.bfloat16)
    rest = v - hi.astype(jnp.float32)
    mid = rest.astype(jnp.bfloat16)
    low = (rest - mid.astype(jnp.float32)).astype(jnp.bfloat16)
    return hi, mid, low


def invert_kernel(gram_ref, out_ref, work):
    nblk, n, _ = gram_ref.shape
    lane = lax.broadcasted_iota(jnp.int32, (1, 1, n), 2)
    sub = lax.broadcasted_iota(jnp.int32, (1, NB, 1), 1)
    lane2 = lax.broadcasted_iota(jnp.int32, (1, n), 1)
    seg = lane2 // NB
    pick = lax.broadcasted_iota(jnp.int32, (n - NB, n), 1) % NB
    rows = lax.broadcasted_iota(jnp.int32, (1, n, n), 1)
    cols = lax.broadcasted_iota(jnp.int32, (1, n, n), 2)
    work[...] = gram_ref[...] + jnp.where(rows == cols, 1.0, 0.0)

    def step(_, carry):
        panel = work[:, 0:NB, :]
        for k in range(NB):
            row = panel[:, k : k + 1, :]
            col = panel[:, :, k : k + 1]
            inv = 1.0 / panel[:, k : k + 1, k : k + 1]
            scaled = jnp.where(lane == k, inv, row * inv)
            panel = jnp.where(sub == k, scaled, jnp.where(lane == k, 0.0, panel) - col * scaled)
        for b in range(nblk):
            rolled = pltpu.roll(panel[b], n - NB, 1)
            rh, rm, rl = three_way(rolled)
            rhs = jnp.concatenate([rh, rm, rh, rl, rm, rh, rl, rm], axis=0)
            rest = work[b, NB:n, :]
            rep = jnp.take_along_axis(rest, pick, axis=1)
            hi = rep.astype(jnp.bfloat16).astype(jnp.float32)
            d1 = rep - hi
            mid = d1.astype(jnp.bfloat16).astype(jnp.float32)
            low = d1 - mid
            lhs = jnp.where(
                (seg == 0) | (seg == 1) | (seg == 3),
                hi,
                jnp.where((seg == 2) | (seg == 4) | (seg == 6), mid, low),
            ).astype(jnp.bfloat16)
            kept = pltpu.roll(jnp.where(lane2 < NB, 0.0, rest), n - NB, 1)
            work[b, 0 : n - NB, :] = kept - dot(lhs, rhs)
            work[b, n - NB : n, :] = rolled
        return carry

    lax.fori_loop(0, n // NB, step, 0)
    out_ref[...] = work[...]


def invert(gram):
    return pl.pallas_call(
        invert_kernel,
        out_shape=jax.ShapeDtypeStruct(gram.shape, jnp.float32),
        scratch_shapes=[pltpu.VMEM(gram.shape, jnp.float32)],
        name="invert_blocks",
    )(gram)


def update_kernel(inverse_ref, moved_ref, *refs):
    out_ref = refs[-1]
    chunks = (len(refs) - 1) // 2
    solved = dot(inverse_ref[0], moved_ref[0], precision=lax.Precision.HIGHEST) * 0.5
    high = solved.astype(jnp.bfloat16)
    low = (solved - high.astype(jnp.float32)).astype(jnp.bfloat16)
    at = 0
    for columns_ref, states_ref in zip(refs[:chunks], refs[chunks:-1]):
        columns = columns_ref[0]
        change = dot(columns, high, TN) + dot(columns, low, TN)
        updated = states_ref[...].astype(jnp.float32) - change
        groups = out_ref.shape[0]
        rows = updated.shape[0] // groups
        out_ref[:, at : at + rows, :] = updated.reshape(groups, rows, 128).astype(jnp.bfloat16)
        at += rows


def update(inverse, moved, columns, states, groups):
    blocks, kslots, _ = inverse.shape
    square = pl.BlockSpec((1, kslots, kslots), lambda i: (i, 0, 0))
    members = sum(s.shape[0] for s in states)
    width = states[0].shape[1]
    return pl.pallas_call(
        update_kernel,
        grid=(blocks,),
        in_specs=[square, square]
        + [pl.BlockSpec((1, kslots, c.shape[2]), lambda i: (i, 0, 0)) for c in columns]
        + [pl.BlockSpec((s.shape[0], kslots), lambda i: (0, i)) for s in states],
        out_specs=pl.BlockSpec((groups, members // groups, kslots), lambda i: (0, 0, i)),
        out_shape=jax.ShapeDtypeStruct((groups, members // groups, width), jnp.bfloat16),
        name="update",
    )(inverse, moved, *columns, *states)


def on_device(deviations, obs_cell, obs_weight, block_obs, block_count):
    groups = lax.axis_size("mem")
    members = deviations.shape[0] * groups
    obs_dev = obs_cell.shape[0]
    edge = obs_dev // 2
    weight = obs_weight * (1.0 / math.sqrt(members - 1))
    cells = jnp.broadcast_to(obs_cell[:, None], (obs_dev, 128))
    weights = jnp.broadcast_to(weight[:, None], (obs_dev, 128))
    line_index = lax.axis_index("space") * groups + lax.axis_index("mem")
    local_index = block_obs - (line_index * obs_dev - edge)
    slot_ids = jnp.arange(block_obs.shape[1], dtype=jnp.int32)
    local_index = jnp.where(slot_ids[None, :] < block_count[:, None], local_index, -1)
    slots = jnp.broadcast_to(local_index.reshape(-1)[:, None], (local_index.size, 128))
    size = lax.axis_size("space") * groups
    up = [(i, i + 1) for i in range(size - 1)]
    down = [(b, a) for a, b in up]
    at = 0
    states, columns, before = [], [], ()
    for rows in ROWS:
        part = lax.slice_in_dim(deviations, at, at + rows, axis=0)
        at += rows
        moved_in = lax.all_to_all(part, "mem", split_axis=1, concat_axis=0, tiled=True)
        own = project(obs_cell, cells, weights, moved_in)
        low = lax.ppermute(own[edge:], ("space", "mem"), up)
        high = lax.ppermute(own[:edge], ("space", "mem"), down)
        chosen, *before = gather_gram(slots, low, own, high, moved_in, before)
        states.append(moved_in)
        columns.append(chosen)
    gram, moved = before
    analysis = update(invert(gram), moved, columns, states, groups)
    return lax.all_to_all(
        analysis.reshape(members, -1), "mem", split_axis=0, concat_axis=1, tiled=True
    )


def solution(mesh):
    in_specs = (
        P("mem", "space"),
        P(("space", "mem")),
        P(("space", "mem")),
        P(("space", "mem"), None),
        P(("space", "mem")),
    )
    out_specs = P("mem", "space")
    return jax.shard_map(
        on_device, mesh=mesh, in_specs=in_specs, out_specs=out_specs, check_vma=False
    )
```

time: 271 us -> 233 us (0.86)
  Pallas kernels: 20.1 us -> 92.3 us
  local copies, waits for them, and re-layouts: 78.2 us -> 20.7 us
  waiting for transfers between devices: 65.2 us -> 34 us
  matrix products: 19.2 us -> 0 us
  other arithmetic: 9.95 us -> 0.08 us
  starting transfers between devices: 14.4 us -> 24 us
  blocking collectives: 63 us -> 59.8 us
    pallas_call x1 -> x6, Pallas kernels: 20.1 us -> 92.3 us  [the longest x2 36.9 us: gather_gram(): pl.pallas_call(gram_kernel, grid=(blocks,), in_specs=[pl.BlockSpec((128,...]
    gather x3 -> x0, local copies, waits for them, and re-layouts: 35.5 us -> none  [the longest x2 21.8 us: on_device(): columns = jnp.take(window, local_index, axis=1)]
    dot_general x5 -> x0, matrix products: 19.2 us -> none  [the longest x1 5.21 us: on_device(): jnp.einsum('mbk,bkc->mbc', columns, high, preferred_element_type=jnp.floa...]
    all_to_all x1 -> x2, waiting for transfers between devices: 52.1 us -> 34 us  [on_device(): lax.all_to_all(part, 'mem', split_axis=1, concat_axis=0, tiled=True)]
    convert_element_type x2 -> x0, local copies, waits for them, and re-layouts: 14.2 us -> none  [on_device(): analysis = updated.reshape(members, dev_cells).astype(jnp.bfloat16)]
    ppermute x2 -> x4, waiting for transfers between devices: 13.2 us -> 0.01 us  [the longest x2 0.01 us: on_device(): high = lax.ppermute(own[:edge], ('space', 'mem'), down)]
    concatenate x1 -> x0, other arithmetic: 7.03 us -> none  [with_halo(): jnp.concatenate([jnp.pad(low, around), shard, jnp.pad(high, around)], axi...]
    reshape x1 -> x0, local copies, waits for them, and re-layouts: 6.68 us -> none  [on_device(): states = regrouped.reshape(members, blocks, block_width)]
  transfers between devices with their start and end apart: 3 -> 6, of which waited for: 3 -> 2; matrix products, arithmetic and copies ran while one was open for 5% -> 5% of each run, Pallas kernels for 0% -> 16%
where the time goes in v2:
time: 233 us; the launch traced here: 231 us
  Pallas kernels  92.3 us (40%)
  blocking collectives  59.8 us (26%)
  waiting for transfers between devices  34 us (15%)
  starting transfers between devices  24 us (10%)
  local copies, waits for them, and re-layouts  20.7 us (9%)
    all_to_all x1, blocking collectives, on_device(): lax.all_to_all(analysis.reshape(members, -1), 'mem', split_axis=0, concat...  59.8 us
    pallas_call x2, Pallas kernels, gather_gram(): pl.pallas_call(gram_kernel, grid=(blocks,), in_specs=[pl.BlockSpec((128,...  36.9 us
    all_to_all x2, waiting for transfers between devices, on_device(): lax.all_to_all(part, 'mem', split_axis=1, concat_axis=0, tiled=True)  34 us
    pallas_call x1, Pallas kernels, invert(): pl.pallas_call(invert_kernel, out_shape=jax.ShapeDtypeStruct(gram.shape,...  20.1 us
    pallas_call x2, Pallas kernels, project(): pl.pallas_call(project_kernel, grid_spec=pltpu.PrefetchScalarGridSpec(num...  19.5 us
    pallas_call x1, Pallas kernels, update(): pl.pallas_call(update_kernel, grid=(blocks,), in_specs=[square, square] +...  15.9 us
    all_to_all x2, starting transfers between devices, on_device(): lax.all_to_all(part, 'mem', split_axis=1, concat_axis=0, tiled=True)  12.9 us
    ppermute x2, starting transfers between devices, on_device(): low = lax.ppermute(own[edge:], ('space', 'mem'), up)  6.07 us
  transfers between devices with their start and end apart: 6, of which 2 were waited for; matrix products, arithmetic and copies ran while one was open for 5% of the time, Pallas kernels for 16%

profile of v2, /device:TPU:97, one launch (start us, length us, event | category | flops | bytes accessed | tf_op | source)
XLA Modules:
  0.0 231.0 jit_solution(4965188045221830764)
XLA Ops:
  0.0 3.8 %fusion = (bf16[16,65536]{1,0:T(8,128)(2,1)S(1)}, bf16[16,65536]{1,0:T(8,128)(2,1)}) fusion(bf16[32,65536]{1,0:T(8,128)(2,1)} %param.5), kind=kLoop, calls=%fused_computation.5 | loop fusion | bytes 8388608 | tf_op jit(solution)/shard_map/slice | solution.py:234
  3.8 1.6 copy.16
  5.4 7.8 %all-to-all-start.1 = ((bf16[16,32,2048]{2,0,1:T(8,128)(2,1)}), bf16[16,32,2048]{2,0,1:T(8,128)(2,1)S(1)}, u32[]{:S(2)}, u32[]{:S(2)}) async-start(bf16[16,32,2048]{2,0,1:T(8,128)(2,1)} %bitcast.24), calls=%async_computation.1 | async-start | bytes 4194304 | tf_op jit(solution)/shard_map/all_to_all | solution.py:236
  13.2 3.2 %copy.17 = bf16[2,32,8,2048]{3,2,0,1:T(8,128)(2,1)} copy(bf16[2,32,8,2048]{3,2,1,0:T(8,128)(2,1)} %bitcast.25) | data formatting | bytes 4194304 | tf_op jit(solution)/shard_map/all_to_all | solution.py:236
  16.4 25.1 %all-to-all-done.1 = bf16[16,32,2048]{2,0,1:T(8,128)(2,1)S(1)} async-done(((bf16[16,32,2048]{2,0,1:T(8,128)(2,1)}), bf16[16,32,2048]{2,0,1:T(8,128)(2,1)S(1)}, u32[]{:S(2)}, u32[]{:S(2)}) %all-to-all-start.1) | async-done | bytes 2097184 | tf_op jit(solution)/shard_map/all_to_all | solution.py:236
  41.5 0.0 copy-start
  41.5 0.0 copy-start.2
  41.5 0.0 copy-start.1
  41.5 1.3 copy-done
  42.8 5.2 %all-to-all-start = ((bf16[16,32,2048]{2,0,1:T(8,128)(2,1)}), bf16[16,32,2048]{2,0,1:T(8,128)(2,1)}, u32[]{:S(2)}, u32[]{:S(2)}) async-start(bf16[16,32,2048]{2,0,1:T(8,128)(2,1)} %bitcast.23), calls=%async_computation | async-start | bytes 4194304 | tf_op jit(solution)/shard_map/all_to_all | solution.py:236
  48.0 0.0 copy-done.2
  48.0 1.3 broadcast_in_dim.29.weight_ref
  49.4 0.0 copy-done.1
  49.4 1.4 broadcast_in_dim.28.cells_ref
  50.7 9.7 %project.3.own_ref = bf16[2048,512]{1,0:T(8,128)(2,1)} custom-call(s32[2048]{0:T(1024)} %cell_ref.3, s32[2048,128]{1,0:T(8,128)} %broadcast_in_dim.28.cells_ref, f32[2048,128]{1,0:T(8,128)} %broadcast_in_dim.29.weight_ref, bf16[512,2048]{1,0:T(8,128)(2,1)} %bitcast.19), custom_call_target="tpu_custom_call" | custom-call | flops 1073741824 | bytes 8388608 | tf_op jit(solution)/shard_map/project/pallas_call | solution.py:45
  60.5 1.7 fusion.1
  62.2 2.3 %collective-permute-start.3 = (bf16[1024,512]{1,0:T(8,128)(2,1)S(1)}, bf16[1024,512]{1,0:T(8,128)(2,1)}, u32[]{:S(2)}, u32[]{:S(2)}) collective-permute-start(bf16[1024,512]{1,0:T(8,128)(2,1)S(1)} %get-tuple-element.19), channel_id=1, source_target_pairs={{1,0},{2,1},{3,2},{4,3},{5,4},{6,5},{7,6},{8,7},{9,8},{10,9},{11,1... | collective-permute-start | bytes 3145736 | tf_op jit(solution)/shard_map/ppermute | solution.py:239
  64.5 3.2 %collective-permute-start.2 = (bf16[1024,512]{1,0:T(8,128)(2,1)S(1)}, bf16[1024,512]{1,0:T(8,128)(2,1)}, u32[]{:S(2)}, u32[]{:S(2)}) collective-permute-start(bf16[1024,512]{1,0:T(8,128)(2,1)S(1)} %get-tuple-element.20), channel_id=1, source_target_pairs={{0,1},{1,2},{2,3},{3,4},{4,5},{5,6},{6,7},{7,8},{8,9},{9,10},{10,1... | collective-permute-start | bytes 3145736 | tf_op jit(solution)/shard_map/ppermute | solution.py:238
  67.7 8.8 %all-to-all-done = bf16[16,32,2048]{2,0,1:T(8,128)(2,1)} async-done(((bf16[16,32,2048]{2,0,1:T(8,128)(2,1)}), bf16[16,32,2048]{2,0,1:T(8,128)(2,1)}, u32[]{:S(2)}, u32[]{:S(2)}) %all-to-all-start) | async-done | bytes 2097184 | tf_op jit(solution)/shard_map/all_to_all | solution.py:236
  76.6 9.7 %project.2.own_ref = bf16[2048,512]{1,0:T(8,128)(2,1)} custom-call(s32[2048]{0:T(1024)} %cell_ref.3, s32[2048,128]{1,0:T(8,128)} %broadcast_in_dim.28.cells_ref, f32[2048,128]{1,0:T(8,128)} %broadcast_in_dim.29.weight_ref, bf16[512,2048]{1,0:T(8,128)(2,1)} %bitcast.2.states_ref.refs_3_), custom_call_target="tpu_custom_call" | custom-call | flops 1073741824 | bytes 8388608 | tf_op jit(solution)/shard_map/project/pallas_call | solution.py:45
  86.3 0.0 copy-start.3
  86.3 0.0 copy-start.4
  86.3 2.7 %fusion.2 = (bf16[1024,512]{1,0:T(8,128)(2,1)}, bf16[1024,512]{1,0:T(8,128)(2,1)S(1)}) fusion(bf16[2048,512]{1,0:T(8,128)(2,1)} %project.2.own_ref), kind=kLoop, calls=%fused_computation.7 | loop fusion | bytes 4194304 | tf_op jit(solution)/shard_map/slice | solution.py:239
  89.0 2.7 %collective-permute-start.1 = (bf16[1024,512]{1,0:T(8,128)(2,1)}, bf16[1024,512]{1,0:T(8,128)(2,1)}, u32[]{:S(2)}, u32[]{:S(2)}) collective-permute-start(bf16[1024,512]{1,0:T(8,128)(2,1)} %get-tuple-element.21), channel_id=1, source_target_pairs={{1,0},{2,1},{3,2},{4,3},{5,4},{6,5},{7,6},{8,7},{9,8},{10,9},{11,1... | collective-permute-start | bytes 3145736 | tf_op jit(solution)/shard_map/ppermute | solution.py:239
  91.7 2.8 %collective-permute-start = (bf16[1024,512]{1,0:T(8,128)(2,1)S(1)}, bf16[1024,512]{1,0:T(8,128)(2,1)}, u32[]{:S(2)}, u32[]{:S(2)}) collective-permute-start(bf16[1024,512]{1,0:T(8,128)(2,1)S(1)} %get-tuple-element.22), channel_id=1, source_target_pairs={{0,1},{1,2},{2,3},{3,4},{4,5},{5,6},{6,7},{7,8},{8,9},{9,10},{10,1... | collective-permute-start | bytes 3145736 | tf_op jit(solution)/shard_map/ppermute | solution.py:238
  94.6 0.0 copy-done.3
  94.6 0.0 copy-done.4
  94.6 0.1 select_bitcast_fusion
  94.7 0.0 collective-permute-done.3.high_ref
  94.7 0.0 collective-permute-done.2.low_ref
  94.7 1.4 broadcast_in_dim.14.slots_ref
  96.1 18.2 %gather_gram.2 = (bf16[16,128,512]{2,1,0:T(8,128)(2,1)}, f32[16,128,128]{2,1,0:T(8,128)}, f32[16,128,128]{2,1,0:T(8,128)}) custom-call(s32[2048,128]{1,0:T(8,128)} %broadcast_in_dim.14.slots_ref, bf16[1024,512]{1,0:T(8,128)(2,1)} %collective-permute-done.2.low_ref, bf16[2048,512]{1,0:T(8,128)(2,1)} %project.3.own_ref, ...), custom_call_target="tpu_custom_call" | custom-call | flops 8589934592 | bytes 16777216 | tf_op jit(solution)/shard_map/gather_gram/pallas_call | solution.py:101
  114.3 0.0 collective-permute-done.1.high_ref
  114.3 0.0 collective-permute-done.low_ref
  114.3 18.7 %gather_gram.3 = (bf16[16,128,512]{2,1,0:T(8,128)(2,1)}, f32[16,128,128]{2,1,0:T(8,128)}, f32[16,128,128]{2,1,0:T(8,128)}) custom-call(s32[2048,128]{1,0:T(8,128)} %broadcast_in_dim.14.slots_ref, bf16[1024,512]{1,0:T(8,128)(2,1)} %collective-permute-done.low_ref, bf16[2048,512]{1,0:T(8,128)(2,1)} %project.2.own_ref, ...), custom_call_target="tpu_custom_call" | custom-call | flops 8589934592 | bytes 16777216 | tf_op jit(solution)/shard_map/gather_gram/pallas_call | solution.py:101
  132.9 20.1 %invert_blocks.1.inverse_ref = f32[16,128,128]{2,1,0:T(8,128)} custom-call(f32[16,128,128]{2,1,0:T(8,128)} %get-tuple-element.13.gram_ref), custom_call_target="tpu_custom_call" | custom-call | tf_op jit(solution)/shard_map/invert_blocks/pallas_call | solution.py:173
  153.0 15.9 %update.1 = bf16[32,32,2048]{2,1,0:T(8,128)(2,1)} custom-call(f32[16,128,128]{2,1,0:T(8,128)} %invert_blocks.1.inverse_ref, f32[16,128,128]{2,1,0:T(8,128)} %get-tuple-element.14.moved_ref, bf16[16,128,512]{2,1,0:T(8,128)(2,1)} %get-tuple-element.15.refs_0_, bf16[16,128,512]{2,1,0:T(8,128)(2,1)} %get-tuple-element.16.refs_1_, bf16[512,2048]{1,0:T(8,128)(2,1)} %bitcast.21, ...), custom_call_target="tpu_custom_call" | custom-call | tf_op jit(solution)/shard_map/update/pallas_call | solution.py:203
  168.9 59.8 %all_to_all.54 = bf16[32,32,2048]{2,1,0:T(8,128)(2,1)S(1)} all-to-all(bf16[32,32,2048]{2,1,0:T(8,128)(2,1)} %update.1), channel_id=1, replica_groups=mesh['space'=8,'mem'=32] {'mem'}, dimensions={0} | all-to-all | bytes 8388608 | tf_op jit(solution)/shard_map/all_to_all | solution.py:245
  228.7 2.3 %copy.13 = bf16[32,4,8,2048]{3,2,0,1:T(8,128)(2,1)} copy(bf16[32,4,8,2048]{3,2,1,0:T(8,128)(2,1)S(1)} %bitcast.22) | data formatting | bytes 8388608 | tf_op jit(solution)/shard_map/all_to_all | solution.py:245
  (1 shorter events, 0.0 us)
Async XLA Ops:
  5.4 36.1 %all-to-all-start.1 = ((bf16[16,32,2048]{2,0,1:T(8,128)(2,1)}), bf16[16,32,2048]{2,0,1:T(8,128)(2,1)S(1)}, u32[]{:S(2)}, u32[]{:S(2)}) async-start(bf16[16,32,2048]{2,0,1:T(8,128)(2,1)} %bitcast.24), calls=%async_computation.1 | async-start | bytes 4194304 | tf_op jit(solution)/shard_map/all_to_all | solution.py:236
  41.5 1.3 copy-start
  41.5 6.5 %copy-start.2 = (f32[2048]{0:T(1024)S(1)}, f32[2048]{0:T(1024)}, u32[]{:S(2)}) copy-start(f32[2048]{0:T(1024)} %param.7) | copy-start | bytes 24580
  41.5 7.8 %copy-start.1 = (s32[2048]{0:T(1024)S(1)}, s32[2048]{0:T(1024)}, u32[]{:S(2)}) copy-start(s32[2048]{0:T(1024)} %cell_ref.3) | copy-start | bytes 24580
  42.8 33.7 %all-to-all-start = ((bf16[16,32,2048]{2,0,1:T(8,128)(2,1)}), bf16[16,32,2048]{2,0,1:T(8,128)(2,1)}, u32[]{:S(2)}, u32[]{:S(2)}) async-start(bf16[16,32,2048]{2,0,1:T(8,128)(2,1)} %bitcast.23), calls=%async_computation | async-start | bytes 4194304 | tf_op jit(solution)/shard_map/all_to_all | solution.py:236
  62.2 32.5 %collective-permute-start.3 = (bf16[1024,512]{1,0:T(8,128)(2,1)S(1)}, bf16[1024,512]{1,0:T(8,128)(2,1)}, u32[]{:S(2)}, u32[]{:S(2)}) collective-permute-start(bf16[1024,512]{1,0:T(8,128)(2,1)S(1)} %get-tuple-element.19), channel_id=1, source_target_pairs={{1,0},{2,1},{3,2},{4,3},{5,4},{6,5},{7,6},{8,7},{9,8},{10,9},{11,1... | collective-permute-start | bytes 3145736 | tf_op jit(solution)/shard_map/ppermute | solution.py:239
  64.5 30.2 %collective-permute-start.2 = (bf16[1024,512]{1,0:T(8,128)(2,1)S(1)}, bf16[1024,512]{1,0:T(8,128)(2,1)}, u32[]{:S(2)}, u32[]{:S(2)}) collective-permute-start(bf16[1024,512]{1,0:T(8,128)(2,1)S(1)} %get-tuple-element.20), channel_id=1, source_target_pairs={{0,1},{1,2},{2,3},{3,4},{4,5},{5,6},{6,7},{7,8},{8,9},{9,10},{10,1... | collective-permute-start | bytes 3145736 | tf_op jit(solution)/shard_map/ppermute | solution.py:238
  86.3 8.3 %copy-start.3 = (s32[16,128]{1,0:T(8,128)S(1)}, s32[16,128]{1,0:T(8,128)}, u32[]{:S(2)}) copy-start(s32[16,128]{1,0:T(8,128)} %param.8) | copy-start | bytes 24580
  86.3 8.3 %copy-start.4 = (s32[16]{0:T(128)S(1)}, s32[16]{0:T(128)}, u32[]{:S(2)}) copy-start(s32[16]{0:T(128)} %param.9) | copy-start | bytes 196
  89.0 25.3 %collective-permute-start.1 = (bf16[1024,512]{1,0:T(8,128)(2,1)}, bf16[1024,512]{1,0:T(8,128)(2,1)}, u32[]{:S(2)}, u32[]{:S(2)}) collective-permute-start(bf16[1024,512]{1,0:T(8,128)(2,1)} %get-tuple-element.21), channel_id=1, source_target_pairs={{1,0},{2,1},{3,2},{4,3},{5,4},{6,5},{7,6},{8,7},{9,8},{10,9},{11,1... | collective-permute-start | bytes 3145736 | tf_op jit(solution)/shard_map/ppermute | solution.py:239
  91.7 22.6 %collective-permute-start = (bf16[1024,512]{1,0:T(8,128)(2,1)S(1)}, bf16[1024,512]{1,0:T(8,128)(2,1)}, u32[]{:S(2)}, u32[]{:S(2)}) collective-permute-start(bf16[1024,512]{1,0:T(8,128)(2,1)S(1)} %get-tuple-element.22), channel_id=1, source_target_pairs={{0,1},{1,2},{2,3},{3,4},{4,5},{5,6},{6,7},{7,8},{8,9},{9,10},{10,1... | collective-permute-start | bytes 3145736 | tf_op jit(solution)/shard_map/ppermute | solution.py:238

commit v3 on v2

v3 whole, which is shorter than its diff:
```python
import math

import jax
import jax.numpy as jnp
from jax import lax
from jax.experimental import pallas as pl
from jax.experimental.pallas import tpu as pltpu
from jax.sharding import PartitionSpec as P

NB = 16
TILE = 256
CHUNKS = 2
SPAN = 512
SPREAD = 32

NT = (((1,), (1,)), ((), ()))
TN = (((0,), (0,)), ((), ()))


def dot(a, b, dims=(((1,), (0,)), ((), ())), precision=None):
    return lax.dot_general(a, b, dims, precision=precision, preferred_element_type=jnp.float32)


def stage_kernel(in_ref, out_ref):
    width = out_ref.shape[2]
    for at in range(out_ref.shape[0]):
        out_ref[at] = in_ref[:, at * width : (at + 1) * width]


def stage(deviations, chunk, rows, groups, per_step=8):
    width = deviations.shape[1] // groups
    return pl.pallas_call(
        stage_kernel,
        grid=(groups // per_step,),
        in_specs=[pl.BlockSpec((rows, width * per_step), lambda i: (chunk, i))],
        out_specs=pl.BlockSpec((per_step, rows, width), lambda i: (i, 0, 0)),
        out_shape=jax.ShapeDtypeStruct((groups, rows, width), deviations.dtype),
        cost_estimate=pl.CostEstimate(
            flops=0, bytes_accessed=4 * groups * rows * width, transcendentals=0
        ),
        name="stage",
    )(deviations)


def project_kernel(cell_ref, cells_ref, weight_ref, states_ref, first_ref, last_ref, acc_ref):
    tile = pl.program_id(0)
    half = pl.num_programs(0) // 2
    width = states_ref.shape[1]
    lane = lax.broadcasted_iota(jnp.int32, (TILE, 128), 1)
    begin = jnp.minimum(cell_ref[tile * TILE] // 128 * 128, width - SPAN)
    end = cell_ref[tile * TILE + TILE - 1]
    cells = cells_ref[...]

    def picked(cells, start):
        start = pl.multiple_of(start, 128)
        pick = jnp.concatenate(
            [(cells == lane + (start + at)).astype(jnp.float32) for at in range(0, SPAN, 128)], axis=1
        ).astype(jnp.bfloat16)
        return dot(pick, states_ref[:, pl.ds(start, SPAN)], NT)

    acc_ref[...] = picked(cells, begin)

    def add(step, carry):
        lower = begin + step * SPAN
        acc_ref[...] += picked(
            jnp.where(cells >= lower, cells, -1), jnp.minimum(lower, width - SPAN)
        )
        return carry

    lax.fori_loop(1, (end - begin) // SPAN + 1, add, 0)
    done = (acc_ref[...] * weight_ref[:, 0:1]).astype(jnp.bfloat16)

    @pl.when(tile < half)
    def _():
        first_ref[...] = done

    @pl.when(tile >= half)
    def _():
        last_ref[...] = done


def project(obs_cell, cells, weight, states):
    members, width = states.shape
    obs = obs_cell.shape[0]
    half = obs // TILE // 2
    side = jax.ShapeDtypeStruct((obs // 2, members), jnp.bfloat16)
    return pl.pallas_call(
        project_kernel,
        grid_spec=pltpu.PrefetchScalarGridSpec(
            num_scalar_prefetch=1,
            grid=(obs // TILE,),
            in_specs=[
                pl.BlockSpec((TILE, 128), lambda i, c: (i, 0)),
                pl.BlockSpec((TILE, 128), lambda i, c: (i, 0)),
                pl.BlockSpec((members, width), lambda i, c: (0, 0)),
            ],
            out_specs=(
                pl.BlockSpec((TILE, members), lambda i, c: (jnp.minimum(i, half - 1), 0)),
                pl.BlockSpec((TILE, members), lambda i, c: (jnp.maximum(i - half, 0), 0)),
            ),
            scratch_shapes=[pltpu.VMEM((TILE, members), jnp.float32)],
        ),
        out_shape=(side, side),
        cost_estimate=pl.CostEstimate(
            flops=2 * obs * members * SPAN, bytes_accessed=8 * obs * members, transcendentals=0
        ),
        name="project",
    )(obs_cell, cells, weight, states)


def gram_kernel(slot_ref, *refs):
    pieces, states = refs[: 4 * CHUNKS], refs[4 * CHUNKS : 5 * CHUNKS]
    columns_ref, gram_ref, moved_ref, rows_ref, picked_ref = refs[5 * CHUNKS :]
    block = pl.program_id(0)
    edge, part = pieces[0].shape
    tiles = part // 128
    width = CHUNKS * tiles
    kslots = gram_ref.shape[1]

    def gather(block, slot):
        for k in range(kslots):
            row = pl.multiple_of(slot_ref[block * kslots + k] * width, width)
            picked_ref[slot, k * width : (k + 1) * width, :] = rows_ref[pl.ds(row, width), :]

    @pl.when(block == 0)
    def _():
        for side in range(4):
            for chunk in range(CHUNKS):
                source = pieces[chunk * 4 + side]

                def spread(step, carry):
                    start = pl.multiple_of(step * SPREAD, SPREAD)
                    for tile in range(tiles):
                        value = source[pl.ds(start, SPREAD), tile * 128 : (tile + 1) * 128]
                        row = (side * edge + start) * width + chunk * tiles + tile
                        rows_ref[pl.ds(row, SPREAD, stride=width), :] = value.astype(jnp.float32)
                    return carry

                lax.fori_loop(0, edge // SPREAD, spread, 0)
        rows_ref[4 * edge * width :, :] = jnp.zeros((width, 128), jnp.float32)
        gather(0, 0)

    now = lax.rem(block, 2)
    gather(jnp.minimum(block + 1, pl.num_programs(0) - 1), 1 - now)
    chosen = jnp.concatenate(
        [picked_ref[now, pl.ds(at, kslots, stride=width), :].astype(jnp.bfloat16) for at in range(width)],
        axis=1,
    )
    columns_ref[0] = chosen
    gram_ref[0] = dot(chosen, chosen, NT)
    moved = 0.0
    for chunk in range(CHUNKS):
        moved = moved + dot(chosen[:, chunk * part : (chunk + 1) * part], states[chunk][...])
    moved_ref[0] = moved


def gather_gram(slots, pieces, states, blocks):
    part, width = states[0].shape
    members = part * CHUNKS
    edge = pieces[0].shape[0]
    kslots = slots.shape[0] // blocks
    square = pl.BlockSpec((1, kslots, kslots), lambda i, s: (i, 0, 0))
    squares = jax.ShapeDtypeStruct((blocks, kslots, kslots), jnp.float32)
    lanes = members // 128
    return pl.pallas_call(
        gram_kernel,
        grid_spec=pltpu.PrefetchScalarGridSpec(
            num_scalar_prefetch=1,
            grid=(blocks,),
            in_specs=[pl.BlockSpec((edge, part), lambda i, s: (0, 0), pipeline_mode=pl.Buffered(1))] * len(pieces)
            + [pl.BlockSpec((part, width // blocks), lambda i, s: (0, i))] * CHUNKS,
            out_specs=(
                pl.BlockSpec((1, kslots, members), lambda i, s: (i, 0, 0)),
                square,
                square,
            ),
            scratch_shapes=[
                pltpu.VMEM(((4 * edge + 1) * lanes, 128), jnp.float32),
                pltpu.VMEM((2, kslots * lanes, 128), jnp.float32),
            ],
        ),
        out_shape=(jax.ShapeDtypeStruct((blocks, kslots, members), jnp.bfloat16), squares, squares),
        compiler_params=pltpu.CompilerParams(vmem_limit_bytes=48 * 1024 * 1024),
        cost_estimate=pl.CostEstimate(
            flops=4 * blocks * kslots * kslots * members,
            bytes_accessed=16 * members * width,
            transcendentals=0,
        ),
        name="gather_gram",
    )(slots, *pieces, *states)


def three_way(v):
    hi = v.astype(jnp.bfloat16)
    rest = v - hi.astype(jnp.float32)
    mid = rest.astype(jnp.bfloat16)
    low = (rest - mid.astype(jnp.float32)).astype(jnp.bfloat16)
    return hi, mid, low


def invert_kernel(gram_ref, out_ref, work):
    nblk, n, _ = gram_ref.shape
    lane = lax.broadcasted_iota(jnp.int32, (1, 1, n), 2)
    sub = lax.broadcasted_iota(jnp.int32, (1, NB, 1), 1)
    lane2 = lax.broadcasted_iota(jnp.int32, (1, n), 1)
    rows = lax.broadcasted_iota(jnp.int32, (1, n, n), 1)
    cols = lax.broadcasted_iota(jnp.int32, (1, n, n), 2)
    work[...] = gram_ref[...] + jnp.where(rows == cols, 1.0, 0.0)

    def step(number, carry):
        panel = work[:, 0:NB, :]
        flip = lane2 >= n - number * NB
        sides = jnp.where(flip[None], -panel, panel)
        for k in range(NB):
            row = panel[:, k : k + 1, :]
            col = panel[:, :, k : k + 1]
            inv = 1.0 / panel[:, k : k + 1, k : k + 1]
            scaled = jnp.where(lane == k, inv, row * inv)
            panel = jnp.where(sub == k, scaled, jnp.where(lane == k, 0.0, panel) - col * scaled)
        for b in range(nblk):
            rolled = pltpu.roll(panel[b], n - NB, 1)
            rh, rm, rl = three_way(rolled)
            ch, cm, cl = three_way(sides[b])
            rhs = jnp.concatenate([rh, rm, rh, rl, rm, rh, rl, rm], axis=0)
            lhs = jnp.concatenate([ch, ch, cm, ch, cm, cl, cm, cl], axis=0)
            change = dot(lhs, rhs, TN)
            kept = pltpu.roll(jnp.where(lane2 < NB, 0.0, work[b, NB:n, :]), n - NB, 1)
            work[b, 0 : n - NB, :] = kept - change[NB:n]
            work[b, n - NB : n, :] = rolled
        return carry

    lax.fori_loop(0, n // NB, step, 0)
    out_ref[...] = work[...]


def invert(gram):
    return pl.pallas_call(
        invert_kernel,
        out_shape=jax.ShapeDtypeStruct(gram.shape, jnp.float32),
        scratch_shapes=[pltpu.VMEM(gram.shape, jnp.float32)],
        name="invert_blocks",
    )(gram)


def update_kernel(inverse_ref, moved_ref, columns_ref, *refs):
    states, out_ref = refs[:-1], refs[-1]
    groups = out_ref.shape[0]
    part = states[0].shape[0]
    rows = part // groups
    for at in range(inverse_ref.shape[0]):
        wh, wm, wl = three_way(inverse_ref[at])
        mh, mm, ml = three_way(moved_ref[at] * 0.5)
        solved = dot(
            jnp.concatenate([wh, wh, wm, wh, wl, wm], axis=1),
            jnp.concatenate([mh, mm, mh, ml, mh, mm], axis=0),
        )
        high = solved.astype(jnp.bfloat16)
        low = (solved - high.astype(jnp.float32)).astype(jnp.bfloat16)
        both = jnp.concatenate([high, low], axis=0)
        columns = columns_ref[at].T
        twice = jnp.concatenate([columns, columns], axis=1)
        cells = slice(at * 128, at * 128 + 128)
        for chunk, states_ref in enumerate(states):
            change = dot(twice[chunk * part : (chunk + 1) * part], both)
            updated = (states_ref[:, cells].astype(jnp.float32) - change).astype(jnp.bfloat16)
            out_ref[:, chunk * rows : (chunk + 1) * rows, cells] = updated.reshape(groups, rows, 128)


def update(inverse, moved, columns, states, groups, per_step=2):
    blocks, kslots, _ = inverse.shape
    square = pl.BlockSpec((per_step, kslots, kslots), lambda i: (i, 0, 0))
    members = columns.shape[2]
    part, width = states[0].shape
    return pl.pallas_call(
        update_kernel,
        grid=(blocks // per_step,),
        in_specs=[square, square, pl.BlockSpec((per_step, kslots, members), lambda i: (i, 0, 0))]
        + [pl.BlockSpec((part, per_step * kslots), lambda i: (0, i))] * len(states),
        out_specs=pl.BlockSpec((groups, members // groups, per_step * kslots), lambda i: (0, 0, i)),
        out_shape=jax.ShapeDtypeStruct((groups, members // groups, width), jnp.bfloat16),
        name="update",
    )(inverse, moved, columns, *states)


def on_device(deviations, obs_cell, obs_weight, block_obs, block_count):
    groups = lax.axis_size("mem")
    members = deviations.shape[0] * groups
    obs_dev = obs_cell.shape[0]
    weight = obs_weight * (1.0 / math.sqrt(members - 1))
    cells = jnp.broadcast_to(obs_cell[:, None], (obs_dev, 128))
    weights = jnp.broadcast_to(weight[:, None], (obs_dev, 128))
    line_index = lax.axis_index("space") * groups + lax.axis_index("mem")
    local_index = block_obs - (line_index * obs_dev - obs_dev // 2)
    slot_ids = jnp.arange(block_obs.shape[1], dtype=jnp.int32)
    slots = jnp.where(slot_ids[None, :] < block_count[:, None], local_index, 2 * obs_dev).reshape(-1)
    size = lax.axis_size("space") * groups
    up = [(i, i + 1) for i in range(size - 1)]
    down = [(b, a) for a, b in up]
    rows = deviations.shape[0] // CHUNKS
    states, pieces = [], []
    for chunk in range(CHUNKS):
        part = stage(deviations, chunk, rows, groups)
        part = lax.all_to_all(part, "mem", split_axis=0, concat_axis=0, tiled=True)
        states.append(part.reshape(groups * rows, -1))
        first, last = project(obs_cell, cells, weights, states[-1])
        low = lax.ppermute(last, ("space", "mem"), up)
        high = lax.ppermute(first, ("space", "mem"), down)
        pieces += [low, first, last, high]
    columns, gram, moved = gather_gram(slots, pieces, states, block_obs.shape[0])
    analysis = update(invert(gram), moved, columns, states, groups)
    return lax.all_to_all(
        analysis.reshape(members, -1), "mem", split_axis=0, concat_axis=1, tiled=True
    )


def solution(mesh):
    in_specs = (
        P("mem", "space"),
        P(("space", "mem")),
        P(("space", "mem")),
        P(("space", "mem"), None),
        P(("space", "mem")),
    )
    out_specs = P("mem", "space")
    return jax.shard_map(
        on_device, mesh=mesh, in_specs=in_specs, out_specs=out_specs, check_vma=False
    )
```

time: 233 us -> 235 us (level)
  waiting for transfers between devices: 34 us -> 56.3 us
  Pallas kernels: 92.3 us -> 76.8 us
  local copies, waits for them, and re-layouts: 20.7 us -> 7.09 us
  blocking collectives: 59.8 us -> 65.6 us
  starting transfers between devices: 24 us -> 27.3 us
    ppermute x4, waiting for transfers between devices: 0.01 us -> 15.4 us  [the longest x2 8.91 us: on_device(): high = lax.ppermute(first, ('space', 'mem'), down)]
    pallas_call x3 -> x4, Pallas kernels: 52.7 us -> 39.2 us  [the longest x1 20.3 us: gather_gram(): pl.pallas_call(gram_kernel, grid_spec=pltpu.PrefetchScalarGridSpec(num_sc...]
    slice x3 -> x0, local copies, waits for them, and re-layouts: 8.18 us -> none  [the longest x2 4.37 us: on_device(): high = lax.ppermute(own[:edge], ('space', 'mem'), down)]
    all_to_all x2, waiting for transfers between devices: 34 us -> 41 us  [on_device(): part = lax.all_to_all(part, 'mem', split_axis=0, concat_axis=0, tiled=True)]
    all_to_all x1, blocking collectives: 59.8 us -> 65.6 us  [on_device(): lax.all_to_all(analysis.reshape(members, -1), 'mem', split_axis=0, concat...]
    all_to_all x2 -> x0, local copies, waits for them, and re-layouts: 4.78 us -> none  [on_device(): lax.all_to_all(part, 'mem', split_axis=1, concat_axis=0, tiled=True)]
    ppermute x4, starting transfers between devices: 11.1 us -> 14.4 us  [the longest x2 9.38 us: on_device(): high = lax.ppermute(first, ('space', 'mem'), down)]
  transfers between devices with their start and end apart: 6 -> 6, of which waited for: 2 -> 5; matrix products, arithmetic and copies ran while one was open for 5% -> 1% of each run, Pallas kernels for 16% -> 6%
where the time goes in v3:
time: 235 us; the launch traced here: 233 us
  Pallas kernels  76.8 us (33%)
  blocking collectives  65.6 us (28%)
  waiting for transfers between devices  56.3 us (24%)
  starting transfers between devices  27.3 us (12%)
  local copies, waits for them, and re-layouts  7.09 us (3%)
    all_to_all x1, blocking collectives, on_device(): lax.all_to_all(analysis.reshape(members, -1), 'mem', split_axis=0, concat...  65.6 us
    all_to_all x2, waiting for transfers between devices, on_device(): part = lax.all_to_all(part, 'mem', split_axis=0, concat_axis=0, tiled=True)  41 us
    pallas_call x1, Pallas kernels, gather_gram(): pl.pallas_call(gram_kernel, grid_spec=pltpu.PrefetchScalarGridSpec(num_sc...  20.3 us
    pallas_call x1, Pallas kernels, invert(): pl.pallas_call(invert_kernel, out_shape=jax.ShapeDtypeStruct(gram.shape,...  19.2 us
    pallas_call x2, Pallas kernels, project(): pl.pallas_call(project_kernel, grid_spec=pltpu.PrefetchScalarGridSpec(num...  18.4 us
    all_to_all x2, starting transfers between devices, on_device(): part = lax.all_to_all(part, 'mem', split_axis=0, concat_axis=0, tiled=True)  12.9 us
    pallas_call x1, Pallas kernels, update(): pl.pallas_call(update_kernel, grid=(blocks // per_step,), in_specs=[squar...  11.3 us
    ppermute x2, starting transfers between devices, on_device(): high = lax.ppermute(first, ('space', 'mem'), down)  9.38 us
  transfers between devices with their start and end apart: 6, of which 5 were waited for; matrix products, arithmetic and copies ran while one was open for 1% of the time, Pallas kernels for 6%

profile of v3, /device:TPU:97, one launch (start us, length us, event | category | flops | bytes accessed | tf_op | source)
XLA Modules:
  0.0 233.3 jit_solution(9997357386777794266)
XLA Ops:
  0.0 3.8 %stage.2 = bf16[32,16,2048]{2,1,0:T(8,128)(2,1)} custom-call(bf16[32,65536]{1,0:T(8,128)(2,1)} %in_ref.3), custom_call_target="tpu_custom_call" | custom-call | bytes 4194304 | tf_op jit(solution)/shard_map/stage/pallas_call | solution.py:32
  3.8 7.8 %all-to-all-start = ((bf16[32,16,2048]{2,1,0:T(8,128)(2,1)}), bf16[32,16,2048]{2,1,0:T(8,128)(2,1)S(1)}, u32[]{:S(2)}, u32[]{:S(2)}) async-start(bf16[32,16,2048]{2,1,0:T(8,128)(2,1)} %stage.2), calls=%async_computation | async-start | bytes 4194304 | tf_op jit(solution)/shard_map/all_to_all | solution.py:303
  11.5 0.0 copy-start.6
  11.6 3.8 %stage.3 = bf16[32,16,2048]{2,1,0:T(8,128)(2,1)} custom-call(bf16[32,65536]{1,0:T(8,128)(2,1)} %in_ref.3), custom_call_target="tpu_custom_call" | custom-call | bytes 4194304 | tf_op jit(solution)/shard_map/stage/pallas_call | solution.py:32
  15.4 0.0 copy-start.5
  15.4 24.5 %all-to-all-done = bf16[32,16,2048]{2,1,0:T(8,128)(2,1)S(1)} async-done(((bf16[32,16,2048]{2,1,0:T(8,128)(2,1)}), bf16[32,16,2048]{2,1,0:T(8,128)(2,1)S(1)}, u32[]{:S(2)}, u32[]{:S(2)}) %all-to-all-start) | async-done | bytes 2097184 | tf_op jit(solution)/shard_map/all_to_all | solution.py:303
  39.9 0.0 copy-start.4
  39.9 5.2 %all-to-all-start.1 = ((bf16[32,16,2048]{2,1,0:T(8,128)(2,1)}), bf16[32,16,2048]{2,1,0:T(8,128)(2,1)}, u32[]{:S(2)}, u32[]{:S(2)}) async-start(bf16[32,16,2048]{2,1,0:T(8,128)(2,1)} %stage.3), calls=%async_computation.1 | async-start | bytes 4194304 | tf_op jit(solution)/shard_map/all_to_all | solution.py:303
  45.1 0.0 copy-done.6
  45.1 1.4 broadcast_in_dim.9.weight_ref
  46.5 0.0 copy-done.5
  46.5 1.3 broadcast_in_dim.8.cells_ref
  47.8 0.0 copy-done.4
  47.8 0.0 copy-start.7
  47.8 0.0 copy-start.8
  47.8 9.3 %project.2 = (bf16[1024,512]{1,0:T(8,128)(2,1)}, bf16[1024,512]{1,0:T(8,128)(2,1)}) custom-call(s32[2048]{0:T(1024)} %cell_ref.3, s32[2048,128]{1,0:T(8,128)} %broadcast_in_dim.8.cells_ref, f32[2048,128]{1,0:T(8,128)} %broadcast_in_dim.9.weight_ref, bf16[512,2048]{1,0:T(8,128)(2,1)} %bitcast.7), custom_call_target="tpu_custom_call" | custom-call | flops 1073741824 | bytes 8388608 | tf_op jit(solution)/shard_map/project/pallas_call | solution.py:87
  57.0 0.0 copy-start.3
  57.0 0.0 copy-start.2
  57.0 16.5 %all-to-all-done.1 = bf16[32,16,2048]{2,1,0:T(8,128)(2,1)} async-done(((bf16[32,16,2048]{2,1,0:T(8,128)(2,1)}), bf16[32,16,2048]{2,1,0:T(8,128)(2,1)}, u32[]{:S(2)}, u32[]{:S(2)}) %all-to-all-start.1) | async-done | bytes 2097184 | tf_op jit(solution)/shard_map/all_to_all | solution.py:303
  73.5 9.1 %project.3 = (bf16[1024,512]{1,0:T(8,128)(2,1)}, bf16[1024,512]{1,0:T(8,128)(2,1)}) custom-call(s32[2048]{0:T(1024)} %cell_ref.3, s32[2048,128]{1,0:T(8,128)} %broadcast_in_dim.8.cells_ref, f32[2048,128]{1,0:T(8,128)} %broadcast_in_dim.9.weight_ref, bf16[512,2048]{1,0:T(8,128)(2,1)} %bitcast.2.states_ref.refs_9_.refs_1_), custom_call_target="tpu_custom_call" | custom-call | flops 1073741824 | bytes 8388608 | tf_op jit(solution)/shard_map/project/pallas_call | solution.py:87
  82.7 2.1 collective-permute-start.2
  84.7 2.6 %collective-permute-start.3 = (bf16[1024,512]{1,0:T(8,128)(2,1)}, bf16[1024,512]{1,0:T(8,128)(2,1)}, u32[]{:S(2)}, u32[]{:S(2)}) collective-permute-start(bf16[1024,512]{1,0:T(8,128)(2,1)} %get-tuple-element.15.refs_5_), channel_id=1, source_target_pairs={{1,0},{2,1},{3,2},{4,3},{5,4},{6,5},{7,6},{8,7},{9,8},{10,9},{11,1... | collective-permute-start | bytes 3145736 | tf_op jit(solution)/shard_map/ppermute | solution.py:307
  87.3 0.0 copy-done.3
  87.3 3.0 %collective-permute-start = (bf16[1024,512]{1,0:T(8,128)(2,1)S(1)}, bf16[1024,512]{1,0:T(8,128)(2,1)S(1)}, u32[]{:S(2)}, u32[]{:S(2)}) collective-permute-start(bf16[1024,512]{1,0:T(8,128)(2,1)S(1)} %copy-done.3), channel_id=1, source_target_pairs={{0,1},{1,2},{2,3},{3,4},{4,5},{5,6},{6,7},{7,8},{8,9},{9,10},{10,1... | collective-permute-start | bytes 3145736 | tf_op jit(solution)/shard_map/ppermute | solution.py:306
  90.3 0.0 copy-done.2
  90.3 6.8 %collective-permute-start.1 = (bf16[1024,512]{1,0:T(8,128)(2,1)S(1)}, bf16[1024,512]{1,0:T(8,128)(2,1)}, u32[]{:S(2)}, u32[]{:S(2)}) collective-permute-start(bf16[1024,512]{1,0:T(8,128)(2,1)S(1)} %copy-done.2), channel_id=1, source_target_pairs={{1,0},{2,1},{3,2},{4,3},{5,4},{6,5},{7,6},{8,7},{9,8},{10,9},{11,1... | collective-permute-start | bytes 3145736 | tf_op jit(solution)/shard_map/ppermute | solution.py:307
  97.1 0.0 copy-done.7
  97.2 0.0 copy-done.8
  97.2 0.1 select_bitcast_fusion.slot_ref
  97.2 0.0 collective-permute-done.2.refs_4_
  97.2 4.2 %collective-permute-done.3.refs_7_ = bf16[1024,512]{1,0:T(8,128)(2,1)} collective-permute-done((bf16[1024,512]{1,0:T(8,128)(2,1)}, bf16[1024,512]{1,0:T(8,128)(2,1)}, u32[]{:S(2)}, u32[]{:S(2)}) %collective-permute-start.3) | collective-permute-done | bytes 1048608 | tf_op jit(solution)/shard_map/ppermute | solution.py:307
  101.5 6.4 %collective-permute-done.refs_0_ = bf16[1024,512]{1,0:T(8,128)(2,1)S(1)} collective-permute-done((bf16[1024,512]{1,0:T(8,128)(2,1)S(1)}, bf16[1024,512]{1,0:T(8,128)(2,1)S(1)}, u32[]{:S(2)}, u32[]{:S(2)}) %collective-permute-start) | collective-permute-done | bytes 1048608 | tf_op jit(solution)/shard_map/ppermute | solution.py:306
  107.9 4.7 %collective-permute-done.1.refs_3_ = bf16[1024,512]{1,0:T(8,128)(2,1)} collective-permute-done((bf16[1024,512]{1,0:T(8,128)(2,1)S(1)}, bf16[1024,512]{1,0:T(8,128)(2,1)}, u32[]{:S(2)}, u32[]{:S(2)}) %collective-permute-start.1) | collective-permute-done | bytes 1048608 | tf_op jit(solution)/shard_map/ppermute | solution.py:307
  112.6 20.3 %gather_gram.1 = (bf16[16,128,1024]{2,1,0:T(8,128)(2,1)}, f32[16,128,128]{2,1,0:T(8,128)S(1)}, f32[16,128,128]{2,1,0:T(8,128)S(1)}) custom-call(s32[2048]{0:T(1024)S(1)} %select_bitcast_fusion.slot_ref, bf16[1024,512]{1,0:T(8,128)(2,1)S(1)} %collective-permute-done.refs_0_, bf16[1024,512]{1,0:T(8,128)(2,1)S(1)} %copy-done.2, ...), custom_call_target="tpu_custom_call" | custom-call | flops 1073741824 | bytes 33554432 | tf_op jit(solution)/shard_map/gather_gram/pallas_call | solution.py:165
  132.9 0.0 copy-start
  132.9 1.1 copy-done
  134.0 0.0 copy-start.1
  134.0 1.0 copy-done.1
  135.0 19.2 %invert_blocks.1.inverse_ref = f32[16,128,128]{2,1,0:T(8,128)} custom-call(f32[16,128,128]{2,1,0:T(8,128)} %copy-done.1), custom_call_target="tpu_custom_call" | custom-call | tf_op jit(solution)/shard_map/invert_blocks/pallas_call | solution.py:237
  154.2 11.3 %update.1 = bf16[32,32,2048]{2,1,0:T(8,128)(2,1)} custom-call(f32[16,128,128]{2,1,0:T(8,128)} %invert_blocks.1.inverse_ref, f32[16,128,128]{2,1,0:T(8,128)} %copy-done, bf16[16,128,1024]{2,1,0:T(8,128)(2,1)} %get-tuple-element.18.columns_ref, bf16[512,2048]{1,0:T(8,128)(2,1)} %bitcast.9, bf16[512,2048]{1,0:T(8,128)(2,1)} %bitcast.2.states_ref.refs_9_.refs_1_), custom_call_target="tpu_custom_call" | custom-call | tf_op jit(solution)/shard_map/update/pallas_call | solution.py:274
  165.4 65.6 %all_to_all.26 = bf16[32,32,2048]{2,1,0:T(8,128)(2,1)S(1)} all-to-all(bf16[32,32,2048]{2,1,0:T(8,128)(2,1)} %update.1), channel_id=1, replica_groups=mesh['space'=8,'mem'=32] {'mem'}, dimensions={0} | all-to-all | bytes 8388608 | tf_op jit(solution)/shard_map/all_to_all | solution.py:311
  231.0 2.3 copy.7
  (1 shorter events, 0.0 us)
Async XLA Ops:
  3.8 36.1 %all-to-all-start = ((bf16[32,16,2048]{2,1,0:T(8,128)(2,1)}), bf16[32,16,2048]{2,1,0:T(8,128)(2,1)S(1)}, u32[]{:S(2)}, u32[]{:S(2)}) async-start(bf16[32,16,2048]{2,1,0:T(8,128)(2,1)} %stage.2), calls=%async_computation | async-start | bytes 4194304 | tf_op jit(solution)/shard_map/all_to_all | solution.py:303
  11.5 33.5 %copy-start.6 = (f32[2048]{0:T(1024)S(1)}, f32[2048]{0:T(1024)}, u32[]{:S(2)}) copy-start(f32[2048]{0:T(1024)} %param.7) | copy-start | bytes 24580
  15.4 31.1 %copy-start.5 = (s32[2048]{0:T(1024)S(1)}, s32[2048]{0:T(1024)}, u32[]{:S(2)}) copy-start(s32[2048]{0:T(1024)} %cell_ref.3) | copy-start | bytes 24580
  39.9 7.9 %copy-start.4 = (bf16[32,16,2048]{2,1,0:T(8,128)(2,1)}, bf16[32,16,2048]{2,1,0:T(8,128)(2,1)S(1)}, u32[]{:S(2)}) copy-start(bf16[32,16,2048]{2,1,0:T(8,128)(2,1)S(1)} %all-to-all-done) | copy-start | bytes 6291460
  39.9 33.6 %all-to-all-start.1 = ((bf16[32,16,2048]{2,1,0:T(8,128)(2,1)}), bf16[32,16,2048]{2,1,0:T(8,128)(2,1)}, u32[]{:S(2)}, u32[]{:S(2)}) async-start(bf16[32,16,2048]{2,1,0:T(8,128)(2,1)} %stage.3), calls=%async_computation.1 | async-start | bytes 4194304 | tf_op jit(solution)/shard_map/all_to_all | solution.py:303
  47.8 49.4 %copy-start.7 = (s32[16,128]{1,0:T(8,128)S(1)}, s32[16,128]{1,0:T(8,128)}, u32[]{:S(2)}) copy-start(s32[16,128]{1,0:T(8,128)} %param.8) | copy-start | bytes 24580
  47.8 49.4 %copy-start.8 = (s32[16]{0:T(128)S(1)}, s32[16]{0:T(128)}, u32[]{:S(2)}) copy-start(s32[16]{0:T(128)} %param.9) | copy-start | bytes 196
  57.0 30.3 %copy-start.3 = (bf16[1024,512]{1,0:T(8,128)(2,1)S(1)}, bf16[1024,512]{1,0:T(8,128)(2,1)}, u32[]{:S(2)}) copy-start(bf16[1024,512]{1,0:T(8,128)(2,1)} %get-tuple-element.12.refs_2_) | copy-start | bytes 3145732
  57.0 33.3 %copy-start.2 = (bf16[1024,512]{1,0:T(8,128)(2,1)S(1)}, bf16[1024,512]{1,0:T(8,128)(2,1)}, u32[]{:S(2)}) copy-start(bf16[1024,512]{1,0:T(8,128)(2,1)} %get-tuple-element.13.refs_1_) | copy-start | bytes 3145732
  82.7 14.6 %collective-permute-start.2 = (bf16[1024,512]{1,0:T(8,128)(2,1)}, bf16[1024,512]{1,0:T(8,128)(2,1)}, u32[]{:S(2)}, u32[]{:S(2)}) collective-permute-start(bf16[1024,512]{1,0:T(8,128)(2,1)} %get-tuple-element.14.refs_6_), channel_id=1, source_target_pairs={{0,1},{1,2},{2,3},{3,4},{4,5},{5,6},{6,7},{7,8},{8,9},{9,10},{10,1... | collective-permute-start | bytes 3145736 | tf_op jit(solution)/shard_map/ppermute | solution.py:306
  84.7 16.7 %collective-permute-start.3 = (bf16[1024,512]{1,0:T(8,128)(2,1)}, bf16[1024,512]{1,0:T(8,128)(2,1)}, u32[]{:S(2)}, u32[]{:S(2)}) collective-permute-start(bf16[1024,512]{1,0:T(8,128)(2,1)} %get-tuple-element.15.refs_5_), channel_id=1, source_target_pairs={{1,0},{2,1},{3,2},{4,3},{5,4},{6,5},{7,6},{8,7},{9,8},{10,9},{11,1... | collective-permute-start | bytes 3145736 | tf_op jit(solution)/shard_map/ppermute | solution.py:307
  87.3 20.6 %collective-permute-start = (bf16[1024,512]{1,0:T(8,128)(2,1)S(1)}, bf16[1024,512]{1,0:T(8,128)(2,1)S(1)}, u32[]{:S(2)}, u32[]{:S(2)}) collective-permute-start(bf16[1024,512]{1,0:T(8,128)(2,1)S(1)} %copy-done.3), channel_id=1, source_target_pairs={{0,1},{1,2},{2,3},{3,4},{4,5},{5,6},{6,7},{7,8},{8,9},{9,10},{10,1... | collective-permute-start | bytes 3145736 | tf_op jit(solution)/shard_map/ppermute | solution.py:306
  90.3 22.3 %collective-permute-start.1 = (bf16[1024,512]{1,0:T(8,128)(2,1)S(1)}, bf16[1024,512]{1,0:T(8,128)(2,1)}, u32[]{:S(2)}, u32[]{:S(2)}) collective-permute-start(bf16[1024,512]{1,0:T(8,128)(2,1)S(1)} %copy-done.2), channel_id=1, source_target_pairs={{1,0},{2,1},{3,2},{4,3},{5,4},{6,5},{7,6},{8,7},{9,8},{10,9},{11,1... | collective-permute-start | bytes 3145736 | tf_op jit(solution)/shard_map/ppermute | solution.py:307
  132.9 1.1 copy-start
  134.0 1.0 copy-start.1

commit v4 on v3

--- a/solution.py
+++ b/solution.py
@@ -7,11 +7,13 @@
 from jax.experimental.pallas import tpu as pltpu
 from jax.sharding import PartitionSpec as P
 
+
 NB = 16
-TILE = 256
+TILE = 512
 CHUNKS = 2
-SPAN = 512
-SPREAD = 32
+SPAN = 640
+GRAM_STEP = 4
+SPREAD = 64
 
 NT = (((1,), (1,)), ((), ()))
 TN = (((0,), (0,)), ((), ()))
@@ -110,77 +112,80 @@
 
 def gram_kernel(slot_ref, *refs):
     pieces, states = refs[: 4 * CHUNKS], refs[4 * CHUNKS : 5 * CHUNKS]
-    columns_ref, gram_ref, moved_ref, rows_ref, picked_ref = refs[5 * CHUNKS :]
-    block = pl.program_id(0)
+    columns_ref, gram_ref, moved_ref, landed_ref, rows_ref, picked_ref, sems = refs[5 * CHUNKS :]
+    step = pl.program_id(0)
     edge, part = pieces[0].shape
     tiles = part // 128
     width = CHUNKS * tiles
-    kslots = gram_ref.shape[1]
-
-    def gather(block, slot):
+    per_step, kslots, _ = gram_ref.shape
+
+    @pl.when(step == 0)
+    def _():
+        copies = [
+            pltpu.make_async_copy(piece, landed_ref.at[at], sems.at[at]) for at, piece in enumerate(pieces)
+        ]
+        order = [chunk * 4 + side for side in (1, 2, 0, 3) for chunk in range(CHUNKS)]
+        for at in order:
+            copies[at].start()
+        rows_ref[4 * edge * width :, :] = jnp.zeros((width, 128), jnp.float32)
+        for at in order:
+            chunk, side = divmod(at, 4)
+            copies[at].wait()
+
+            def spread(turn, carry):
+                start = pl.multiple_of(turn * SPREAD, SPREAD)
+                for tile in range(tiles):
+                    value = landed_ref[at, pl.ds(start, SPREAD), tile * 128 : (tile + 1) * 128]
+                    row = (side * edge + start) * width + chunk * tiles + tile
+                    rows_ref[pl.ds(row, SPREAD, stride=width), :] = value.astype(jnp.float32)
+                return carry
+
+            lax.fori_loop(0, edge // SPREAD, spread, 0)
+
+    for j in range(per_step):
         for k in range(kslots):
-            row = pl.multiple_of(slot_ref[block * kslots + k] * width, width)
-            picked_ref[slot, k * width : (k + 1) * width, :] = rows_ref[pl.ds(row, width), :]
-
-    @pl.when(block == 0)
-    def _():
-        for side in range(4):
-            for chunk in range(CHUNKS):
-                source = pieces[chunk * 4 + side]
-
-                def spread(step, carry):
-                    start = pl.multiple_of(step * SPREAD, SPREAD)
-                    for tile in range(tiles):
-                        value = source[pl.ds(start, SPREAD), tile * 128 : (tile + 1) * 128]
-                        row = (side * edge + start) * width + chunk * tiles + tile
-                        rows_ref[pl.ds(row, SPREAD, stride=width), :] = value.astype(jnp.float32)
-                    return carry
-
-                lax.fori_loop(0, edge // SPREAD, spread, 0)
-        rows_ref[4 * edge * width :, :] = jnp.zeros((width, 128), jnp.float32)
-        gather(0, 0)
-
-    now = lax.rem(block, 2)
-    gather(jnp.minimum(block + 1, pl.num_programs(0) - 1), 1 - now)
-    chosen = jnp.concatenate(
-        [picked_ref[now, pl.ds(at, kslots, stride=width), :].astype(jnp.bfloat16) for at in range(width)],
-        axis=1,
-    )
-    columns_ref[0] = chosen
-    gram_ref[0] = dot(chosen, chosen, NT)
-    moved = 0.0
-    for chunk in range(CHUNKS):
-        moved = moved + dot(chosen[:, chunk * part : (chunk + 1) * part], states[chunk][...])
-    moved_ref[0] = moved
-
-
-def gather_gram(slots, pieces, states, blocks):
+            row = pl.multiple_of(slot_ref[(step * per_step + j) * kslots + k], width)
+            picked_ref[j, k * width : (k + 1) * width, :] = rows_ref[pl.ds(row, width), :]
+    for j in range(per_step):
+        chosen = jnp.concatenate(
+            [picked_ref[j, pl.ds(at, kslots, stride=width), :].astype(jnp.bfloat16) for at in range(width)],
+            axis=1,
+        )
+        columns_ref[j] = chosen
+        gram_ref[j] = dot(chosen, chosen, NT)
+        cells = slice(j * 128, j * 128 + 128)
+        moved_ref[j] = dot(chosen, jnp.concatenate([s[:, cells] for s in states], axis=0))
+
+
+def gather_gram(slots, pieces, states, blocks, per_step=GRAM_STEP):
     part, width = states[0].shape
     members = part * CHUNKS
     edge = pieces[0].shape[0]
     kslots = slots.shape[0] // blocks
-    square = pl.BlockSpec((1, kslots, kslots), lambda i, s: (i, 0, 0))
+    square = pl.BlockSpec((per_step, kslots, kslots), lambda i, s: (i, 0, 0))
     squares = jax.ShapeDtypeStruct((blocks, kslots, kslots), jnp.float32)
     lanes = members // 128
     return pl.pallas_call(
         gram_kernel,
         grid_spec=pltpu.PrefetchScalarGridSpec(
             num_scalar_prefetch=1,
-            grid=(blocks,),
-            in_specs=[pl.BlockSpec((edge, part), lambda i, s: (0, 0), pipeline_mode=pl.Buffered(1))] * len(pieces)
-            + [pl.BlockSpec((part, width // blocks), lambda i, s: (0, i))] * CHUNKS,
+            grid=(blocks // per_step,),
+            in_specs=[pl.BlockSpec(memory_space=pl.ANY)] * len(pieces)
+            + [pl.BlockSpec((part, per_step * width // blocks), lambda i, s: (0, i))] * CHUNKS,
             out_specs=(
-                pl.BlockSpec((1, kslots, members), lambda i, s: (i, 0, 0)),
+                pl.BlockSpec((per_step, kslots, members), lambda i, s: (i, 0, 0)),
                 square,
                 square,
             ),
             scratch_shapes=[
+                pltpu.VMEM((len(pieces), edge, part), jnp.bfloat16),
                 pltpu.VMEM(((4 * edge + 1) * lanes, 128), jnp.float32),
-                pltpu.VMEM((2, kslots * lanes, 128), jnp.float32),
+                pltpu.VMEM((per_step, kslots * lanes, 128), jnp.float32),
+                pltpu.SemaphoreType.DMA((len(pieces),)),
             ],
         ),
         out_shape=(jax.ShapeDtypeStruct((blocks, kslots, members), jnp.bfloat16), squares, squares),
-        compiler_params=pltpu.CompilerParams(vmem_limit_bytes=48 * 1024 * 1024),
+        compiler_params=pltpu.CompilerParams(vmem_limit_bytes=60 * 1024 * 1024),
         cost_estimate=pl.CostEstimate(
             flops=4 * blocks * kslots * kslots * members,
             bytes_accessed=16 * members * width,
@@ -200,27 +205,33 @@
 
 def invert_kernel(gram_ref, out_ref, work):
     nblk, n, _ = gram_ref.shape
-    lane = lax.broadcasted_iota(jnp.int32, (1, 1, n), 2)
-    sub = lax.broadcasted_iota(jnp.int32, (1, NB, 1), 1)
+    lane = lax.broadcasted_iota(jnp.int32, (8, n), 1)
+    sub = lax.broadcasted_iota(jnp.int32, (8, n), 0)
     lane2 = lax.broadcasted_iota(jnp.int32, (1, n), 1)
     rows = lax.broadcasted_iota(jnp.int32, (1, n, n), 1)
     cols = lax.broadcasted_iota(jnp.int32, (1, n, n), 2)
     work[...] = gram_ref[...] + jnp.where(rows == cols, 1.0, 0.0)
 
     def step(number, carry):
-        panel = work[:, 0:NB, :]
         flip = lane2 >= n - number * NB
-        sides = jnp.where(flip[None], -panel, panel)
+        panel = [[work[b, at : at + 8, :] for at in range(0, NB, 8)] for b in range(nblk)]
         for k in range(NB):
-            row = panel[:, k : k + 1, :]
-            col = panel[:, :, k : k + 1]
-            inv = 1.0 / panel[:, k : k + 1, k : k + 1]
-            scaled = jnp.where(lane == k, inv, row * inv)
-            panel = jnp.where(sub == k, scaled, jnp.where(lane == k, 0.0, panel) - col * scaled)
+            here = lane == k
+            own, at = divmod(k, 8)
+            for b in range(nblk):
+                col = [jnp.broadcast_to(p[:, k : k + 1], (8, n)) for p in panel[b]]
+                inv = 1.0 / col[own][at : at + 1, :]
+                scaled = jnp.where(here[0:1], inv, panel[b][own][at : at + 1, :] * inv)
+                scaled = jnp.broadcast_to(scaled, (8, n))
+                new = [jnp.where(here, 0.0, p) - c * scaled for p, c in zip(panel[b], col)]
+                new[own] = jnp.where(sub == at, scaled, new[own])
+                panel[b] = new
         for b in range(nblk):
-            rolled = pltpu.roll(panel[b], n - NB, 1)
+            sides = work[b, 0:NB, :]
+            sides = jnp.where(flip, -sides, sides)
+            rolled = pltpu.roll(jnp.concatenate(panel[b], axis=0), n - NB, 1)
             rh, rm, rl = three_way(rolled)
-            ch, cm, cl = three_way(sides[b])
+            ch, cm, cl = three_way(sides)
             rhs = jnp.concatenate([rh, rm, rh, rl, rm, rh, rl, rm], axis=0)
             lhs = jnp.concatenate([ch, ch, cm, ch, cm, cl, cm, cl], axis=0)
             change = dot(lhs, rhs, TN)
@@ -266,7 +277,7 @@
             out_ref[:, chunk * rows : (chunk + 1) * rows, cells] = updated.reshape(groups, rows, 128)
 
 
-def update(inverse, moved, columns, states, groups, per_step=2):
+def update(inverse, moved, columns, states, groups, per_step=4):
     blocks, kslots, _ = inverse.shape
     square = pl.BlockSpec((per_step, kslots, kslots), lambda i: (i, 0, 0))
     members = columns.shape[2]
@@ -292,7 +303,8 @@
     line_index = lax.axis_index("space") * groups + lax.axis_index("mem")
     local_index = block_obs - (line_index * obs_dev - obs_dev // 2)
     slot_ids = jnp.arange(block_obs.shape[1], dtype=jnp.int32)
-    slots = jnp.where(slot_ids[None, :] < block_count[:, None], local_index, 2 * obs_dev).reshape(-1)
+    slots = jnp.where(slot_ids[None, :] < block_count[:, None], local_index, 2 * obs_dev)
+    slots = slots.reshape(-1) * (members // 128)
     size = lax.axis_size("space") * groups
     up = [(i, i + 1) for i in range(size - 1)]
     down = [(b, a) for a, b in up]
@@ -322,6 +334,7 @@
         P(("space", "mem")),
     )
     out_specs = P("mem", "space")
+
     return jax.shard_map(
         on_device, mesh=mesh, in_specs=in_specs, out_specs=out_specs, check_vma=False
     )

time: 235 us -> 220 us (0.936)
  Pallas kernels: 76.8 us -> 62.8 us
    pallas_call x1, Pallas kernels: 20.3 us -> 13.1 us  [gather_gram(): pl.pallas_call(gram_kernel, grid_spec=pltpu.PrefetchScalarGridSpec(num_sc...]
    pallas_call x2, Pallas kernels: 18.4 us -> 14.7 us  [project(): pl.pallas_call(project_kernel, grid_spec=pltpu.PrefetchScalarGridSpec(num...]
  transfers between devices with their start and end apart: 6 -> 6, of which waited for: 5 -> 5; matrix products, arithmetic and copies ran while one was open for 1% -> 2% of each run, Pallas kernels for 6% -> 5%
where the time goes in v4:
time: 220 us; the launch traced here: 219 us
  blocking collectives  65.5 us (30%)
  Pallas kernels  62.8 us (29%)
  waiting for transfers between devices  57.3 us (26%)
  starting transfers between devices  27.8 us (13%)
  local copies, waits for them, and re-layouts  5.04 us (2%)
    all_to_all x1, blocking collectives, on_device(): lax.all_to_all(analysis.reshape(members, -1), 'mem', split_axis=0, concat...  65.5 us
    all_to_all x2, waiting for transfers between devices, on_device(): part = lax.all_to_all(part, 'mem', split_axis=0, concat_axis=0, tiled=True)  42.9 us
    pallas_call x1, Pallas kernels, invert(): pl.pallas_call(invert_kernel, out_shape=jax.ShapeDtypeStruct(gram.shape,...  17.8 us
    pallas_call x2, Pallas kernels, project(): pl.pallas_call(project_kernel, grid_spec=pltpu.PrefetchScalarGridSpec(num...  14.7 us
    pallas_call x1, Pallas kernels, gather_gram(): pl.pallas_call(gram_kernel, grid_spec=pltpu.PrefetchScalarGridSpec(num_sc...  13.1 us
    all_to_all x2, starting transfers between devices, on_device(): part = lax.all_to_all(part, 'mem', split_axis=0, concat_axis=0, tiled=True)  12.9 us
    ppermute x2, starting transfers between devices, on_device(): high = lax.ppermute(first, ('space', 'mem'), down)  10.3 us
    pallas_call x1, Pallas kernels, update(): pl.pallas_call(update_kernel, grid=(blocks // per_step,), in_specs=[squar...  9.7 us
  transfers between devices with their start and end apart: 6, of which 5 were waited for; matrix products, arithmetic and copies ran while one was open for 2% of the time, Pallas kernels for 5%

profile of v4, /device:TPU:97, one launch (start us, length us, event | category | flops | bytes accessed | tf_op | source)
XLA Modules:
  0.0 219.2 jit_solution(14991283361956749814)
XLA Ops:
  0.0 3.8 %stage.2 = bf16[32,16,2048]{2,1,0:T(8,128)(2,1)} custom-call(bf16[32,65536]{1,0:T(8,128)(2,1)} %in_ref.3), custom_call_target="tpu_custom_call" | custom-call | bytes 4194304 | tf_op jit(solution)/shard_map/stage/pallas_call | solution.py:34
  3.8 7.8 %all-to-all-start = ((bf16[32,16,2048]{2,1,0:T(8,128)(2,1)}), bf16[32,16,2048]{2,1,0:T(8,128)(2,1)S(1)}, u32[]{:S(2)}, u32[]{:S(2)}) async-start(bf16[32,16,2048]{2,1,0:T(8,128)(2,1)} %stage.2), calls=%async_computation | async-start | bytes 4194304 | tf_op jit(solution)/shard_map/all_to_all | solution.py:315
  11.5 0.0 copy-start.5
  11.6 3.8 %stage.3 = bf16[32,16,2048]{2,1,0:T(8,128)(2,1)} custom-call(bf16[32,65536]{1,0:T(8,128)(2,1)} %in_ref.3), custom_call_target="tpu_custom_call" | custom-call | bytes 4194304 | tf_op jit(solution)/shard_map/stage/pallas_call | solution.py:34
  15.4 0.0 copy-start.4
  15.4 24.5 %all-to-all-done = bf16[32,16,2048]{2,1,0:T(8,128)(2,1)S(1)} async-done(((bf16[32,16,2048]{2,1,0:T(8,128)(2,1)}), bf16[32,16,2048]{2,1,0:T(8,128)(2,1)S(1)}, u32[]{:S(2)}, u32[]{:S(2)}) %all-to-all-start) | async-done | bytes 2097184 | tf_op jit(solution)/shard_map/all_to_all | solution.py:315
  39.9 0.0 copy-start
  39.9 5.2 %all-to-all-start.1 = ((bf16[32,16,2048]{2,1,0:T(8,128)(2,1)}), bf16[32,16,2048]{2,1,0:T(8,128)(2,1)}, u32[]{:S(2)}, u32[]{:S(2)}) async-start(bf16[32,16,2048]{2,1,0:T(8,128)(2,1)} %stage.3), calls=%async_computation.1 | async-start | bytes 4194304 | tf_op jit(solution)/shard_map/all_to_all | solution.py:315
  45.1 0.0 copy-done.5
  45.1 1.4 broadcast_in_dim.9.weight_ref
  46.5 0.0 copy-done.4
  46.5 1.3 broadcast_in_dim.8.cells_ref
  47.8 0.0 copy-done
  47.8 0.0 copy-start.6
  47.8 0.0 copy-start.7
  47.8 7.4 %project.2 = (bf16[1024,512]{1,0:T(8,128)(2,1)}, bf16[1024,512]{1,0:T(8,128)(2,1)}) custom-call(s32[2048]{0:T(1024)} %cell_ref.3, s32[2048,128]{1,0:T(8,128)} %broadcast_in_dim.8.cells_ref, f32[2048,128]{1,0:T(8,128)} %broadcast_in_dim.9.weight_ref, bf16[512,2048]{1,0:T(8,128)(2,1)} %bitcast.7), custom_call_target="tpu_custom_call" | custom-call | flops 1342177280 | bytes 8388608 | tf_op jit(solution)/shard_map/project/pallas_call | solution.py:89
  55.2 0.0 copy-start.2
  55.2 0.0 copy-start.1
  55.2 18.3 %all-to-all-done.1 = bf16[32,16,2048]{2,1,0:T(8,128)(2,1)} async-done(((bf16[32,16,2048]{2,1,0:T(8,128)(2,1)}), bf16[32,16,2048]{2,1,0:T(8,128)(2,1)}, u32[]{:S(2)}, u32[]{:S(2)}) %all-to-all-start.1) | async-done | bytes 2097184 | tf_op jit(solution)/shard_map/all_to_all | solution.py:315
  73.6 7.3 %project.3 = (bf16[1024,512]{1,0:T(8,128)(2,1)}, bf16[1024,512]{1,0:T(8,128)(2,1)}) custom-call(s32[2048]{0:T(1024)} %cell_ref.3, s32[2048,128]{1,0:T(8,128)} %broadcast_in_dim.8.cells_ref, f32[2048,128]{1,0:T(8,128)} %broadcast_in_dim.9.weight_ref, bf16[512,2048]{1,0:T(8,128)(2,1)} %bitcast.2.states_ref.refs_9_.refs_1_), custom_call_target="tpu_custom_call" | custom-call | flops 1342177280 | bytes 8388608 | tf_op jit(solution)/shard_map/project/pallas_call | solution.py:89
  80.8 2.1 collective-permute-start.2
  82.9 3.0 %collective-permute-start.3 = (bf16[1024,512]{1,0:T(8,128)(2,1)}, bf16[1024,512]{1,0:T(8,128)(2,1)}, u32[]{:S(2)}, u32[]{:S(2)}) collective-permute-start(bf16[1024,512]{1,0:T(8,128)(2,1)} %get-tuple-element.15.refs_5_), channel_id=1, source_target_pairs={{1,0},{2,1},{3,2},{4,3},{5,4},{6,5},{7,6},{8,7},{9,8},{10,9},{11,1... | collective-permute-start | bytes 3145736 | tf_op jit(solution)/shard_map/ppermute | solution.py:319
  85.9 0.0 copy-done.2
  85.9 2.5 %collective-permute-start = (bf16[1024,512]{1,0:T(8,128)(2,1)S(1)}, bf16[1024,512]{1,0:T(8,128)(2,1)}, u32[]{:S(2)}, u32[]{:S(2)}) collective-permute-start(bf16[1024,512]{1,0:T(8,128)(2,1)S(1)} %copy-done.2), channel_id=1, source_target_pairs={{0,1},{1,2},{2,3},{3,4},{4,5},{5,6},{6,7},{7,8},{8,9},{9,10},{10,1... | collective-permute-start | bytes 3145736 | tf_op jit(solution)/shard_map/ppermute | solution.py:318
  88.5 0.0 copy-done.1
  88.5 7.2 %collective-permute-start.1 = (bf16[1024,512]{1,0:T(8,128)(2,1)S(1)}, bf16[1024,512]{1,0:T(8,128)(2,1)}, u32[]{:S(2)}, u32[]{:S(2)}) collective-permute-start(bf16[1024,512]{1,0:T(8,128)(2,1)S(1)} %copy-done.1), channel_id=1, source_target_pairs={{1,0},{2,1},{3,2},{4,3},{5,4},{6,5},{7,6},{8,7},{9,8},{10,9},{11,1... | collective-permute-start | bytes 3145736 | tf_op jit(solution)/shard_map/ppermute | solution.py:319
  95.7 0.0 copy-done.6
  95.7 0.0 copy-done.7
  95.8 0.7 multiply_bitcast_fusion.slot_ref
  96.4 0.0 collective-permute-done.2.refs_4_
  96.4 0.0 copy-start.3
  96.4 3.1 %collective-permute-done.3.refs_7_ = bf16[1024,512]{1,0:T(8,128)(2,1)} collective-permute-done((bf16[1024,512]{1,0:T(8,128)(2,1)}, bf16[1024,512]{1,0:T(8,128)(2,1)}, u32[]{:S(2)}, u32[]{:S(2)}) %collective-permute-start.3) | collective-permute-done | bytes 1048608 | tf_op jit(solution)/shard_map/ppermute | solution.py:319
  99.5 6.5 %collective-permute-done.refs_0_ = bf16[1024,512]{1,0:T(8,128)(2,1)} collective-permute-done((bf16[1024,512]{1,0:T(8,128)(2,1)S(1)}, bf16[1024,512]{1,0:T(8,128)(2,1)}, u32[]{:S(2)}, u32[]{:S(2)}) %collective-permute-start) | collective-permute-done | bytes 1048608 | tf_op jit(solution)/shard_map/ppermute | solution.py:318
  106.0 4.8 %collective-permute-done.1.refs_3_ = bf16[1024,512]{1,0:T(8,128)(2,1)} collective-permute-done((bf16[1024,512]{1,0:T(8,128)(2,1)S(1)}, bf16[1024,512]{1,0:T(8,128)(2,1)}, u32[]{:S(2)}, u32[]{:S(2)}) %collective-permute-start.1) | collective-permute-done | bytes 1048608 | tf_op jit(solution)/shard_map/ppermute | solution.py:319
  110.8 0.0 copy-done.3
  110.8 13.1 %gather_gram.1 = (bf16[16,128,1024]{2,1,0:T(8,128)(2,1)}, f32[16,128,128]{2,1,0:T(8,128)}, f32[16,128,128]{2,1,0:T(8,128)}) custom-call(s32[2048]{0:T(1024)} %multiply_bitcast_fusion.slot_ref, bf16[1024,512]{1,0:T(8,128)(2,1)} %collective-permute-done.refs_0_, bf16[1024,512]{1,0:T(8,128)(2,1)} %get-tuple-element.13.refs_1_, ...), custom_call_target="tpu_custom_call" | custom-call | flops 1073741824 | bytes 33554432 | tf_op jit(solution)/shard_map/gather_gram/pallas_call | solution.py:168
  123.9 17.8 %invert_blocks.1.inverse_ref = f32[16,128,128]{2,1,0:T(8,128)} custom-call(f32[16,128,128]{2,1,0:T(8,128)} %get-tuple-element.16.gram_ref), custom_call_target="tpu_custom_call" | custom-call | tf_op jit(solution)/shard_map/invert_blocks/pallas_call | solution.py:248
  141.7 9.7 %update.1 = bf16[32,32,2048]{2,1,0:T(8,128)(2,1)} custom-call(f32[16,128,128]{2,1,0:T(8,128)} %invert_blocks.1.inverse_ref, f32[16,128,128]{2,1,0:T(8,128)} %get-tuple-element.17.moved_ref, bf16[16,128,1024]{2,1,0:T(8,128)(2,1)} %get-tuple-element.18.columns_ref, bf16[512,2048]{1,0:T(8,128)(2,1)} %bitcast.9, bf16[512,2048]{1,0:T(8,128)(2,1)} %bitcast.2.states_ref.refs_9_.refs_1_), custom_call_target="tpu_custom_call" | custom-call | tf_op jit(solution)/shard_map/update/pallas_call | solution.py:285
  151.4 65.5 %all_to_all.26 = bf16[32,32,2048]{2,1,0:T(8,128)(2,1)S(1)} all-to-all(bf16[32,32,2048]{2,1,0:T(8,128)(2,1)} %update.1), channel_id=1, replica_groups=mesh['space'=8,'mem'=32] {'mem'}, dimensions={0} | all-to-all | bytes 8388608 | tf_op jit(solution)/shard_map/all_to_all | solution.py:323
  216.9 2.3 %copy.7 = bf16[32,4,8,2048]{3,2,0,1:T(8,128)(2,1)} copy(bf16[32,4,8,2048]{3,2,1,0:T(8,128)(2,1)S(1)} %bitcast.10) | data formatting | bytes 8388608 | tf_op jit(solution)/shard_map/all_to_all | solution.py:323
  (1 shorter events, 0.0 us)
Async XLA Ops:
  3.8 36.1 %all-to-all-start = ((bf16[32,16,2048]{2,1,0:T(8,128)(2,1)}), bf16[32,16,2048]{2,1,0:T(8,128)(2,1)S(1)}, u32[]{:S(2)}, u32[]{:S(2)}) async-start(bf16[32,16,2048]{2,1,0:T(8,128)(2,1)} %stage.2), calls=%async_computation | async-start | bytes 4194304 | tf_op jit(solution)/shard_map/all_to_all | solution.py:315
  11.5 33.5 %copy-start.5 = (f32[2048]{0:T(1024)S(1)}, f32[2048]{0:T(1024)}, u32[]{:S(2)}) copy-start(f32[2048]{0:T(1024)} %param.7) | copy-start | bytes 24580
  15.4 31.1 %copy-start.4 = (s32[2048]{0:T(1024)S(1)}, s32[2048]{0:T(1024)}, u32[]{:S(2)}) copy-start(s32[2048]{0:T(1024)} %cell_ref.3) | copy-start | bytes 24580
  39.9 7.9 %copy-start = (bf16[32,16,2048]{2,1,0:T(8,128)(2,1)}, bf16[32,16,2048]{2,1,0:T(8,128)(2,1)S(1)}, u32[]{:S(2)}) copy-start(bf16[32,16,2048]{2,1,0:T(8,128)(2,1)S(1)} %all-to-all-done) | copy-start | bytes 6291460
  39.9 33.7 %all-to-all-start.1 = ((bf16[32,16,2048]{2,1,0:T(8,128)(2,1)}), bf16[32,16,2048]{2,1,0:T(8,128)(2,1)}, u32[]{:S(2)}, u32[]{:S(2)}) async-start(bf16[32,16,2048]{2,1,0:T(8,128)(2,1)} %stage.3), calls=%async_computation.1 | async-start | bytes 4194304 | tf_op jit(solution)/shard_map/all_to_all | solution.py:315
  47.8 47.9 %copy-start.6 = (s32[16,128]{1,0:T(8,128)S(1)}, s32[16,128]{1,0:T(8,128)}, u32[]{:S(2)}) copy-start(s32[16,128]{1,0:T(8,128)} %param.8) | copy-start | bytes 24580
  47.8 48.0 %copy-start.7 = (s32[16]{0:T(128)S(1)}, s32[16]{0:T(128)}, u32[]{:S(2)}) copy-start(s32[16]{0:T(128)} %param.9) | copy-start | bytes 196
  55.2 30.7 %copy-start.2 = (bf16[1024,512]{1,0:T(8,128)(2,1)S(1)}, bf16[1024,512]{1,0:T(8,128)(2,1)}, u32[]{:S(2)}) copy-start(bf16[1024,512]{1,0:T(8,128)(2,1)} %get-tuple-element.12.refs_2_) | copy-start | bytes 3145732
  55.2 33.3 %copy-start.1 = (bf16[1024,512]{1,0:T(8,128)(2,1)S(1)}, bf16[1024,512]{1,0:T(8,128)(2,1)}, u32[]{:S(2)}) copy-start(bf16[1024,512]{1,0:T(8,128)(2,1)} %get-tuple-element.13.refs_1_) | copy-start | bytes 3145732
  80.8 15.6 %collective-permute-start.2 = (bf16[1024,512]{1,0:T(8,128)(2,1)}, bf16[1024,512]{1,0:T(8,128)(2,1)S(1)}, u32[]{:S(2)}, u32[]{:S(2)}) collective-permute-start(bf16[1024,512]{1,0:T(8,128)(2,1)} %get-tuple-element.14.refs_6_), channel_id=1, source_target_pairs={{0,1},{1,2},{2,3},{3,4},{4,5},{5,6},{6,7},{7,8},{8,9},{9,10},{10,1... | collective-permute-start | bytes 3145736 | tf_op jit(solution)/shard_map/ppermute | solution.py:318
  82.9 16.6 %collective-permute-start.3 = (bf16[1024,512]{1,0:T(8,128)(2,1)}, bf16[1024,512]{1,0:T(8,128)(2,1)}, u32[]{:S(2)}, u32[]{:S(2)}) collective-permute-start(bf16[1024,512]{1,0:T(8,128)(2,1)} %get-tuple-element.15.refs_5_), channel_id=1, source_target_pairs={{1,0},{2,1},{3,2},{4,3},{5,4},{6,5},{7,6},{8,7},{9,8},{10,9},{11,1... | collective-permute-start | bytes 3145736 | tf_op jit(solution)/shard_map/ppermute | solution.py:319
  85.9 20.1 %collective-permute-start = (bf16[1024,512]{1,0:T(8,128)(2,1)S(1)}, bf16[1024,512]{1,0:T(8,128)(2,1)}, u32[]{:S(2)}, u32[]{:S(2)}) collective-permute-start(bf16[1024,512]{1,0:T(8,128)(2,1)S(1)} %copy-done.2), channel_id=1, source_target_pairs={{0,1},{1,2},{2,3},{3,4},{4,5},{5,6},{6,7},{7,8},{8,9},{9,10},{10,1... | collective-permute-start | bytes 3145736 | tf_op jit(solution)/shard_map/ppermute | solution.py:318
  88.5 22.4 %collective-permute-start.1 = (bf16[1024,512]{1,0:T(8,128)(2,1)S(1)}, bf16[1024,512]{1,0:T(8,128)(2,1)}, u32[]{:S(2)}, u32[]{:S(2)}) collective-permute-start(bf16[1024,512]{1,0:T(8,128)(2,1)S(1)} %copy-done.1), channel_id=1, source_target_pairs={{1,0},{2,1},{3,2},{4,3},{5,4},{6,5},{7,6},{8,7},{9,8},{10,9},{11,1... | collective-permute-start | bytes 3145736 | tf_op jit(solution)/shard_map/ppermute | solution.py:319
  96.4 14.4 %copy-start.3 = (bf16[1024,512]{1,0:T(8,128)(2,1)}, bf16[1024,512]{1,0:T(8,128)(2,1)S(1)}, u32[]{:S(2)}) copy-start(bf16[1024,512]{1,0:T(8,128)(2,1)S(1)} %collective-permute-done.2.refs_4_) | copy-start | bytes 3145732

commit v5 on v4

--- a/solution.py
+++ b/solution.py
@@ -10,7 +10,7 @@
 
 NB = 16
 TILE = 512
-CHUNKS = 2
+PIECES = 2
 SPAN = 640
 GRAM_STEP = 4
 SPREAD = 64
@@ -21,27 +21,6 @@
 
 def dot(a, b, dims=(((1,), (0,)), ((), ())), precision=None):
     return lax.dot_general(a, b, dims, precision=precision, preferred_element_type=jnp.float32)
-
-
-def stage_kernel(in_ref, out_ref):
-    width = out_ref.shape[2]
-    for at in range(out_ref.shape[0]):
-        out_ref[at] = in_ref[:, at * width : (at + 1) * width]
-
-
-def stage(deviations, chunk, rows, groups, per_step=8):
-    width = deviations.shape[1] // groups
-    return pl.pallas_call(
-        stage_kernel,
-        grid=(groups // per_step,),
-        in_specs=[pl.BlockSpec((rows, width * per_step), lambda i: (chunk, i))],
-        out_specs=pl.BlockSpec((per_step, rows, width), lambda i: (i, 0, 0)),
-        out_shape=jax.ShapeDtypeStruct((groups, rows, width), deviations.dtype),
-        cost_estimate=pl.CostEstimate(
-            flops=0, bytes_accessed=4 * groups * rows * width, transcendentals=0
-        ),
-        name="stage",
-    )(deviations)
 
 
 def project_kernel(cell_ref, cells_ref, weight_ref, states_ref, first_ref, last_ref, acc_ref):
@@ -81,8 +60,9 @@
         last_ref[...] = done
 
 
-def project(obs_cell, cells, weight, states):
-    members, width = states.shape
+def project(obs_cell, cells, weight, states, piece):
+    width = states.shape[1]
+    members = states.shape[0] // PIECES
     obs = obs_cell.shape[0]
     half = obs // TILE // 2
     side = jax.ShapeDtypeStruct((obs // 2, members), jnp.bfloat16)
@@ -94,7 +74,7 @@
             in_specs=[
                 pl.BlockSpec((TILE, 128), lambda i, c: (i, 0)),
                 pl.BlockSpec((TILE, 128), lambda i, c: (i, 0)),
-                pl.BlockSpec((members, width), lambda i, c: (0, 0)),
+                pl.BlockSpec((members, width), lambda i, c: (piece, 0)),
             ],
             out_specs=(
                 pl.BlockSpec((TILE, members), lambda i, c: (jnp.minimum(i, half - 1), 0)),
@@ -111,12 +91,12 @@
 
 
 def gram_kernel(slot_ref, *refs):
-    pieces, states = refs[: 4 * CHUNKS], refs[4 * CHUNKS : 5 * CHUNKS]
-    columns_ref, gram_ref, moved_ref, landed_ref, rows_ref, picked_ref, sems = refs[5 * CHUNKS :]
+    pieces, states_ref = refs[: 4 * PIECES], refs[4 * PIECES]
+    columns_ref, gram_ref, moved_ref, landed_ref, rows_ref, picked_ref, sems = refs[4 * PIECES + 1 :]
     step = pl.program_id(0)
     edge, part = pieces[0].shape
     tiles = part // 128
-    width = CHUNKS * tiles
+    width = PIECES * tiles
     per_step, kslots, _ = gram_ref.shape
 
     @pl.when(step == 0)
@@ -124,7 +104,7 @@
         copies = [
             pltpu.make_async_copy(piece, landed_ref.at[at], sems.at[at]) for at, piece in enumerate(pieces)
         ]
-        order = [chunk * 4 + side for side in (1, 2, 0, 3) for chunk in range(CHUNKS)]
+        order = [chunk * 4 + side for side in (1, 2, 0, 3) for chunk in range(PIECES)]
         for at in order:
             copies[at].start()
         rows_ref[4 * edge * width :, :] = jnp.zeros((width, 128), jnp.float32)
@@ -154,13 +134,12 @@
         columns_ref[j] = chosen
         gram_ref[j] = dot(chosen, chosen, NT)
         cells = slice(j * 128, j * 128 + 128)
-        moved_ref[j] = dot(chosen, jnp.concatenate([s[:, cells] for s in states], axis=0))
+        moved_ref[j] = dot(chosen, states_ref[:, cells])
 
 
 def gather_gram(slots, pieces, states, blocks, per_step=GRAM_STEP):
-    part, width = states[0].shape
-    members = part * CHUNKS
-    edge = pieces[0].shape[0]
+    members, width = states.shape
+    edge, part = pieces[0].shape
     kslots = slots.shape[0] // blocks
     square = pl.BlockSpec((per_step, kslots, kslots), lambda i, s: (i, 0, 0))
     squares = jax.ShapeDtypeStruct((blocks, kslots, kslots), jnp.float32)
@@ -171,7 +150,7 @@
             num_scalar_prefetch=1,
             grid=(blocks // per_step,),
             in_specs=[pl.BlockSpec(memory_space=pl.ANY)] * len(pieces)
-            + [pl.BlockSpec((part, per_step * width // blocks), lambda i, s: (0, i))] * CHUNKS,
+            + [pl.BlockSpec((members, per_step * width // blocks), lambda i, s: (0, i))],
             out_specs=(
                 pl.BlockSpec((per_step, kslots, members), lambda i, s: (i, 0, 0)),
                 square,
@@ -192,7 +171,7 @@
             transcendentals=0,
         ),
         name="gather_gram",
-    )(slots, *pieces, *states)
+    )(slots, *pieces, states)
 
 
 def three_way(v):
@@ -253,11 +232,8 @@
     )(gram)
 
 
-def update_kernel(inverse_ref, moved_ref, columns_ref, *refs):
-    states, out_ref = refs[:-1], refs[-1]
-    groups = out_ref.shape[0]
-    part = states[0].shape[0]
-    rows = part // groups
+def update_kernel(inverse_ref, moved_ref, columns_ref, states_ref, out_ref):
+    groups, rows, _ = out_ref.shape
     for at in range(inverse_ref.shape[0]):
         wh, wm, wl = three_way(inverse_ref[at])
         mh, mm, ml = three_way(moved_ref[at] * 0.5)
@@ -267,30 +243,32 @@
         )
         high = solved.astype(jnp.bfloat16)
         low = (solved - high.astype(jnp.float32)).astype(jnp.bfloat16)
-        both = jnp.concatenate([high, low], axis=0)
         columns = columns_ref[at].T
-        twice = jnp.concatenate([columns, columns], axis=1)
+        change = dot(
+            jnp.concatenate([columns, columns], axis=1), jnp.concatenate([high, low], axis=0)
+        )
         cells = slice(at * 128, at * 128 + 128)
-        for chunk, states_ref in enumerate(states):
-            change = dot(twice[chunk * part : (chunk + 1) * part], both)
-            updated = (states_ref[:, cells].astype(jnp.float32) - change).astype(jnp.bfloat16)
-            out_ref[:, chunk * rows : (chunk + 1) * rows, cells] = updated.reshape(groups, rows, 128)
+        updated = (states_ref[:, cells].astype(jnp.float32) - change).astype(jnp.bfloat16)
+        out_ref[:, :, cells] = updated.reshape(groups, rows, 128)
 
 
 def update(inverse, moved, columns, states, groups, per_step=4):
     blocks, kslots, _ = inverse.shape
     square = pl.BlockSpec((per_step, kslots, kslots), lambda i: (i, 0, 0))
-    members = columns.shape[2]
-    part, width = states[0].shape
+    members, width = states.shape
     return pl.pallas_call(
         update_kernel,
         grid=(blocks // per_step,),
-        in_specs=[square, square, pl.BlockSpec((per_step, kslots, members), lambda i: (i, 0, 0))]
-        + [pl.BlockSpec((part, per_step * kslots), lambda i: (0, i))] * len(states),
+        in_specs=[
+            square,
+            square,
+            pl.BlockSpec((per_step, kslots, members), lambda i: (i, 0, 0)),
+            pl.BlockSpec((members, per_step * kslots), lambda i: (0, i)),
+        ],
         out_specs=pl.BlockSpec((groups, members // groups, per_step * kslots), lambda i: (0, 0, i)),
         out_shape=jax.ShapeDtypeStruct((groups, members // groups, width), jnp.bfloat16),
         name="update",
-    )(inverse, moved, columns, *states)
+    )(inverse, moved, columns, states)
 
 
 def on_device(deviations, obs_cell, obs_weight, block_obs, block_count):
@@ -308,13 +286,10 @@
     size = lax.axis_size("space") * groups
     up = [(i, i + 1) for i in range(size - 1)]
     down = [(b, a) for a, b in up]
-    rows = deviations.shape[0] // CHUNKS
-    states, pieces = [], []
-    for chunk in range(CHUNKS):
-        part = stage(deviations, chunk, rows, groups)
-        part = lax.all_to_all(part, "mem", split_axis=0, concat_axis=0, tiled=True)
-        states.append(part.reshape(groups * rows, -1))
-        first, last = project(obs_cell, cells, weights, states[-1])
+    states = lax.all_to_all(deviations, "mem", split_axis=1, concat_axis=0, tiled=True)
+    pieces = []
+    for piece in range(PIECES):
+        first, last = project(obs_cell, cells, weights, states, piece)
         low = lax.ppermute(last, ("space", "mem"), up)
         high = lax.ppermute(first, ("space", "mem"), down)
         pieces += [low, first, last, high]

time: 220 us -> 220 us (level)
  waiting for transfers between devices: 57.3 us -> 68.7 us
  Pallas kernels: 62.8 us -> 54.3 us
  local copies, waits for them, and re-layouts: 5.04 us -> 9.84 us
  starting transfers between devices: 27.8 us -> 23.1 us
  blocking collectives: 65.5 us -> 62.8 us
    all_to_all x2 -> x1, waiting for transfers between devices: 42.9 us -> 52.1 us  [on_device(): lax.all_to_all(deviations, 'mem', split_axis=1, concat_axis=0, tiled=True)]
    pallas_call x2 -> x0, Pallas kernels: 7.59 us -> none  [stage(): pl.pallas_call(stage_kernel, grid=(groups // per_step,), in_specs=[pl.Blo...]
    all_to_all x2 -> x1, starting transfers between devices: 12.9 us -> 7.95 us  [on_device(): lax.all_to_all(deviations, 'mem', split_axis=1, concat_axis=0, tiled=True)]
    all_to_all x0 -> x1, local copies, waits for them, and re-layouts: none -> 4.79 us  [on_device(): lax.all_to_all(deviations, 'mem', split_axis=1, concat_axis=0, tiled=True)]
    ppermute x2, starting transfers between devices: 4.59 us -> 8.2 us  [on_device(): low = lax.ppermute(last, ('space', 'mem'), up)]
    ppermute x2, starting transfers between devices: 10.3 us -> 6.95 us  [on_device(): high = lax.ppermute(first, ('space', 'mem'), down)]
    all_to_all x1, blocking collectives: 65.5 us -> 62.8 us  [on_device(): lax.all_to_all(analysis.reshape(members, -1), 'mem', split_axis=0, concat...]
  transfers between devices with their start and end apart: 6 -> 5, of which waited for: 5 -> 5; matrix products, arithmetic and copies ran while one was open for 2% -> 0% of each run, Pallas kernels for 5% -> 0%
where the time goes in v5:
time: 220 us
  waiting for transfers between devices  68.7 us (31%)
  blocking collectives  62.8 us (29%)
  Pallas kernels  54.3 us (25%)
  starting transfers between devices  23.1 us (10%)
  local copies, waits for them, and re-layouts  9.84 us (4%)
    all_to_all x1, blocking collectives, on_device(): lax.all_to_all(analysis.reshape(members, -1), 'mem', split_axis=0, concat...  62.8 us
    all_to_all x1, waiting for transfers between devices, on_device(): lax.all_to_all(deviations, 'mem', split_axis=1, concat_axis=0, tiled=True)  52.1 us
    pallas_call x1, Pallas kernels, invert(): pl.pallas_call(invert_kernel, out_shape=jax.ShapeDtypeStruct(gram.shape,...  17.8 us
    pallas_call x2, Pallas kernels, project(): pl.pallas_call(project_kernel, grid_spec=pltpu.PrefetchScalarGridSpec(num...  14.7 us
    pallas_call x1, Pallas kernels, gather_gram(): pl.pallas_call(gram_kernel, grid_spec=pltpu.PrefetchScalarGridSpec(num_sc...  13.1 us
    ppermute x2, waiting for transfers between devices, on_device(): high = lax.ppermute(first, ('space', 'mem'), down)  9.38 us
    pallas_call x1, Pallas kernels, update(): pl.pallas_call(update_kernel, grid=(blocks // per_step,), in_specs=[squar...  8.69 us
    ppermute x2, starting transfers between devices, on_device(): low = lax.ppermute(last, ('space', 'mem'), up)  8.2 us
  transfers between devices with their start and end apart: 5, of which 5 were waited for; matrix products, arithmetic and copies ran while one was open for 0% of the time, Pallas kernels for 0%

profile of v5, /device:TPU:97, one launch (start us, length us, event | category | flops | bytes accessed | tf_op | source)
XLA Modules:
  0.0 219.6 jit_solution(3748971590867758361)
XLA Ops:
  0.0 4.8 %copy.12 = bf16[4,32,8,2048]{3,2,0,1:T(8,128)(2,1)} copy(bf16[4,32,8,2048]{3,2,1,0:T(8,128)(2,1)} %bitcast.14) | data formatting | bytes 8388608 | tf_op jit(solution)/shard_map/all_to_all | solution.py:289
  4.8 0.0 copy-start.4
  4.8 0.0 copy-start.3
  4.8 7.9 %all-to-all-start = ((bf16[32,32,2048]{2,0,1:T(8,128)(2,1)}), bf16[32,32,2048]{2,0,1:T(8,128)(2,1)}, u32[]{:S(2)}, u32[]{:S(2)}) async-start(bf16[32,32,2048]{2,0,1:T(8,128)(2,1)} %bitcast.12), calls=%async_computation | async-start | bytes 8388608 | tf_op jit(solution)/shard_map/all_to_all | solution.py:289
  12.7 0.0 copy-done.4
  12.8 52.1 %all-to-all-done = bf16[32,32,2048]{2,0,1:T(8,128)(2,1)} async-done(((bf16[32,32,2048]{2,0,1:T(8,128)(2,1)}), bf16[32,32,2048]{2,0,1:T(8,128)(2,1)}, u32[]{:S(2)}, u32[]{:S(2)}) %all-to-all-start) | async-done | bytes 4194336 | tf_op jit(solution)/shard_map/all_to_all | solution.py:289
  64.9 1.4 broadcast_in_dim.9.weight_ref
  66.3 0.0 copy-done.3
  66.3 1.3 broadcast_in_dim.8.cells_ref
  67.6 7.3 %project.3 = (bf16[1024,512]{1,0:T(8,128)(2,1)}, bf16[1024,512]{1,0:T(8,128)(2,1)}) custom-call(s32[2048]{0:T(1024)} %cell_ref.3, s32[2048,128]{1,0:T(8,128)} %broadcast_in_dim.8.cells_ref, f32[2048,128]{1,0:T(8,128)} %broadcast_in_dim.9.weight_ref, bf16[1024,2048]{1,0:T(8,128)(2,1)} %bitcast.2.states_ref.refs_8_), custom_call_target="tpu_custom_call" | custom-call | flops 1342177280 | bytes 8388608 | tf_op jit(solution)/shard_map/project/pallas_call | solution.py:69
  74.8 0.0 copy-start.1
  74.8 0.0 copy-start
  74.9 0.0 copy-start.5
  74.9 0.0 copy-start.6
  74.9 7.4 %project.2 = (bf16[1024,512]{1,0:T(8,128)(2,1)}, bf16[1024,512]{1,0:T(8,128)(2,1)}) custom-call(s32[2048]{0:T(1024)} %cell_ref.3, s32[2048,128]{1,0:T(8,128)} %broadcast_in_dim.8.cells_ref, f32[2048,128]{1,0:T(8,128)} %broadcast_in_dim.9.weight_ref, bf16[1024,2048]{1,0:T(8,128)(2,1)} %bitcast.2.states_ref.refs_8_), custom_call_target="tpu_custom_call" | custom-call | flops 1342177280 | bytes 8388608 | tf_op jit(solution)/shard_map/project/pallas_call | solution.py:69
  82.3 4.6 %collective-permute-start = (bf16[1024,512]{1,0:T(8,128)(2,1)}, bf16[1024,512]{1,0:T(8,128)(2,1)S(1)}, u32[]{:S(2)}, u32[]{:S(2)}) collective-permute-start(bf16[1024,512]{1,0:T(8,128)(2,1)} %get-tuple-element.12.refs_2_), channel_id=1, source_target_pairs={{0,1},{1,2},{2,3},{3,4},{4,5},{5,6},{6,7},{7,8},{8,9},{9,10},{10,1... | collective-permute-start | bytes 3145736 | tf_op jit(solution)/shard_map/ppermute | solution.py:293
  86.8 1.9 collective-permute-start.1
  88.8 0.0 copy-done.1
  88.8 3.6 %collective-permute-start.2 = (bf16[1024,512]{1,0:T(8,128)(2,1)S(1)}, bf16[1024,512]{1,0:T(8,128)(2,1)}, u32[]{:S(2)}, u32[]{:S(2)}) collective-permute-start(bf16[1024,512]{1,0:T(8,128)(2,1)S(1)} %copy-done.1), channel_id=1, source_target_pairs={{0,1},{1,2},{2,3},{3,4},{4,5},{5,6},{6,7},{7,8},{8,9},{9,10},{10,1... | collective-permute-start | bytes 3145736 | tf_op jit(solution)/shard_map/ppermute | solution.py:293
  92.4 0.0 copy-done
  92.4 5.0 %collective-permute-start.3 = (bf16[1024,512]{1,0:T(8,128)(2,1)S(1)}, bf16[1024,512]{1,0:T(8,128)(2,1)}, u32[]{:S(2)}, u32[]{:S(2)}) collective-permute-start(bf16[1024,512]{1,0:T(8,128)(2,1)S(1)} %copy-done), channel_id=1, source_target_pairs={{1,0},{2,1},{3,2},{4,3},{5,4},{6,5},{7,6},{8,7},{9,8},{10,9},{11,1... | collective-permute-start | bytes 3145736 | tf_op jit(solution)/shard_map/ppermute | solution.py:294
  97.5 0.0 copy-done.5
  97.5 0.0 copy-done.6
  97.5 0.7 multiply_bitcast_fusion.slot_ref
  98.2 0.7 collective-permute-done.refs_0_
  98.9 0.0 copy-start.2
  98.9 4.6 %collective-permute-done.1.refs_3_ = bf16[1024,512]{1,0:T(8,128)(2,1)} collective-permute-done((bf16[1024,512]{1,0:T(8,128)(2,1)}, bf16[1024,512]{1,0:T(8,128)(2,1)}, u32[]{:S(2)}, u32[]{:S(2)}) %collective-permute-start.1) | collective-permute-done | bytes 1048608 | tf_op jit(solution)/shard_map/ppermute | solution.py:294
  103.5 6.5 %collective-permute-done.2.refs_4_ = bf16[1024,512]{1,0:T(8,128)(2,1)} collective-permute-done((bf16[1024,512]{1,0:T(8,128)(2,1)S(1)}, bf16[1024,512]{1,0:T(8,128)(2,1)}, u32[]{:S(2)}, u32[]{:S(2)}) %collective-permute-start.2) | collective-permute-done | bytes 1048608 | tf_op jit(solution)/shard_map/ppermute | solution.py:293
  110.0 4.8 %collective-permute-done.3.refs_7_ = bf16[1024,512]{1,0:T(8,128)(2,1)} collective-permute-done((bf16[1024,512]{1,0:T(8,128)(2,1)S(1)}, bf16[1024,512]{1,0:T(8,128)(2,1)}, u32[]{:S(2)}, u32[]{:S(2)}) %collective-permute-start.3) | collective-permute-done | bytes 1048608 | tf_op jit(solution)/shard_map/ppermute | solution.py:294
  114.8 0.0 copy-done.2
  114.8 13.1 %gather_gram.1 = (bf16[16,128,1024]{2,1,0:T(8,128)(2,1)}, f32[16,128,128]{2,1,0:T(8,128)}, f32[16,128,128]{2,1,0:T(8,128)}) custom-call(s32[2048]{0:T(1024)} %multiply_bitcast_fusion.slot_ref, bf16[1024,512]{1,0:T(8,128)(2,1)} %copy-done.2, bf16[1024,512]{1,0:T(8,128)(2,1)} %get-tuple-element.13.refs_1_, bf16[1024,512]{1,0:T(8,128)(2,1)} %get-tuple-element.12.refs_2_, ...), custom_call_target="tpu_custom_call" | custom-call | flops 1073741824 | bytes 33554432 | tf_op jit(solution)/shard_map/gather_gram/pallas_call | solution.py:147
  127.9 17.8 %invert_blocks.1.inverse_ref = f32[16,128,128]{2,1,0:T(8,128)} custom-call(f32[16,128,128]{2,1,0:T(8,128)} %get-tuple-element.16.gram_ref), custom_call_target="tpu_custom_call" | custom-call | tf_op jit(solution)/shard_map/invert_blocks/pallas_call | solution.py:227
  145.7 8.7 %update.1 = bf16[32,32,2048]{2,1,0:T(8,128)(2,1)} custom-call(f32[16,128,128]{2,1,0:T(8,128)} %invert_blocks.1.inverse_ref, f32[16,128,128]{2,1,0:T(8,128)} %get-tuple-element.17.moved_ref, bf16[16,128,1024]{2,1,0:T(8,128)(2,1)} %get-tuple-element.18.columns_ref, bf16[1024,2048]{1,0:T(8,128)(2,1)} %bitcast.2.states_ref.refs_8_), custom_call_target="tpu_custom_call" | custom-call | tf_op jit(solution)/shard_map/update/pallas_call | solution.py:259
  154.4 62.8 %all_to_all.35 = bf16[32,32,2048]{2,1,0:T(8,128)(2,1)S(1)} all-to-all(bf16[32,32,2048]{2,1,0:T(8,128)(2,1)} %update.1), channel_id=1, replica_groups=mesh['space'=8,'mem'=32] {'mem'}, dimensions={0} | all-to-all | bytes 8388608 | tf_op jit(solution)/shard_map/all_to_all | solution.py:298
  217.2 2.3 %copy.10 = bf16[32,4,8,2048]{3,2,0,1:T(8,128)(2,1)} copy(bf16[32,4,8,2048]{3,2,1,0:T(8,128)(2,1)S(1)} %bitcast.13) | data formatting | bytes 8388608 | tf_op jit(solution)/shard_map/all_to_all | solution.py:298
  (1 shorter events, 0.0 us)
Async XLA Ops:
  4.8 8.0 %copy-start.4 = (f32[2048]{0:T(1024)S(1)}, f32[2048]{0:T(1024)}, u32[]{:S(2)}) copy-start(f32[2048]{0:T(1024)} %param.7) | copy-start | bytes 24580
  4.8 61.5 %copy-start.3 = (s32[2048]{0:T(1024)S(1)}, s32[2048]{0:T(1024)}, u32[]{:S(2)}) copy-start(s32[2048]{0:T(1024)} %cell_ref.3) | copy-start | bytes 24580
  4.8 60.1 %all-to-all-start = ((bf16[32,32,2048]{2,0,1:T(8,128)(2,1)}), bf16[32,32,2048]{2,0,1:T(8,128)(2,1)}, u32[]{:S(2)}, u32[]{:S(2)}) async-start(bf16[32,32,2048]{2,0,1:T(8,128)(2,1)} %bitcast.12), calls=%async_computation | async-start | bytes 8388608 | tf_op jit(solution)/shard_map/all_to_all | solution.py:289
  74.8 13.9 %copy-start.1 = (bf16[1024,512]{1,0:T(8,128)(2,1)S(1)}, bf16[1024,512]{1,0:T(8,128)(2,1)}, u32[]{:S(2)}) copy-start(bf16[1024,512]{1,0:T(8,128)(2,1)} %get-tuple-element.14.refs_6_) | copy-start | bytes 3145732
  74.8 17.6 %copy-start = (bf16[1024,512]{1,0:T(8,128)(2,1)S(1)}, bf16[1024,512]{1,0:T(8,128)(2,1)}, u32[]{:S(2)}) copy-start(bf16[1024,512]{1,0:T(8,128)(2,1)} %get-tuple-element.15.refs_5_) | copy-start | bytes 3145732
  74.9 22.6 %copy-start.5 = (s32[16,128]{1,0:T(8,128)S(1)}, s32[16,128]{1,0:T(8,128)}, u32[]{:S(2)}) copy-start(s32[16,128]{1,0:T(8,128)} %param.8) | copy-start | bytes 24580
  74.9 22.6 %copy-start.6 = (s32[16]{0:T(128)S(1)}, s32[16]{0:T(128)}, u32[]{:S(2)}) copy-start(s32[16]{0:T(128)} %param.9) | copy-start | bytes 196
  82.3 16.6 %collective-permute-start = (bf16[1024,512]{1,0:T(8,128)(2,1)}, bf16[1024,512]{1,0:T(8,128)(2,1)S(1)}, u32[]{:S(2)}, u32[]{:S(2)}) collective-permute-start(bf16[1024,512]{1,0:T(8,128)(2,1)} %get-tuple-element.12.refs_2_), channel_id=1, source_target_pairs={{0,1},{1,2},{2,3},{3,4},{4,5},{5,6},{6,7},{7,8},{8,9},{9,10},{10,1... | collective-permute-start | bytes 3145736 | tf_op jit(solution)/shard_map/ppermute | solution.py:293
  86.8 16.6 %collective-permute-start.1 = (bf16[1024,512]{1,0:T(8,128)(2,1)}, bf16[1024,512]{1,0:T(8,128)(2,1)}, u32[]{:S(2)}, u32[]{:S(2)}) collective-permute-start(bf16[1024,512]{1,0:T(8,128)(2,1)} %get-tuple-element.13.refs_1_), channel_id=1, source_target_pairs={{1,0},{2,1},{3,2},{4,3},{5,4},{6,5},{7,6},{8,7},{9,8},{10,9},{11,1... | collective-permute-start | bytes 3145736 | tf_op jit(solution)/shard_map/ppermute | solution.py:294
  88.8 21.2 %collective-permute-start.2 = (bf16[1024,512]{1,0:T(8,128)(2,1)S(1)}, bf16[1024,512]{1,0:T(8,128)(2,1)}, u32[]{:S(2)}, u32[]{:S(2)}) collective-permute-start(bf16[1024,512]{1,0:T(8,128)(2,1)S(1)} %copy-done.1), channel_id=1, source_target_pairs={{0,1},{1,2},{2,3},{3,4},{4,5},{5,6},{6,7},{7,8},{8,9},{9,10},{10,1... | collective-permute-start | bytes 3145736 | tf_op jit(solution)/shard_map/ppermute | solution.py:293
  92.4 22.4 %collective-permute-start.3 = (bf16[1024,512]{1,0:T(8,128)(2,1)S(1)}, bf16[1024,512]{1,0:T(8,128)(2,1)}, u32[]{:S(2)}, u32[]{:S(2)}) collective-permute-start(bf16[1024,512]{1,0:T(8,128)(2,1)S(1)} %copy-done), channel_id=1, source_target_pairs={{1,0},{2,1},{3,2},{4,3},{5,4},{6,5},{7,6},{8,7},{9,8},{10,9},{11,1... | collective-permute-start | bytes 3145736 | tf_op jit(solution)/shard_map/ppermute | solution.py:294
  98.9 15.9 %copy-start.2 = (bf16[1024,512]{1,0:T(8,128)(2,1)}, bf16[1024,512]{1,0:T(8,128)(2,1)S(1)}, u32[]{:S(2)}) copy-start(bf16[1024,512]{1,0:T(8,128)(2,1)S(1)} %collective-permute-done.refs_0_) | copy-start | bytes 3145732

commit v6 on v5

--- a/solution.py
+++ b/solution.py
@@ -11,7 +11,8 @@
 NB = 16
 TILE = 512
 PIECES = 2
-SPAN = 640
+SUB = 256
+SPAN = 512
 GRAM_STEP = 4
 SPREAD = 64
 
@@ -23,44 +24,61 @@
     return lax.dot_general(a, b, dims, precision=precision, preferred_element_type=jnp.float32)
 
 
-def project_kernel(cell_ref, cells_ref, weight_ref, states_ref, first_ref, last_ref, acc_ref):
+def project_kernel(cell_ref, lists_ref, states_ref, first_ref, last_ref, acc_ref):
     tile = pl.program_id(0)
     half = pl.num_programs(0) // 2
     width = states_ref.shape[1]
-    lane = lax.broadcasted_iota(jnp.int32, (TILE, 128), 1)
-    begin = jnp.minimum(cell_ref[tile * TILE] // 128 * 128, width - SPAN)
-    end = cell_ref[tile * TILE + TILE - 1]
-    cells = cells_ref[...]
-
-    def picked(cells, start):
+    lane = lax.broadcasted_iota(jnp.int32, (TILE, 128), 1).astype(jnp.float32)
+    parts = TILE // 128
+    upright = lists_ref[0].T
+
+    def column(at):
+        return jnp.concatenate(
+            [jnp.broadcast_to(upright[:, at + k : at + k + 1], (128, 128)) for k in range(parts)], axis=0
+        )
+
+    beyond = column(0) - lane
+    weights = column(parts)
+    members = states_ref.shape[0]
+
+    def picked(beyond, start):
         start = pl.multiple_of(start, 128)
+        base = start.astype(jnp.float32)
         pick = jnp.concatenate(
-            [(cells == lane + (start + at)).astype(jnp.float32) for at in range(0, SPAN, 128)], axis=1
+            [(beyond == base + at).astype(jnp.float32) for at in range(0, SPAN, 128)], axis=1
         ).astype(jnp.bfloat16)
         return dot(pick, states_ref[:, pl.ds(start, SPAN)], NT)
 
-    acc_ref[...] = picked(cells, begin)
-
-    def add(step, carry):
-        lower = begin + step * SPAN
-        acc_ref[...] += picked(
-            jnp.where(cells >= lower, cells, -1), jnp.minimum(lower, width - SPAN)
-        )
-        return carry
-
-    lax.fori_loop(1, (end - begin) // SPAN + 1, add, 0)
-    done = (acc_ref[...] * weight_ref[:, 0:1]).astype(jnp.bfloat16)
+    def scaled(values, weights):
+        return (values * jnp.concatenate([weights] * (members // 128), axis=1)).astype(jnp.bfloat16)
+
+    for sub in range(0, TILE, SUB):
+        rows = slice(sub, sub + SUB)
+        begin = jnp.minimum(cell_ref[tile * TILE + sub] // 128 * 128, width - SPAN)
+        end = cell_ref[tile * TILE + sub + SUB - 1]
+        last_ref[rows] = scaled(picked(beyond[rows], begin), weights[rows])
+
+        @pl.when(end >= begin + SPAN)
+        def _():
+            acc_ref[...] = picked(beyond[rows], begin)
+
+            def add(step, carry):
+                lower = begin + step * SPAN
+                own = jnp.where(
+                    beyond[rows] + lane[rows] >= lower.astype(jnp.float32), beyond[rows], -2.0 * width
+                )
+                acc_ref[...] += picked(own, jnp.minimum(lower, width - SPAN))
+                return carry
+
+            lax.fori_loop(1, (end - begin) // SPAN + 1, add, 0)
+            last_ref[rows] = scaled(acc_ref[...], weights[rows])
 
     @pl.when(tile < half)
     def _():
-        first_ref[...] = done
-
-    @pl.when(tile >= half)
-    def _():
-        last_ref[...] = done
-
-
-def project(obs_cell, cells, weight, states, piece):
+        first_ref[...] = last_ref[...]
+
+
+def project(obs_cell, lists, states, piece):
     width = states.shape[1]
     members = states.shape[0] // PIECES
     obs = obs_cell.shape[0]
@@ -72,22 +90,22 @@
             num_scalar_prefetch=1,
             grid=(obs // TILE,),
             in_specs=[
-                pl.BlockSpec((TILE, 128), lambda i, c: (i, 0)),
-                pl.BlockSpec((TILE, 128), lambda i, c: (i, 0)),
+                pl.BlockSpec((1, 2 * TILE // 128, 128), lambda i, c: (i, 0, 0)),
                 pl.BlockSpec((members, width), lambda i, c: (piece, 0)),
             ],
             out_specs=(
                 pl.BlockSpec((TILE, members), lambda i, c: (jnp.minimum(i, half - 1), 0)),
                 pl.BlockSpec((TILE, members), lambda i, c: (jnp.maximum(i - half, 0), 0)),
             ),
-            scratch_shapes=[pltpu.VMEM((TILE, members), jnp.float32)],
+            scratch_shapes=[pltpu.VMEM((SUB, members), jnp.float32)],
         ),
         out_shape=(side, side),
+        compiler_params=pltpu.CompilerParams(vmem_limit_bytes=16 * 1024 * 1024),
         cost_estimate=pl.CostEstimate(
             flops=2 * obs * members * SPAN, bytes_accessed=8 * obs * members, transcendentals=0
         ),
         name="project",
-    )(obs_cell, cells, weight, states)
+    )(obs_cell, lists, states)
 
 
 def gram_kernel(slot_ref, *refs):
@@ -164,7 +182,7 @@
             ],
         ),
         out_shape=(jax.ShapeDtypeStruct((blocks, kslots, members), jnp.bfloat16), squares, squares),
-        compiler_params=pltpu.CompilerParams(vmem_limit_bytes=60 * 1024 * 1024),
+        compiler_params=pltpu.CompilerParams(vmem_limit_bytes=38 * 1024 * 1024),
         cost_estimate=pl.CostEstimate(
             flops=4 * blocks * kslots * kslots * members,
             bytes_accessed=16 * members * width,
@@ -228,6 +246,7 @@
         invert_kernel,
         out_shape=jax.ShapeDtypeStruct(gram.shape, jnp.float32),
         scratch_shapes=[pltpu.VMEM(gram.shape, jnp.float32)],
+        compiler_params=pltpu.CompilerParams(vmem_limit_bytes=10 * 1024 * 1024),
         name="invert_blocks",
     )(gram)
 
@@ -267,6 +286,7 @@
         ],
         out_specs=pl.BlockSpec((groups, members // groups, per_step * kslots), lambda i: (0, 0, i)),
         out_shape=jax.ShapeDtypeStruct((groups, members // groups, width), jnp.bfloat16),
+        compiler_params=pltpu.CompilerParams(vmem_limit_bytes=24 * 1024 * 1024),
         name="update",
     )(inverse, moved, columns, states)
 
@@ -276,8 +296,9 @@
     members = deviations.shape[0] * groups
     obs_dev = obs_cell.shape[0]
     weight = obs_weight * (1.0 / math.sqrt(members - 1))
-    cells = jnp.broadcast_to(obs_cell[:, None], (obs_dev, 128))
-    weights = jnp.broadcast_to(weight[:, None], (obs_dev, 128))
+    lists = jnp.concatenate(
+        [v.reshape(-1, TILE // 128, 128) for v in (obs_cell.astype(jnp.float32), weight)], axis=1
+    )
     line_index = lax.axis_index("space") * groups + lax.axis_index("mem")
     local_index = block_obs - (line_index * obs_dev - obs_dev // 2)
     slot_ids = jnp.arange(block_obs.shape[1], dtype=jnp.int32)
@@ -289,7 +310,7 @@
     states = lax.all_to_all(deviations, "mem", split_axis=1, concat_axis=0, tiled=True)
     pieces = []
     for piece in range(PIECES):
-        first, last = project(obs_cell, cells, weights, states, piece)
+        first, last = project(obs_cell, lists, states, piece)
         low = lax.ppermute(last, ("space", "mem"), up)
         high = lax.ppermute(first, ("space", "mem"), down)
         pieces += [low, first, last, high]

time: 220 us -> 207 us (0.941)
  Pallas kernels: 54.3 us -> 44.8 us
  local copies, waits for them, and re-layouts: 9.84 us -> 7.12 us
    broadcast_in_dim x2 -> x0, local copies, waits for them, and re-layouts: 2.7 us -> none  [the longest x1 1.4 us: on_device(): weights = jnp.broadcast_to(weight[:, None], (obs_dev, 128))]
    pallas_call x2, Pallas kernels: 14.7 us -> 12 us  [project(): pl.pallas_call(project_kernel, grid_spec=pltpu.PrefetchScalarGridSpec(num...]
    pallas_call x1, Pallas kernels: 13.1 us -> 10.7 us  [gather_gram(): pl.pallas_call(gram_kernel, grid_spec=pltpu.PrefetchScalarGridSpec(num_sc...]
    pallas_call x1, Pallas kernels: 8.69 us -> 6.42 us  [update(): pl.pallas_call(update_kernel, grid=(blocks // per_step,), in_specs=[squar...]
    pallas_call x1, Pallas kernels: 17.8 us -> 15.6 us  [invert(): pl.pallas_call(invert_kernel, out_shape=jax.ShapeDtypeStruct(gram.shape,...]
where the time goes in v6:
time: 207 us
  waiting for transfers between devices  69.7 us (34%)
  blocking collectives  62.9 us (30%)
  Pallas kernels  44.8 us (22%)
  starting transfers between devices  22.2 us (11%)
  local copies, waits for them, and re-layouts  7.12 us (3%)
    all_to_all x1, blocking collectives, on_device(): lax.all_to_all(analysis.reshape(members, -1), 'mem', split_axis=0, concat...  62.9 us
    all_to_all x1, waiting for transfers between devices, on_device(): lax.all_to_all(deviations, 'mem', split_axis=1, concat_axis=0, tiled=True)  52.1 us
    pallas_call x1, Pallas kernels, invert(): pl.pallas_call(invert_kernel, out_shape=jax.ShapeDtypeStruct(gram.shape,...  15.6 us
    pallas_call x2, Pallas kernels, project(): pl.pallas_call(project_kernel, grid_spec=pltpu.PrefetchScalarGridSpec(num...  12 us
    pallas_call x1, Pallas kernels, gather_gram(): pl.pallas_call(gram_kernel, grid_spec=pltpu.PrefetchScalarGridSpec(num_sc...  10.7 us
    ppermute x2, waiting for transfers between devices, on_device(): high = lax.ppermute(first, ('space', 'mem'), down)  9.19 us
    ppermute x2, waiting for transfers between devices, on_device(): low = lax.ppermute(last, ('space', 'mem'), up)  8.46 us
    ppermute x2, starting transfers between devices, on_device(): low = lax.ppermute(last, ('space', 'mem'), up)  8.21 us
  transfers between devices with their start and end apart: 5, of which 5 were waited for; matrix products, arithmetic and copies ran while one was open for 0% of the time, Pallas kernels for 0%

profile of v6, /device:TPU:97, one launch (start us, length us, event | category | flops | bytes accessed | tf_op | source)
XLA Modules:
  0.0 206.9 jit_solution(11836013623401985014)
XLA Ops:
  0.0 4.8 %copy.12 = bf16[4,32,8,2048]{3,2,0,1:T(8,128)(2,1)} copy(bf16[4,32,8,2048]{3,2,1,0:T(8,128)(2,1)} %bitcast.16) | data formatting | bytes 8388608 | tf_op jit(solution)/shard_map/all_to_all | solution.py:310
  4.8 0.0 copy-start
  4.8 0.0 copy-start.1
  4.8 7.9 %all-to-all-start = ((bf16[32,32,2048]{2,0,1:T(8,128)(2,1)}), bf16[32,32,2048]{2,0,1:T(8,128)(2,1)}, u32[]{:S(2)}, u32[]{:S(2)}) async-start(bf16[32,32,2048]{2,0,1:T(8,128)(2,1)} %bitcast.14), calls=%async_computation | async-start | bytes 8388608 | tf_op jit(solution)/shard_map/all_to_all | solution.py:310
  12.7 0.0 copy-done
  12.8 0.0 copy-done.1
  12.8 52.1 %all-to-all-done = bf16[32,32,2048]{2,0,1:T(8,128)(2,1)} async-done(((bf16[32,32,2048]{2,0,1:T(8,128)(2,1)}), bf16[32,32,2048]{2,0,1:T(8,128)(2,1)}, u32[]{:S(2)}, u32[]{:S(2)}) %all-to-all-start) | async-done | bytes 4194336 | tf_op jit(solution)/shard_map/all_to_all | solution.py:310
  64.9 0.0 copy-start.2
  64.9 0.0 copy-start.3
  64.9 5.6 %project.3 = (bf16[1024,512]{1,0:T(8,128)(2,1)S(1)}, bf16[1024,512]{1,0:T(8,128)(2,1)S(1)}) custom-call(s32[2048]{0:T(1024)S(1)} %copy-done, f32[4,8,128]{2,1,0:T(8,128)S(1)} %pad_maximum_fusion.lists_ref, bf16[1024,2048]{1,0:T(8,128)(2,1)} %bitcast.4.states_ref.refs_8_), custom_call_target="tpu_custom_call" | custom-call | flops 1073741824 | bytes 8388608 | tf_op jit(solution)/shard_map/project/pallas_call | solution.py:87
  70.5 6.4 %project.2 = (bf16[1024,512]{1,0:T(8,128)(2,1)S(1)}, bf16[1024,512]{1,0:T(8,128)(2,1)}) custom-call(s32[2048]{0:T(1024)S(1)} %copy-done, f32[4,8,128]{2,1,0:T(8,128)S(1)} %pad_maximum_fusion.lists_ref, bf16[1024,2048]{1,0:T(8,128)(2,1)} %bitcast.4.states_ref.refs_8_), custom_call_target="tpu_custom_call" | custom-call | flops 1073741824 | bytes 8388608 | tf_op jit(solution)/shard_map/project/pallas_call | solution.py:87
  76.9 4.6 %collective-permute-start.2 = (bf16[1024,512]{1,0:T(8,128)(2,1)S(1)}, bf16[1024,512]{1,0:T(8,128)(2,1)}, u32[]{:S(2)}, u32[]{:S(2)}) collective-permute-start(bf16[1024,512]{1,0:T(8,128)(2,1)S(1)} %get-tuple-element.14.refs_6_), channel_id=1, source_target_pairs={{0,1},{1,2},{2,3},{3,4},{4,5},{5,6},{6,7},{7,8},{8,9},{9,10},{10,1... | collective-permute-start | bytes 3145736 | tf_op jit(solution)/shard_map/ppermute | solution.py:314
  81.5 1.9 collective-permute-start.3
  83.4 3.6 %collective-permute-start = (bf16[1024,512]{1,0:T(8,128)(2,1)}, bf16[1024,512]{1,0:T(8,128)(2,1)}, u32[]{:S(2)}, u32[]{:S(2)}) collective-permute-start(bf16[1024,512]{1,0:T(8,128)(2,1)} %get-tuple-element.12.refs_2_), channel_id=1, source_target_pairs={{0,1},{1,2},{2,3},{3,4},{4,5},{5,6},{6,7},{7,8},{8,9},{9,10},{10,1... | collective-permute-start | bytes 3145736 | tf_op jit(solution)/shard_map/ppermute | solution.py:314
  87.1 4.1 %collective-permute-start.1 = (bf16[1024,512]{1,0:T(8,128)(2,1)S(1)}, bf16[1024,512]{1,0:T(8,128)(2,1)}, u32[]{:S(2)}, u32[]{:S(2)}) collective-permute-start(bf16[1024,512]{1,0:T(8,128)(2,1)S(1)} %get-tuple-element.13.refs_1_), channel_id=1, source_target_pairs={{1,0},{2,1},{3,2},{4,3},{5,4},{6,5},{7,6},{8,7},{9,8},{10,9},{11,1... | collective-permute-start | bytes 3145736 | tf_op jit(solution)/shard_map/ppermute | solution.py:315
  91.2 0.0 copy-done.2
  91.2 0.0 copy-done.3
  91.2 0.1 multiply_bitcast_fusion.slot_ref
  91.3 1.9 collective-permute-done.2.refs_4_
  93.2 4.8 %collective-permute-done.3.refs_7_ = bf16[1024,512]{1,0:T(8,128)(2,1)} collective-permute-done((bf16[1024,512]{1,0:T(8,128)(2,1)S(1)}, bf16[1024,512]{1,0:T(8,128)(2,1)}, u32[]{:S(2)}, u32[]{:S(2)}) %collective-permute-start.3) | collective-permute-done | bytes 1048608 | tf_op jit(solution)/shard_map/ppermute | solution.py:315
  98.0 6.5 %collective-permute-done.refs_0_ = bf16[1024,512]{1,0:T(8,128)(2,1)} collective-permute-done((bf16[1024,512]{1,0:T(8,128)(2,1)}, bf16[1024,512]{1,0:T(8,128)(2,1)}, u32[]{:S(2)}, u32[]{:S(2)}) %collective-permute-start) | collective-permute-done | bytes 1048608 | tf_op jit(solution)/shard_map/ppermute | solution.py:314
  104.5 4.4 %collective-permute-done.1.refs_3_ = bf16[1024,512]{1,0:T(8,128)(2,1)} collective-permute-done((bf16[1024,512]{1,0:T(8,128)(2,1)S(1)}, bf16[1024,512]{1,0:T(8,128)(2,1)}, u32[]{:S(2)}, u32[]{:S(2)}) %collective-permute-start.1) | collective-permute-done | bytes 1048608 | tf_op jit(solution)/shard_map/ppermute | solution.py:315
  108.9 10.7 %gather_gram.1 = (bf16[16,128,1024]{2,1,0:T(8,128)(2,1)S(1)}, f32[16,128,128]{2,1,0:T(8,128)S(1)}, f32[16,128,128]{2,1,0:T(8,128)S(1)}) custom-call(s32[2048]{0:T(1024)S(1)} %multiply_bitcast_fusion.slot_ref, bf16[1024,512]{1,0:T(8,128)(2,1)} %collective-permute-done.refs_0_, bf16[1024,512]{1,0:T(8,128)(2,1)S(1)} %get-tuple-element.13.refs_1_, ...), custom_call_target="tpu_custom_call" | custom-call | flops 1073741824 | bytes 33554432 | tf_op jit(solution)/shard_map/gather_gram/pallas_call | solution.py:165
  119.6 15.6 %invert_blocks.1.inverse_ref = f32[16,128,128]{2,1,0:T(8,128)S(1)} custom-call(f32[16,128,128]{2,1,0:T(8,128)S(1)} %get-tuple-element.16.gram_ref), custom_call_target="tpu_custom_call" | custom-call | tf_op jit(solution)/shard_map/invert_blocks/pallas_call | solution.py:245
  135.3 6.4 %update.1 = bf16[32,32,2048]{2,1,0:T(8,128)(2,1)S(1)} custom-call(f32[16,128,128]{2,1,0:T(8,128)S(1)} %invert_blocks.1.inverse_ref, f32[16,128,128]{2,1,0:T(8,128)S(1)} %get-tuple-element.17.moved_ref, bf16[16,128,1024]{2,1,0:T(8,128)(2,1)S(1)} %get-tuple-element.18.columns_ref, bf16[1024,2048]{1,0:T(8,128)(2,1)} %bitcast.4.states_ref.refs_8_), custom_call_target="tpu_custom_call" | custom-call | tf_op jit(solution)/shard_map/update/pallas_call | solution.py:278
  141.7 62.9 %all_to_all.35 = bf16[32,32,2048]{2,1,0:T(8,128)(2,1)S(1)} all-to-all(bf16[32,32,2048]{2,1,0:T(8,128)(2,1)S(1)} %update.1), channel_id=1, replica_groups=mesh['space'=8,'mem'=32] {'mem'}, dimensions={0} | all-to-all | bytes 8388608 | tf_op jit(solution)/shard_map/all_to_all | solution.py:319
  204.6 2.3 %copy.10 = bf16[32,4,8,2048]{3,2,0,1:T(8,128)(2,1)} copy(bf16[32,4,8,2048]{3,2,1,0:T(8,128)(2,1)S(1)} %bitcast.15) | data formatting | bytes 8388608 | tf_op jit(solution)/shard_map/all_to_all | solution.py:319
  (3 shorter events, 0.0 us)
Async XLA Ops:
  4.8 8.0 %copy-start = (s32[2048]{0:T(1024)S(1)}, s32[2048]{0:T(1024)}, u32[]{:S(2)}) copy-start(s32[2048]{0:T(1024)} %cell_ref.3) | copy-start | bytes 24580
  4.8 8.0 %copy-start.1 = (f32[2048]{0:T(1024)S(1)}, f32[2048]{0:T(1024)}, u32[]{:S(2)}) copy-start(f32[2048]{0:T(1024)} %param.7) | copy-start | bytes 24580
  4.8 60.1 %all-to-all-start = ((bf16[32,32,2048]{2,0,1:T(8,128)(2,1)}), bf16[32,32,2048]{2,0,1:T(8,128)(2,1)}, u32[]{:S(2)}, u32[]{:S(2)}) async-start(bf16[32,32,2048]{2,0,1:T(8,128)(2,1)} %bitcast.14), calls=%async_computation | async-start | bytes 8388608 | tf_op jit(solution)/shard_map/all_to_all | solution.py:310
  64.9 26.3 %copy-start.2 = (s32[16,128]{1,0:T(8,128)S(1)}, s32[16,128]{1,0:T(8,128)}, u32[]{:S(2)}) copy-start(s32[16,128]{1,0:T(8,128)} %param.8) | copy-start | bytes 24580
  64.9 26.3 %copy-start.3 = (s32[16]{0:T(128)S(1)}, s32[16]{0:T(128)}, u32[]{:S(2)}) copy-start(s32[16]{0:T(128)} %param.9) | copy-start | bytes 196
  76.9 16.3 %collective-permute-start.2 = (bf16[1024,512]{1,0:T(8,128)(2,1)S(1)}, bf16[1024,512]{1,0:T(8,128)(2,1)}, u32[]{:S(2)}, u32[]{:S(2)}) collective-permute-start(bf16[1024,512]{1,0:T(8,128)(2,1)S(1)} %get-tuple-element.14.refs_6_), channel_id=1, source_target_pairs={{0,1},{1,2},{2,3},{3,4},{4,5},{5,6},{6,7},{7,8},{8,9},{9,10},{10,1... | collective-permute-start | bytes 3145736 | tf_op jit(solution)/shard_map/ppermute | solution.py:314
  81.5 16.5 %collective-permute-start.3 = (bf16[1024,512]{1,0:T(8,128)(2,1)S(1)}, bf16[1024,512]{1,0:T(8,128)(2,1)}, u32[]{:S(2)}, u32[]{:S(2)}) collective-permute-start(bf16[1024,512]{1,0:T(8,128)(2,1)S(1)} %get-tuple-element.15.refs_5_), channel_id=1, source_target_pairs={{1,0},{2,1},{3,2},{4,3},{5,4},{6,5},{7,6},{8,7},{9,8},{10,9},{11,1... | collective-permute-start | bytes 3145736 | tf_op jit(solution)/shard_map/ppermute | solution.py:315
  83.4 21.1 %collective-permute-start = (bf16[1024,512]{1,0:T(8,128)(2,1)}, bf16[1024,512]{1,0:T(8,128)(2,1)}, u32[]{:S(2)}, u32[]{:S(2)}) collective-permute-start(bf16[1024,512]{1,0:T(8,128)(2,1)} %get-tuple-element.12.refs_2_), channel_id=1, source_target_pairs={{0,1},{1,2},{2,3},{3,4},{4,5},{5,6},{6,7},{7,8},{8,9},{9,10},{10,1... | collective-permute-start | bytes 3145736 | tf_op jit(solution)/shard_map/ppermute | solution.py:314
  87.1 21.9 %collective-permute-start.1 = (bf16[1024,512]{1,0:T(8,128)(2,1)S(1)}, bf16[1024,512]{1,0:T(8,128)(2,1)}, u32[]{:S(2)}, u32[]{:S(2)}) collective-permute-start(bf16[1024,512]{1,0:T(8,128)(2,1)S(1)} %get-tuple-element.13.refs_1_), channel_id=1, source_target_pairs={{1,0},{2,1},{3,2},{4,3},{5,4},{6,5},{7,6},{8,7},{9,8},{10,9},{11,1... | collective-permute-start | bytes 3145736 | tf_op jit(solution)/shard_map/ppermute | solution.py:315

commit v7 on v6

--- a/solution.py
+++ b/solution.py
@@ -209,35 +209,35 @@
     cols = lax.broadcasted_iota(jnp.int32, (1, n, n), 2)
     work[...] = gram_ref[...] + jnp.where(rows == cols, 1.0, 0.0)
 
-    def step(number, carry):
-        flip = lane2 >= n - number * NB
-        panel = [[work[b, at : at + 8, :] for at in range(0, NB, 8)] for b in range(nblk)]
+    for start in range(0, n, NB):
+        panel = [[work[b, at : at + 8, :] for at in range(start, start + NB, 8)] for b in range(nblk)]
         for k in range(NB):
-            here = lane == k
+            here = lane == start + k
             own, at = divmod(k, 8)
             for b in range(nblk):
-                col = [jnp.broadcast_to(p[:, k : k + 1], (8, n)) for p in panel[b]]
+                col = [jnp.broadcast_to(p[:, start + k : start + k + 1], (8, n)) for p in panel[b]]
                 inv = 1.0 / col[own][at : at + 1, :]
                 scaled = jnp.where(here[0:1], inv, panel[b][own][at : at + 1, :] * inv)
                 scaled = jnp.broadcast_to(scaled, (8, n))
                 new = [jnp.where(here, 0.0, p) - c * scaled for p, c in zip(panel[b], col)]
                 new[own] = jnp.where(sub == at, scaled, new[own])
                 panel[b] = new
+        inside = (lane2 >= start) & (lane2 < start + NB)
         for b in range(nblk):
-            sides = work[b, 0:NB, :]
-            sides = jnp.where(flip, -sides, sides)
-            rolled = pltpu.roll(jnp.concatenate(panel[b], axis=0), n - NB, 1)
-            rh, rm, rl = three_way(rolled)
+            sides = work[b, start : start + NB, :]
+            sides = jnp.where(lane2 < start, -sides, sides)
+            done = jnp.concatenate(panel[b], axis=0)
+            rh, rm, rl = three_way(done)
             ch, cm, cl = three_way(sides)
             rhs = jnp.concatenate([rh, rm, rh, rl, rm, rh, rl, rm], axis=0)
             lhs = jnp.concatenate([ch, ch, cm, ch, cm, cl, cm, cl], axis=0)
             change = dot(lhs, rhs, TN)
-            kept = pltpu.roll(jnp.where(lane2 < NB, 0.0, work[b, NB:n, :]), n - NB, 1)
-            work[b, 0 : n - NB, :] = kept - change[NB:n]
-            work[b, n - NB : n, :] = rolled
-        return carry
-
-    lax.fori_loop(0, n // NB, step, 0)
+            for rows_at, count in ((0, start), (start + NB, n - NB - start)):
+                if count:
+                    rows = slice(rows_at, rows_at + count)
+                    work[b, rows, :] = jnp.where(inside, 0.0, work[b, rows, :]) - change[rows]
+            work[b, start : start + NB, :] = done
+
     out_ref[...] = work[...]
 
 
@@ -296,9 +296,7 @@
     members = deviations.shape[0] * groups
     obs_dev = obs_cell.shape[0]
     weight = obs_weight * (1.0 / math.sqrt(members - 1))
-    lists = jnp.concatenate(
-        [v.reshape(-1, TILE // 128, 128) for v in (obs_cell.astype(jnp.float32), weight)], axis=1
-    )
+    lists = jnp.concatenate([v.reshape(-1, TILE // 128, 128) for v in (obs_cell.astype(jnp.float32), weight)], axis=1)
     line_index = lax.axis_index("space") * groups + lax.axis_index("mem")
     local_index = block_obs - (line_index * obs_dev - obs_dev // 2)
     slot_ids = jnp.arange(block_obs.shape[1], dtype=jnp.int32)
@@ -307,6 +305,7 @@
     size = lax.axis_size("space") * groups
     up = [(i, i + 1) for i in range(size - 1)]
     down = [(b, a) for a, b in up]
+    deviations, lists = lax.optimization_barrier((deviations, lists))
     states = lax.all_to_all(deviations, "mem", split_axis=1, concat_axis=0, tiled=True)
     pieces = []
     for piece in range(PIECES):
@@ -331,6 +330,4 @@
     )
     out_specs = P("mem", "space")
 
-    return jax.shard_map(
-        on_device, mesh=mesh, in_specs=in_specs, out_specs=out_specs, check_vma=False
-    )
+    return jax.shard_map(on_device, mesh=mesh, in_specs=in_specs, out_specs=out_specs, check_vma=False)

time: 207 us -> 199 us (0.961)
  blocking collectives: 62.9 us -> 123 us
  waiting for transfers between devices: 69.7 us -> 15.9 us
  starting transfers between devices: 22.2 us -> 13.9 us
  Pallas kernels: 44.8 us -> 39.4 us
  local copies, waits for them, and re-layouts: 7.12 us -> 4.84 us
    all_to_all x0 -> x1, blocking collectives: none -> 58.2 us  [on_device(): lax.all_to_all(deviations, 'mem', split_axis=1, concat_axis=0, tiled=True)]
    all_to_all x1 -> x0, waiting for transfers between devices: 52.1 us -> none  [on_device(): lax.all_to_all(deviations, 'mem', split_axis=1, concat_axis=0, tiled=True)]
    all_to_all x1 -> x0, starting transfers between devices: 7.95 us -> none  [on_device(): lax.all_to_all(deviations, 'mem', split_axis=1, concat_axis=0, tiled=True)]
    pallas_call x2, Pallas kernels: 12 us -> 8.81 us  [project(): pl.pallas_call(project_kernel, grid_spec=pltpu.PrefetchScalarGridSpec(num...]
    ppermute x2, starting transfers between devices: 8.21 us -> 5.54 us  [on_device(): low = lax.ppermute(last, ('space', 'mem'), up)]
    ppermute x2, starting transfers between devices: 6.04 us -> 8.36 us  [on_device(): high = lax.ppermute(first, ('space', 'mem'), down)]
    all_to_all x1, local copies, waits for them, and re-layouts: 4.79 us -> 2.5 us  [on_device(): lax.all_to_all(deviations, 'mem', split_axis=1, concat_axis=0, tiled=True)]
  transfers between devices with their start and end apart: 5 -> 4, of which waited for: 5 -> 3; matrix products, arithmetic and copies ran while one was open for 0% -> 0% of each run, Pallas kernels for 0% -> 0%
where the time goes in v7:
time: 199 us; the launch traced here: 198 us
  blocking collectives  123 us (62%)
  Pallas kernels  39.4 us (20%)
  waiting for transfers between devices  15.9 us (8%)
  starting transfers between devices  13.9 us (7%)
  local copies, waits for them, and re-layouts  4.84 us (2%)
    all_to_all x1, blocking collectives, on_device(): lax.all_to_all(analysis.reshape(members, -1), 'mem', split_axis=0, concat...  64.5 us
    all_to_all x1, blocking collectives, on_device(): lax.all_to_all(deviations, 'mem', split_axis=1, concat_axis=0, tiled=True)  58.2 us
    pallas_call x1, Pallas kernels, invert(): pl.pallas_call(invert_kernel, out_shape=jax.ShapeDtypeStruct(gram.shape,...  14 us
    pallas_call x1, Pallas kernels, gather_gram(): pl.pallas_call(gram_kernel, grid_spec=pltpu.PrefetchScalarGridSpec(num_sc...  11 us
    ppermute x2, waiting for transfers between devices, on_device(): high = lax.ppermute(first, ('space', 'mem'), down)  9.33 us
    pallas_call x2, Pallas kernels, project(): pl.pallas_call(project_kernel, grid_spec=pltpu.PrefetchScalarGridSpec(num...  8.81 us
    ppermute x2, starting transfers between devices, on_device(): high = lax.ppermute(first, ('space', 'mem'), down)  8.36 us
    ppermute x2, waiting for transfers between devices, on_device(): low = lax.ppermute(last, ('space', 'mem'), up)  6.55 us
  transfers between devices with their start and end apart: 4, of which 3 were waited for; matrix products, arithmetic and copies ran while one was open for 0% of the time, Pallas kernels for 0%

profile of v7, /device:TPU:97, one launch (start us, length us, event | category | flops | bytes accessed | tf_op | source)
XLA Modules:
  0.0 198.3 jit_solution(17940094004647849742)
XLA Ops:
  0.0 0.7 broadcast_multiply_fusion
  0.7 0.7 convert_element_type.3
  1.4 2.5 %copy.12 = bf16[4,32,8,2048]{3,2,0,1:T(8,128)(2,1)S(1)} copy(bf16[4,32,8,2048]{3,2,1,0:T(8,128)(2,1)} %bitcast.20) | data formatting | bytes 8388608 | tf_op jit(solution)/shard_map/all_to_all | solution.py:309
  3.9 0.0 copy-start.2
  3.9 58.2 %all_to_all.35 = bf16[32,32,2048]{2,0,1:T(8,128)(2,1)S(1)} all-to-all(bf16[32,32,2048]{2,0,1:T(8,128)(2,1)S(1)} %bitcast.19), channel_id=1, replica_groups=mesh['space'=8,'mem'=32] {'mem'}, dimensions={1} | all-to-all | bytes 8388608 | tf_op jit(solution)/shard_map/all_to_all | solution.py:309
  62.1 0.0 copy-start
  62.1 0.0 copy-done.2
  62.1 0.0 copy-start.3
  62.1 0.0 copy-start.4
  62.1 4.0 %project.3 = (bf16[1024,512]{1,0:T(8,128)(2,1)S(1)}, bf16[1024,512]{1,0:T(8,128)(2,1)S(1)}) custom-call(s32[2048]{0:T(1024)S(1)} %copy-done.2, f32[4,8,128]{2,1,0:T(8,128)S(1)} %pad_maximum_fusion.lists_ref, bf16[1024,2048]{1,0:T(8,128)(2,1)S(1)} %bitcast.14), custom_call_target="tpu_custom_call" | custom-call | flops 1073741824 | bytes 8388608 | tf_op jit(solution)/shard_map/project/pallas_call | solution.py:87
  66.1 4.8 %project.2 = (bf16[1024,512]{1,0:T(8,128)(2,1)S(1)}, bf16[1024,512]{1,0:T(8,128)(2,1)}) custom-call(s32[2048]{0:T(1024)S(1)} %copy-done.2, f32[4,8,128]{2,1,0:T(8,128)S(1)} %pad_maximum_fusion.lists_ref, bf16[1024,2048]{1,0:T(8,128)(2,1)S(1)} %bitcast.15), custom_call_target="tpu_custom_call" | custom-call | flops 1073741824 | bytes 8388608 | tf_op jit(solution)/shard_map/project/pallas_call | solution.py:87
  70.9 0.0 copy-done
  70.9 2.1 %collective-permute-start.2 = (bf16[1024,512]{1,0:T(8,128)(2,1)S(1)}, bf16[1024,512]{1,0:T(8,128)(2,1)}, u32[]{:S(2)}, u32[]{:S(2)}) collective-permute-start(bf16[1024,512]{1,0:T(8,128)(2,1)S(1)} %get-tuple-element.18.refs_6_), channel_id=1, source_target_pairs={{0,1},{1,2},{2,3},{3,4},{4,5},{5,6},{6,7},{7,8},{8,9},{9,10},{10,1... | collective-permute-start | bytes 3145736 | tf_op jit(solution)/shard_map/ppermute | solution.py:313
  73.1 2.2 %collective-permute-start.3 = (bf16[1024,512]{1,0:T(8,128)(2,1)S(1)}, bf16[1024,512]{1,0:T(8,128)(2,1)}, u32[]{:S(2)}, u32[]{:S(2)}) collective-permute-start(bf16[1024,512]{1,0:T(8,128)(2,1)S(1)} %get-tuple-element.19.refs_5_), channel_id=1, source_target_pairs={{1,0},{2,1},{3,2},{4,3},{5,4},{6,5},{7,6},{8,7},{9,8},{10,9},{11,1... | collective-permute-start | bytes 3145736 | tf_op jit(solution)/shard_map/ppermute | solution.py:314
  75.3 3.4 %collective-permute-start = (bf16[1024,512]{1,0:T(8,128)(2,1)}, bf16[1024,512]{1,0:T(8,128)(2,1)}, u32[]{:S(2)}, u32[]{:S(2)}) collective-permute-start(bf16[1024,512]{1,0:T(8,128)(2,1)} %get-tuple-element.16.refs_2_), channel_id=1, source_target_pairs={{0,1},{1,2},{2,3},{3,4},{4,5},{5,6},{6,7},{7,8},{8,9},{9,10},{10,1... | collective-permute-start | bytes 3145736 | tf_op jit(solution)/shard_map/ppermute | solution.py:313
  78.7 6.2 %collective-permute-start.1 = (bf16[1024,512]{1,0:T(8,128)(2,1)S(1)}, bf16[1024,512]{1,0:T(8,128)(2,1)}, u32[]{:S(2)}, u32[]{:S(2)}) collective-permute-start(bf16[1024,512]{1,0:T(8,128)(2,1)S(1)} %get-tuple-element.17.refs_1_), channel_id=1, source_target_pairs={{1,0},{2,1},{3,2},{4,3},{5,4},{6,5},{7,6},{8,7},{9,8},{10,9},{11,1... | collective-permute-start | bytes 3145736 | tf_op jit(solution)/shard_map/ppermute | solution.py:314
  84.9 0.0 copy-done.3
  84.9 0.0 copy-done.4
  84.9 0.1 multiply_bitcast_fusion.slot_ref
  85.0 0.0 collective-permute-done.2.refs_4_
  85.0 4.6 %collective-permute-done.3.refs_7_ = bf16[1024,512]{1,0:T(8,128)(2,1)} collective-permute-done((bf16[1024,512]{1,0:T(8,128)(2,1)S(1)}, bf16[1024,512]{1,0:T(8,128)(2,1)}, u32[]{:S(2)}, u32[]{:S(2)}) %collective-permute-start.3) | collective-permute-done | bytes 1048608 | tf_op jit(solution)/shard_map/ppermute | solution.py:314
  89.6 6.5 %collective-permute-done.refs_0_ = bf16[1024,512]{1,0:T(8,128)(2,1)} collective-permute-done((bf16[1024,512]{1,0:T(8,128)(2,1)}, bf16[1024,512]{1,0:T(8,128)(2,1)}, u32[]{:S(2)}, u32[]{:S(2)}) %collective-permute-start) | collective-permute-done | bytes 1048608 | tf_op jit(solution)/shard_map/ppermute | solution.py:313
  96.2 4.7 %collective-permute-done.1.refs_3_ = bf16[1024,512]{1,0:T(8,128)(2,1)} collective-permute-done((bf16[1024,512]{1,0:T(8,128)(2,1)S(1)}, bf16[1024,512]{1,0:T(8,128)(2,1)}, u32[]{:S(2)}, u32[]{:S(2)}) %collective-permute-start.1) | collective-permute-done | bytes 1048608 | tf_op jit(solution)/shard_map/ppermute | solution.py:314
  100.8 0.0 copy-start.1
  100.8 11.0 %gather_gram.1 = (bf16[16,128,1024]{2,1,0:T(8,128)(2,1)S(1)}, f32[16,128,128]{2,1,0:T(8,128)S(1)}, f32[16,128,128]{2,1,0:T(8,128)S(1)}) custom-call(s32[2048]{0:T(1024)S(1)} %multiply_bitcast_fusion.slot_ref, bf16[1024,512]{1,0:T(8,128)(2,1)} %collective-permute-done.refs_0_, bf16[1024,512]{1,0:T(8,128)(2,1)S(1)} %get-tuple-element.17.refs_1_, ...), custom_call_target="tpu_custom_call" | custom-call | flops 1073741824 | bytes 33554432 | tf_op jit(solution)/shard_map/gather_gram/pallas_call | solution.py:165
  111.9 14.0 %invert_blocks.1.inverse_ref = f32[16,128,128]{2,1,0:T(8,128)S(1)} custom-call(f32[16,128,128]{2,1,0:T(8,128)S(1)} %get-tuple-element.20.gram_ref), custom_call_target="tpu_custom_call" | custom-call | tf_op jit(solution)/shard_map/invert_blocks/pallas_call | solution.py:245
  125.9 0.0 copy-done.1
  125.9 5.5 %update.1 = bf16[32,32,2048]{2,1,0:T(8,128)(2,1)S(1)} custom-call(f32[16,128,128]{2,1,0:T(8,128)S(1)} %invert_blocks.1.inverse_ref, f32[16,128,128]{2,1,0:T(8,128)S(1)} %get-tuple-element.21.moved_ref, bf16[16,128,1024]{2,1,0:T(8,128)(2,1)S(1)} %get-tuple-element.22.columns_ref, bf16[1024,2048]{1,0:T(8,128)(2,1)S(1)} %bitcast.17), custom_call_target="tpu_custom_call" | custom-call | tf_op jit(solution)/shard_map/update/pallas_call | solution.py:278
  131.4 64.5 %all_to_all.36 = bf16[32,32,2048]{2,1,0:T(8,128)(2,1)S(1)} all-to-all(bf16[32,32,2048]{2,1,0:T(8,128)(2,1)S(1)} %update.1), channel_id=1, replica_groups=mesh['space'=8,'mem'=32] {'mem'}, dimensions={0} | all-to-all | bytes 8388608 | tf_op jit(solution)/shard_map/all_to_all | solution.py:318
  195.9 2.3 %copy.10 = bf16[32,4,8,2048]{3,2,0,1:T(8,128)(2,1)} copy(bf16[32,4,8,2048]{3,2,1,0:T(8,128)(2,1)S(1)} %bitcast.18) | data formatting | bytes 8388608 | tf_op jit(solution)/shard_map/all_to_all | solution.py:318
  (1 shorter events, 0.0 us)
Async XLA Ops:
  3.9 58.2 %copy-start.2 = (s32[2048]{0:T(1024)S(1)}, s32[2048]{0:T(1024)}, u32[]{:S(2)}) copy-start(s32[2048]{0:T(1024)} %cell_ref.3) | copy-start | bytes 24580
  62.1 8.8 %copy-start = (bf16[32,32,2048]{2,0,1:T(8,128)(2,1)}, bf16[32,32,2048]{2,0,1:T(8,128)(2,1)S(1)}, u32[]{:S(2)}) copy-start(bf16[32,32,2048]{2,0,1:T(8,128)(2,1)S(1)} %all_to_all.35) | copy-start | bytes 12582916
  62.1 22.8 %copy-start.3 = (s32[16,128]{1,0:T(8,128)S(1)}, s32[16,128]{1,0:T(8,128)}, u32[]{:S(2)}) copy-start(s32[16,128]{1,0:T(8,128)} %param.8) | copy-start | bytes 24580
  62.1 22.8 %copy-start.4 = (s32[16]{0:T(128)S(1)}, s32[16]{0:T(128)}, u32[]{:S(2)}) copy-start(s32[16]{0:T(128)} %param.9) | copy-start | bytes 196
  70.9 14.0 %collective-permute-start.2 = (bf16[1024,512]{1,0:T(8,128)(2,1)S(1)}, bf16[1024,512]{1,0:T(8,128)(2,1)}, u32[]{:S(2)}, u32[]{:S(2)}) collective-permute-start(bf16[1024,512]{1,0:T(8,128)(2,1)S(1)} %get-tuple-element.18.refs_6_), channel_id=1, source_target_pairs={{0,1},{1,2},{2,3},{3,4},{4,5},{5,6},{6,7},{7,8},{8,9},{9,10},{10,1... | collective-permute-start | bytes 3145736 | tf_op jit(solution)/shard_map/ppermute | solution.py:313
  73.1 16.5 %collective-permute-start.3 = (bf16[1024,512]{1,0:T(8,128)(2,1)S(1)}, bf16[1024,512]{1,0:T(8,128)(2,1)}, u32[]{:S(2)}, u32[]{:S(2)}) collective-permute-start(bf16[1024,512]{1,0:T(8,128)(2,1)S(1)} %get-tuple-element.19.refs_5_), channel_id=1, source_target_pairs={{1,0},{2,1},{3,2},{4,3},{5,4},{6,5},{7,6},{8,7},{9,8},{10,9},{11,1... | collective-permute-start | bytes 3145736 | tf_op jit(solution)/shard_map/ppermute | solution.py:314
  75.3 20.9 %collective-permute-start = (bf16[1024,512]{1,0:T(8,128)(2,1)}, bf16[1024,512]{1,0:T(8,128)(2,1)}, u32[]{:S(2)}, u32[]{:S(2)}) collective-permute-start(bf16[1024,512]{1,0:T(8,128)(2,1)} %get-tuple-element.16.refs_2_), channel_id=1, source_target_pairs={{0,1},{1,2},{2,3},{3,4},{4,5},{5,6},{6,7},{7,8},{8,9},{9,10},{10,1... | collective-permute-start | bytes 3145736 | tf_op jit(solution)/shard_map/ppermute | solution.py:313
  78.7 22.2 %collective-permute-start.1 = (bf16[1024,512]{1,0:T(8,128)(2,1)S(1)}, bf16[1024,512]{1,0:T(8,128)(2,1)}, u32[]{:S(2)}, u32[]{:S(2)}) collective-permute-start(bf16[1024,512]{1,0:T(8,128)(2,1)S(1)} %get-tuple-element.17.refs_1_), channel_id=1, source_target_pairs={{1,0},{2,1},{3,2},{4,3},{5,4},{6,5},{7,6},{8,7},{9,8},{10,9},{11,1... | collective-permute-start | bytes 3145736 | tf_op jit(solution)/shard_map/ppermute | solution.py:314
  100.8 25.1 %copy-start.1 = (bf16[32,32,2048]{2,0,1:T(8,128)(2,1)S(1)}, bf16[32,32,2048]{2,0,1:T(8,128)(2,1)}, u32[]{:S(2)}) copy-start(bf16[32,32,2048]{2,0,1:T(8,128)(2,1)} %copy-done) | copy-start | bytes 12582916

commit v8 on v7

--- a/solution.py
+++ b/solution.py
@@ -1,3 +1,4 @@
+import functools
 import math
 
 import jax
@@ -24,13 +25,13 @@
     return lax.dot_general(a, b, dims, precision=precision, preferred_element_type=jnp.float32)
 
 
-def project_kernel(cell_ref, lists_ref, states_ref, first_ref, last_ref, acc_ref):
+def project_kernel(cell_ref, cells_ref, weights_ref, states_ref, first_ref, last_ref, acc_ref, *, scale):
     tile = pl.program_id(0)
     half = pl.num_programs(0) // 2
     width = states_ref.shape[1]
     lane = lax.broadcasted_iota(jnp.int32, (TILE, 128), 1).astype(jnp.float32)
     parts = TILE // 128
-    upright = lists_ref[0].T
+    upright = jnp.concatenate([cells_ref[0].astype(jnp.float32), weights_ref[0] * scale], axis=0).T
 
     def column(at):
         return jnp.concatenate(
@@ -78,19 +79,22 @@
         first_ref[...] = last_ref[...]
 
 
-def project(obs_cell, lists, states, piece):
+def project(obs_cell, obs_weight, states, piece):
+    lists = [v.reshape(-1, TILE // 128, 128) for v in (obs_cell, obs_weight)]
+    scale = 1.0 / math.sqrt(states.shape[0] - 1)
     width = states.shape[1]
     members = states.shape[0] // PIECES
     obs = obs_cell.shape[0]
     half = obs // TILE // 2
     side = jax.ShapeDtypeStruct((obs // 2, members), jnp.bfloat16)
     return pl.pallas_call(
-        project_kernel,
+        functools.partial(project_kernel, scale=scale),
         grid_spec=pltpu.PrefetchScalarGridSpec(
             num_scalar_prefetch=1,
             grid=(obs // TILE,),
             in_specs=[
-                pl.BlockSpec((1, 2 * TILE // 128, 128), lambda i, c: (i, 0, 0)),
+                pl.BlockSpec((1, TILE // 128, 128), lambda i, c: (i, 0, 0)),
+                pl.BlockSpec((1, TILE // 128, 128), lambda i, c: (i, 0, 0)),
                 pl.BlockSpec((members, width), lambda i, c: (piece, 0)),
             ],
             out_specs=(
@@ -105,7 +109,7 @@
             flops=2 * obs * members * SPAN, bytes_accessed=8 * obs * members, transcendentals=0
         ),
         name="project",
-    )(obs_cell, lists, states)
+    )(obs_cell, *lists, states)
 
 
 def gram_kernel(slot_ref, *refs):
@@ -295,8 +299,6 @@
     groups = lax.axis_size("mem")
     members = deviations.shape[0] * groups
     obs_dev = obs_cell.shape[0]
-    weight = obs_weight * (1.0 / math.sqrt(members - 1))
-    lists = jnp.concatenate([v.reshape(-1, TILE // 128, 128) for v in (obs_cell.astype(jnp.float32), weight)], axis=1)
     line_index = lax.axis_index("space") * groups + lax.axis_index("mem")
     local_index = block_obs - (line_index * obs_dev - obs_dev // 2)
     slot_ids = jnp.arange(block_obs.shape[1], dtype=jnp.int32)
@@ -305,11 +307,10 @@
     size = lax.axis_size("space") * groups
     up = [(i, i + 1) for i in range(size - 1)]
     down = [(b, a) for a, b in up]
-    deviations, lists = lax.optimization_barrier((deviations, lists))
     states = lax.all_to_all(deviations, "mem", split_axis=1, concat_axis=0, tiled=True)
     pieces = []
     for piece in range(PIECES):
-        first, last = project(obs_cell, lists, states, piece)
+        first, last = project(obs_cell, obs_weight, states, piece)
         low = lax.ppermute(last, ("space", "mem"), up)
         high = lax.ppermute(first, ("space", "mem"), down)
         pieces += [low, first, last, high]

time: 199 us -> 197 us (0.990)
  no operation moved by 1% of the time
where the time goes in v8:
time: 197 us
  blocking collectives  123 us (62%)
  Pallas kernels  39.4 us (20%)
  waiting for transfers between devices  15.9 us (8%)
  starting transfers between devices  13.9 us (7%)
  local copies, waits for them, and re-layouts  4.85 us (2%)
    all_to_all x1, blocking collectives, on_device(): lax.all_to_all(analysis.reshape(members, -1), 'mem', split_axis=0, concat...  64.5 us
    all_to_all x1, blocking collectives, on_device(): lax.all_to_all(deviations, 'mem', split_axis=1, concat_axis=0, tiled=True)  58.2 us
    pallas_call x1, Pallas kernels, invert(): pl.pallas_call(invert_kernel, out_shape=jax.ShapeDtypeStruct(gram.shape,...  14 us
    pallas_call x1, Pallas kernels, gather_gram(): pl.pallas_call(gram_kernel, grid_spec=pltpu.PrefetchScalarGridSpec(num_sc...  11 us
    ppermute x2, waiting for transfers between devices, on_device(): high = lax.ppermute(first, ('space', 'mem'), down)  9.33 us
    pallas_call x2, Pallas kernels, project(): pl.pallas_call(functools.partial(project_kernel, scale=scale), grid_spec=...  8.86 us
    ppermute x2, starting transfers between devices, on_device(): high = lax.ppermute(first, ('space', 'mem'), down)  8.37 us
    ppermute x2, waiting for transfers between devices, on_device(): low = lax.ppermute(last, ('space', 'mem'), up)  6.55 us
  transfers between devices with their start and end apart: 4, of which 3 were waited for; matrix products, arithmetic and copies ran while one was open for 0% of the time, Pallas kernels for 0%

profile of v8, /device:TPU:97, one launch (start us, length us, event | category | flops | bytes accessed | tf_op | source)
XLA Modules:
  0.0 196.9 jit_solution(12664769150001571075)
XLA Ops:
  0.0 2.5 %copy.12 = bf16[4,32,8,2048]{3,2,0,1:T(8,128)(2,1)S(1)} copy(bf16[4,32,8,2048]{3,2,1,0:T(8,128)(2,1)} %bitcast.24) | data formatting | bytes 8388608 | tf_op jit(solution)/shard_map/all_to_all | solution.py:310
  2.5 0.0 copy-start.2
  2.5 0.0 copy-start.3
  2.5 58.2 %all_to_all.35 = bf16[32,32,2048]{2,0,1:T(8,128)(2,1)S(1)} all-to-all(bf16[32,32,2048]{2,0,1:T(8,128)(2,1)S(1)} %bitcast.23), channel_id=1, replica_groups=mesh['space'=8,'mem'=32] {'mem'}, dimensions={1} | all-to-all | bytes 8388608 | tf_op jit(solution)/shard_map/all_to_all | solution.py:310
  60.7 0.0 copy-start
  60.7 0.0 copy-done.2
  60.7 0.0 copy-done.3
  60.7 0.0 copy-start.4
  60.7 0.0 copy-start.5
  60.7 4.0 %project.3 = (bf16[1024,512]{1,0:T(8,128)(2,1)S(1)}, bf16[1024,512]{1,0:T(8,128)(2,1)S(1)}) custom-call(s32[2048]{0:T(1024)S(1)} %copy-done.2, s32[4,4,128]{2,1,0:T(4,128)S(1)} %bitcast.18, f32[4,4,128]{2,1,0:T(4,128)S(1)} %bitcast.20, bf16[1024,2048]{1,0:T(8,128)(2,1)S(1)} %bitcast.14), custom_call_target="tpu_custom_call" | custom-call | flops 1073741824 | bytes 8388608 | tf_op jit(solution)/shard_map/project/pallas_call | solution.py:90
  64.8 4.8 %project.2 = (bf16[1024,512]{1,0:T(8,128)(2,1)S(1)}, bf16[1024,512]{1,0:T(8,128)(2,1)}) custom-call(s32[2048]{0:T(1024)S(1)} %copy-done.2, s32[4,4,128]{2,1,0:T(4,128)S(1)} %bitcast.19, f32[4,4,128]{2,1,0:T(4,128)S(1)} %bitcast.21, bf16[1024,2048]{1,0:T(8,128)(2,1)S(1)} %bitcast.15), custom_call_target="tpu_custom_call" | custom-call | flops 1073741824 | bytes 8388608 | tf_op jit(solution)/shard_map/project/pallas_call | solution.py:90
  69.6 0.0 copy-done
  69.6 2.1 %collective-permute-start.2 = (bf16[1024,512]{1,0:T(8,128)(2,1)S(1)}, bf16[1024,512]{1,0:T(8,128)(2,1)}, u32[]{:S(2)}, u32[]{:S(2)}) collective-permute-start(bf16[1024,512]{1,0:T(8,128)(2,1)S(1)} %get-tuple-element.14.refs_6_), channel_id=1, source_target_pairs={{0,1},{1,2},{2,3},{3,4},{4,5},{5,6},{6,7},{7,8},{8,9},{9,10},{10,1... | collective-permute-start | bytes 3145736 | tf_op jit(solution)/shard_map/ppermute | solution.py:314
  71.7 2.2 %collective-permute-start.3 = (bf16[1024,512]{1,0:T(8,128)(2,1)S(1)}, bf16[1024,512]{1,0:T(8,128)(2,1)}, u32[]{:S(2)}, u32[]{:S(2)}) collective-permute-start(bf16[1024,512]{1,0:T(8,128)(2,1)S(1)} %get-tuple-element.15.refs_5_), channel_id=1, source_target_pairs={{1,0},{2,1},{3,2},{4,3},{5,4},{6,5},{7,6},{8,7},{9,8},{10,9},{11,1... | collective-permute-start | bytes 3145736 | tf_op jit(solution)/shard_map/ppermute | solution.py:315
  73.9 3.4 %collective-permute-start = (bf16[1024,512]{1,0:T(8,128)(2,1)}, bf16[1024,512]{1,0:T(8,128)(2,1)}, u32[]{:S(2)}, u32[]{:S(2)}) collective-permute-start(bf16[1024,512]{1,0:T(8,128)(2,1)} %get-tuple-element.12.refs_2_), channel_id=1, source_target_pairs={{0,1},{1,2},{2,3},{3,4},{4,5},{5,6},{6,7},{7,8},{8,9},{9,10},{10,1... | collective-permute-start | bytes 3145736 | tf_op jit(solution)/shard_map/ppermute | solution.py:314
  77.3 6.2 %collective-permute-start.1 = (bf16[1024,512]{1,0:T(8,128)(2,1)S(1)}, bf16[1024,512]{1,0:T(8,128)(2,1)}, u32[]{:S(2)}, u32[]{:S(2)}) collective-permute-start(bf16[1024,512]{1,0:T(8,128)(2,1)S(1)} %get-tuple-element.13.refs_1_), channel_id=1, source_target_pairs={{1,0},{2,1},{3,2},{4,3},{5,4},{6,5},{7,6},{8,7},{9,8},{10,9},{11,1... | collective-permute-start | bytes 3145736 | tf_op jit(solution)/shard_map/ppermute | solution.py:315
  83.5 0.0 copy-done.4
  83.5 0.0 copy-done.5
  83.6 0.1 multiply_bitcast_fusion.slot_ref
  83.6 0.0 collective-permute-done.2.refs_4_
  83.6 4.6 %collective-permute-done.3.refs_7_ = bf16[1024,512]{1,0:T(8,128)(2,1)} collective-permute-done((bf16[1024,512]{1,0:T(8,128)(2,1)S(1)}, bf16[1024,512]{1,0:T(8,128)(2,1)}, u32[]{:S(2)}, u32[]{:S(2)}) %collective-permute-start.3) | collective-permute-done | bytes 1048608 | tf_op jit(solution)/shard_map/ppermute | solution.py:315
  88.3 6.5 %collective-permute-done.refs_0_ = bf16[1024,512]{1,0:T(8,128)(2,1)} collective-permute-done((bf16[1024,512]{1,0:T(8,128)(2,1)}, bf16[1024,512]{1,0:T(8,128)(2,1)}, u32[]{:S(2)}, u32[]{:S(2)}) %collective-permute-start) | collective-permute-done | bytes 1048608 | tf_op jit(solution)/shard_map/ppermute | solution.py:314
  94.8 4.7 %collective-permute-done.1.refs_3_ = bf16[1024,512]{1,0:T(8,128)(2,1)} collective-permute-done((bf16[1024,512]{1,0:T(8,128)(2,1)S(1)}, bf16[1024,512]{1,0:T(8,128)(2,1)}, u32[]{:S(2)}, u32[]{:S(2)}) %collective-permute-start.1) | collective-permute-done | bytes 1048608 | tf_op jit(solution)/shard_map/ppermute | solution.py:315
  99.5 0.0 copy-start.1
  99.5 11.0 %gather_gram.1 = (bf16[16,128,1024]{2,1,0:T(8,128)(2,1)S(1)}, f32[16,128,128]{2,1,0:T(8,128)S(1)}, f32[16,128,128]{2,1,0:T(8,128)S(1)}) custom-call(s32[2048]{0:T(1024)S(1)} %multiply_bitcast_fusion.slot_ref, bf16[1024,512]{1,0:T(8,128)(2,1)} %collective-permute-done.refs_0_, bf16[1024,512]{1,0:T(8,128)(2,1)S(1)} %get-tuple-element.13.refs_1_, ...), custom_call_target="tpu_custom_call" | custom-call | flops 1073741824 | bytes 33554432 | tf_op jit(solution)/shard_map/gather_gram/pallas_call | solution.py:169
  110.5 14.0 %invert_blocks.1.inverse_ref = f32[16,128,128]{2,1,0:T(8,128)S(1)} custom-call(f32[16,128,128]{2,1,0:T(8,128)S(1)} %get-tuple-element.16.gram_ref), custom_call_target="tpu_custom_call" | custom-call | tf_op jit(solution)/shard_map/invert_blocks/pallas_call | solution.py:249
  124.6 0.0 copy-done.1
  124.6 5.5 %update.1 = bf16[32,32,2048]{2,1,0:T(8,128)(2,1)S(1)} custom-call(f32[16,128,128]{2,1,0:T(8,128)S(1)} %invert_blocks.1.inverse_ref, f32[16,128,128]{2,1,0:T(8,128)S(1)} %get-tuple-element.17.moved_ref, bf16[16,128,1024]{2,1,0:T(8,128)(2,1)S(1)} %get-tuple-element.18.columns_ref, bf16[1024,2048]{1,0:T(8,128)(2,1)S(1)} %bitcast.17), custom_call_target="tpu_custom_call" | custom-call | tf_op jit(solution)/shard_map/update/pallas_call | solution.py:282
  130.1 64.5 %all_to_all.36 = bf16[32,32,2048]{2,1,0:T(8,128)(2,1)S(1)} all-to-all(bf16[32,32,2048]{2,1,0:T(8,128)(2,1)S(1)} %update.1), channel_id=1, replica_groups=mesh['space'=8,'mem'=32] {'mem'}, dimensions={0} | all-to-all | bytes 8388608 | tf_op jit(solution)/shard_map/all_to_all | solution.py:319
  194.6 2.3 %copy.10 = bf16[32,4,8,2048]{3,2,0,1:T(8,128)(2,1)} copy(bf16[32,4,8,2048]{3,2,1,0:T(8,128)(2,1)S(1)} %bitcast.22) | data formatting | bytes 8388608 | tf_op jit(solution)/shard_map/all_to_all | solution.py:319
Async XLA Ops:
  2.5 58.2 %copy-start.2 = (s32[2048]{0:T(1024)S(1)}, s32[2048]{0:T(1024)}, u32[]{:S(2)}) copy-start(s32[2048]{0:T(1024)} %cell_ref.3) | copy-start | bytes 24580
  2.5 58.2 %copy-start.3 = (f32[2048]{0:T(1024)S(1)}, f32[2048]{0:T(1024)}, u32[]{:S(2)}) copy-start(f32[2048]{0:T(1024)} %param.7) | copy-start | bytes 24580
  60.7 8.9 %copy-start = (bf16[32,32,2048]{2,0,1:T(8,128)(2,1)}, bf16[32,32,2048]{2,0,1:T(8,128)(2,1)S(1)}, u32[]{:S(2)}) copy-start(bf16[32,32,2048]{2,0,1:T(8,128)(2,1)S(1)} %all_to_all.35) | copy-start | bytes 12582916
  60.7 22.8 %copy-start.4 = (s32[16,128]{1,0:T(8,128)S(1)}, s32[16,128]{1,0:T(8,128)}, u32[]{:S(2)}) copy-start(s32[16,128]{1,0:T(8,128)} %param.8) | copy-start | bytes 24580
  60.7 22.8 %copy-start.5 = (s32[16]{0:T(128)S(1)}, s32[16]{0:T(128)}, u32[]{:S(2)}) copy-start(s32[16]{0:T(128)} %param.9) | copy-start | bytes 196
  69.6 14.0 %collective-permute-start.2 = (bf16[1024,512]{1,0:T(8,128)(2,1)S(1)}, bf16[1024,512]{1,0:T(8,128)(2,1)}, u32[]{:S(2)}, u32[]{:S(2)}) collective-permute-start(bf16[1024,512]{1,0:T(8,128)(2,1)S(1)} %get-tuple-element.14.refs_6_), channel_id=1, source_target_pairs={{0,1},{1,2},{2,3},{3,4},{4,5},{5,6},{6,7},{7,8},{8,9},{9,10},{10,1... | collective-permute-start | bytes 3145736 | tf_op jit(solution)/shard_map/ppermute | solution.py:314
  71.7 16.5 %collective-permute-start.3 = (bf16[1024,512]{1,0:T(8,128)(2,1)S(1)}, bf16[1024,512]{1,0:T(8,128)(2,1)}, u32[]{:S(2)}, u32[]{:S(2)}) collective-permute-start(bf16[1024,512]{1,0:T(8,128)(2,1)S(1)} %get-tuple-element.15.refs_5_), channel_id=1, source_target_pairs={{1,0},{2,1},{3,2},{4,3},{5,4},{6,5},{7,6},{8,7},{9,8},{10,9},{11,1... | collective-permute-start | bytes 3145736 | tf_op jit(solution)/shard_map/ppermute | solution.py:315
  73.9 20.9 %collective-permute-start = (bf16[1024,512]{1,0:T(8,128)(2,1)}, bf16[1024,512]{1,0:T(8,128)(2,1)}, u32[]{:S(2)}, u32[]{:S(2)}) collective-permute-start(bf16[1024,512]{1,0:T(8,128)(2,1)} %get-tuple-element.12.refs_2_), channel_id=1, source_target_pairs={{0,1},{1,2},{2,3},{3,4},{4,5},{5,6},{6,7},{7,8},{8,9},{9,10},{10,1... | collective-permute-start | bytes 3145736 | tf_op jit(solution)/shard_map/ppermute | solution.py:314
  77.3 22.2 %collective-permute-start.1 = (bf16[1024,512]{1,0:T(8,128)(2,1)S(1)}, bf16[1024,512]{1,0:T(8,128)(2,1)}, u32[]{:S(2)}, u32[]{:S(2)}) collective-permute-start(bf16[1024,512]{1,0:T(8,128)(2,1)S(1)} %get-tuple-element.13.refs_1_), channel_id=1, source_target_pairs={{1,0},{2,1},{3,2},{4,3},{5,4},{6,5},{7,6},{8,7},{9,8},{10,9},{11,1... | collective-permute-start | bytes 3145736 | tf_op jit(solution)/shard_map/ppermute | solution.py:315
  99.5 25.1 %copy-start.1 = (bf16[32,32,2048]{2,0,1:T(8,128)(2,1)S(1)}, bf16[32,32,2048]{2,0,1:T(8,128)(2,1)}, u32[]{:S(2)}) copy-start(bf16[32,32,2048]{2,0,1:T(8,128)(2,1)} %copy-done) | copy-start | bytes 12582916
